TPU v7x, 256 devices: a whole 4x4x8 slice. The times are simulated.
256 devices in a mesh: freq: 8 (over z), bl: 32 (over y, x, core).
Axes of the slice: x: 4, y: 4, z: 8, core: 2. Of those that a mesh axis runs over, the one named last changes fastest.
Arguments:
- vis: float32 [2, 256, 65536], P(None, 'freq', 'bl'), may hold values from -60 to 60
- coherency: bfloat16 [2, 4, 256, 65536], P(None, None, 'freq', 'bl'), may hold values from -6 to 6
- gains_init: float32 [2, 4, 256, 512], P(None, None, 'freq', 'bl'), may hold values from -4 to 4
- station_pairs: int32 [2, 65536], P(None, 'bl'), may hold values from 0 to 511, as said below
Outputs:
- gains: float32 [2, 4, 256, 512], P(None, None, 'freq', 'bl')
- consensus: float32 [2, 4, 256, 512], P(None, None, 'freq', 'bl')
Inputs may be any that keep to these rules, and one draw needn't show every extreme that they name: `station_pairs`: in each column the two stations differ.
All inputs are finite; a program needn't handle non-finite values.
Results may differ from a plain program's by a relative error of at most 0.0013.
Values may be sent and summed in bfloat16 or wider, within the bound.
No kernel may reach another device: no remote copies, remote signals or barrier semaphores. Data moves between devices by JAX's collectives and lax.ppermute only.
A program may use at most 64 MiB of HBM per device.

v0:
```python
import jax
import jax.numpy as jnp
from jax import lax
from jax.sharding import PartitionSpec as P

STATION_TOTAL = 512
SKY_DIRECTIONS = 4
ITERS = 2
ROUNDS = 2


def basis_rows(channels):
    position = (2.0 * jnp.arange(channels, dtype=jnp.float32) + 1.0) / channels - 1.0
    raw = [jnp.ones_like(position), position, position * position, position * position * position]
    rows = []
    for vector in raw:
        for other in rows:
            vector = vector - jnp.sum(other * vector) * other
        rows.append(vector / jnp.sqrt(jnp.sum(vector * vector)))
    return jnp.stack(rows)


def model_terms(vis, coherency, near, far):
    coh_re = coherency[0].astype(jnp.float32)
    coh_im = coherency[1].astype(jnp.float32)
    z_re = coh_re * far[0] + coh_im * far[1]
    z_im = coh_im * far[0] - coh_re * far[1]
    x_re = near[0] * coh_re - near[1] * coh_im
    x_im = near[0] * coh_im + near[1] * coh_re
    model_re = jnp.sum(near[0] * z_re - near[1] * z_im, axis=0)
    model_im = jnp.sum(near[0] * z_im + near[1] * z_re, axis=0)
    res_re = (vis[0] - model_re)[None]
    res_im = (vis[1] - model_im)[None]
    first_terms = jnp.stack(
        [res_re * z_re + res_im * z_im, res_im * z_re - res_re * z_im, z_re * z_re + z_im * z_im]
    ).astype(jnp.bfloat16)
    second_terms = jnp.stack(
        [res_re * x_re + res_im * x_im, res_re * x_im - res_im * x_re, x_re * x_re + x_im * x_im]
    ).astype(jnp.bfloat16)
    return (first_terms, second_terms)


def advance(gains, sums, target, penalty_weight):
    return gains + (sums[0:2] + penalty_weight * (target - gains)) / (
        2.0 * sums[2] + penalty_weight
    )


def shards(vis, coherency, gains_init, station_pairs):
    channels_dev = vis.shape[1]
    rows_dev = vis.shape[2]
    owned = gains_init.shape[3]
    penalty_weight = 2.0 * rows_dev * lax.axis_size("bl") / STATION_TOTAL
    station_iota = jnp.arange(STATION_TOTAL, dtype=jnp.int32)
    first_table = (station_pairs[0][:, None] == station_iota[None, :]).astype(jnp.bfloat16)
    second_table = (station_pairs[1][:, None] == station_iota[None, :]).astype(jnp.bfloat16)
    whole_basis = basis_rows(channels_dev * lax.axis_size("freq"))
    local_basis = lax.dynamic_slice_in_dim(
        whole_basis, lax.axis_index("freq") * channels_dev, channels_dev, 1
    )
    width = 2 * SKY_DIRECTIONS * channels_dev
    term_width = 3 * SKY_DIRECTIONS * channels_dev
    contract_cols = (((1,), (1,)), ((), ()))
    contract_rows = (((0,), (1,)), ((), ()))
    gains = gains_init
    target = gains_init
    dual = jnp.zeros_like(gains_init)
    consensus = gains_init
    for round_index in range(ROUNDS):
        for step_index in range(ITERS):
            rounded = gains.astype(jnp.bfloat16).reshape(width, owned)
            piece = lax.all_gather(rounded, "bl", axis=1, tiled=True)
            near_part = lax.dot_general(
                piece, first_table, contract_cols, preferred_element_type=jnp.float32
            )
            far_part = lax.dot_general(
                piece, second_table, contract_cols, preferred_element_type=jnp.float32
            )
            first_terms, second_terms = model_terms(
                vis,
                coherency,
                near_part.reshape(2, SKY_DIRECTIONS, channels_dev, rows_dev),
                far_part.reshape(2, SKY_DIRECTIONS, channels_dev, rows_dev),
            )
            flat_first = first_terms.reshape(term_width, rows_dev)
            flat_second = second_terms.reshape(term_width, rows_dev)
            total = lax.dot_general(
                first_table, flat_first, contract_rows, preferred_element_type=jnp.float32
            )
            totals = lax.psum_scatter(
                total
                + lax.dot_general(
                    second_table, flat_second, contract_rows, preferred_element_type=jnp.float32
                ),
                "bl",
                scatter_dimension=0,
                tiled=True,
            )
            sums = totals.T.reshape(3, SKY_DIRECTIONS, channels_dev, owned)
            gains = advance(gains, sums, target, penalty_weight)
        blend = gains + dual
        partial_fit = jnp.einsum(
            "jk,adks->jads", local_basis, blend, precision=lax.Precision.HIGHEST
        )
        coefficients = lax.psum(partial_fit, "freq")
        consensus = jnp.einsum(
            "jk,jads->adks", local_basis, coefficients, precision=lax.Precision.HIGHEST
        )
        dual = dual + gains - consensus
        target = consensus - dual
    return (gains, consensus)


def solution(mesh):
    placed = (
        P(None, "freq", "bl"),
        P(None, None, "freq", "bl"),
        P(None, None, "freq", "bl"),
        P(None, "bl"),
    )
    return jax.shard_map(
        shards,
        mesh=mesh,
        in_specs=placed,
        out_specs=(P(None, None, "freq", "bl"), P(None, None, "freq", "bl")),
        check_vma=False,
    )
```

profile of v0, /device:TPU:2, one launch (start us, length us, event | category | flops | bytes accessed | tf_op | source)
XLA Modules:
  0.0 535.2 jit_solution(11720419480373013828)
XLA Ops:
  7.2 0.8 fusion.158
  8.0 0.8 convert_element_type.124
  9.0 24.8 %all_gather.12 = bf16[256,512]{0,1:T(8,128)(2,1)S(1)} all-gather(bf16[256,16]{0,1:T(8,128)(2,1)S(1)} %reshape.258), channel_id=1, replica_groups=mesh['freq'=8,'bl'=32] {'bl'}, dimensions={1}, use_global_device_ids=true | all-gather | bytes 270336 | tf_op jit(solution)/shard_map/all_gather | solution.py:72
  33.8 1.4 fusion.43
  35.4 1.0 copy-done
  36.7 1.4 fusion.42
  38.4 0.7 subtract_reduce_fusion.3
  39.5 1.1 add_convert_fusion.15
  41.6 1.7 fusion.11
  43.3 2.6 fusion.60
  46.0 85.9 %reduce-scatter.5.cloned.1.call-done = f32[16,384]{1,0:T(8,128)} async-done(((f32[512,384]{1,0:T(8,128)}), f32[16,384]{1,0:T(8,128)}) %reduce-scatter.5.cloned.1.call-update) | async-done | bytes 24592 | tf_op jit(solution)/shard_map/reduce_scatter | solution.py:90
  131.9 0.7 fusion.117
  132.6 0.7 slice.204
  133.7 23.6 %all_gather.13 = bf16[256,512]{0,1:T(8,128)(2,1)S(1)} all-gather(bf16[256,16]{0,1:T(8,128)(2,1)S(1)} %reshape.259), channel_id=1, replica_groups=mesh['freq'=8,'bl'=32] {'bl'}, dimensions={1}, use_global_device_ids=true | all-gather | bytes 270336 | tf_op jit(solution)/shard_map/all_gather | solution.py:72
  157.3 1.4 fusion.2
  159.2 1.4 fusion.15
  160.8 0.7 subtract_reduce_fusion.2
  161.6 1.1 add_convert_fusion.11
  163.6 1.7 fusion.9
  165.5 2.6 fusion.63
  168.2 84.8 %reduce-scatter.7.cloned.1.call-done = f32[16,384]{1,0:T(8,128)} async-done(((f32[512,384]{1,0:T(8,128)}), f32[16,384]{1,0:T(8,128)}) %reduce-scatter.7.cloned.1.call-update) | async-done | bytes 24592 | tf_op jit(solution)/shard_map/reduce_scatter | solution.py:90
  253.7 0.7 slice.210
  254.8 23.3 %all_gather.14 = bf16[256,512]{0,1:T(8,128)(2,1)S(1)} all-gather(bf16[256,16]{0,1:T(8,128)(2,1)S(1)} %reshape.260), channel_id=1, replica_groups=mesh['freq'=8,'bl'=32] {'bl'}, dimensions={1}, use_global_device_ids=true | all-gather | bytes 270336 | tf_op jit(solution)/shard_map/all_gather | solution.py:72
  278.1 1.4 fusion
  280.0 1.4 fusion.13
  281.6 0.7 subtract_reduce_fusion.1
  282.4 1.1 add_convert_fusion.7
  284.4 1.7 fusion.7
  286.3 2.6 fusion.66
  294.7 1.3 multiply_reduce_fusion.2
  296.7 1.9 multiply_reduce_fusion.1
  298.6 2.6 multiply_reduce_fusion
  301.9 2.0 fusion.128
  304.5 30.2 %psum.14 = f32[4,2,4,16]{3,0,2,1:T(4,128)S(1)} all-reduce(f32[4,2,4,16]{3,0,2,1:T(4,128)S(1)} %fusion.159), channel_id=1, replica_groups=mesh['freq'=8,'bl'=32] {'freq'}, use_global_device_ids=true, to_apply=%region_18.0 | all-reduce | flops 512 | bytes 4096 | tf_op jit(solution)/shard_map/psum | solution.py:105
  334.7 39.2 %reduce-scatter.9.cloned.1.call-done = f32[16,384]{1,0:T(8,128)} async-done(((f32[512,384]{1,0:T(8,128)}), f32[16,384]{1,0:T(8,128)}) %reduce-scatter.9.cloned.1.call-update) | async-done | bytes 24592 | tf_op jit(solution)/shard_map/reduce_scatter | solution.py:90
  373.9 0.7 fusion.115
  374.6 0.7 slice.216
  375.9 23.3 %all_gather.15 = bf16[256,512]{0,1:T(8,128)(2,1)S(1)} all-gather(bf16[256,16]{0,1:T(8,128)(2,1)S(1)} %reshape.261), channel_id=1, replica_groups=mesh['freq'=8,'bl'=32] {'bl'}, dimensions={1}, use_global_device_ids=true | all-gather | bytes 270336 | tf_op jit(solution)/shard_map/all_gather | solution.py:72
  399.2 1.4 fusion.1
  401.1 1.4 fusion.14
  402.8 0.7 subtract_reduce_fusion
  403.6 1.1 add_convert_fusion.3
  405.5 1.7 fusion.5
  407.4 2.6 fusion.69
  410.1 84.9 %reduce-scatter.11.cloned.1.call-done = f32[16,384]{1,0:T(8,128)} async-done(((f32[512,384]{1,0:T(8,128)}), f32[16,384]{1,0:T(8,128)}) %reduce-scatter.11.cloned.1.call-update) | async-done | bytes 24592 | tf_op jit(solution)/shard_map/reduce_scatter | solution.py:90
  495.7 0.7 slice.222
  497.2 30.3 %psum.15 = f32[4,2,4,16]{3,0,2,1:T(4,128)S(1)} all-reduce(f32[4,2,4,16]{3,0,2,1:T(4,128)S(1)} %fusion.112), channel_id=1, replica_groups=mesh['freq'=8,'bl'=32] {'freq'}, use_global_device_ids=true, to_apply=%region_22.0 | all-reduce | flops 512 | bytes 4096 | tf_op jit(solution)/shard_map/psum | solution.py:105
  527.5 0.9 convolution_bitcast_fusion
  (78 shorter events, 15.0 us)
Async XLA Ops:
  7.2 124.8 %reduce-scatter.5.cloned.1.call-start = ((), (), s32[]{:S(2)}) async-start(), calls=%async_computation.4 | async-start | bytes 811008 | tf_op jit(solution)/shard_map/reduce_scatter | solution.py:90
  35.2 1.2 copy-start
  38.3 1.0 copy-start.1
  43.3 90.2 %copy-start.2 = (f32[2,4,32,16]{2,3,1,0:T(8,128)S(1)}, f32[2,4,32,16]{2,3,1,0:T(8,128)}, u32[]{:S(2)}) copy-start(f32[2,4,32,16]{2,3,1,0:T(8,128)} %param.6) | copy-start | bytes 49156
  46.0 207.0 %reduce-scatter.7.cloned.1.call-start = ((), (), s32[]{:S(2)}) async-start(), calls=%async_computation.5 | async-start | bytes 811008 | tf_op jit(solution)/shard_map/reduce_scatter | solution.py:90
  168.1 205.7 %reduce-scatter.9.cloned.1.call-start = ((), (), s32[]{:S(2)}) async-start(), calls=%async_computation.6 | async-start | bytes 811008 | tf_op jit(solution)/shard_map/reduce_scatter | solution.py:90
  288.9 206.1 %reduce-scatter.11.cloned.1.call-start = ((), (), s32[]{:S(2)}) async-start(), calls=%async_computation.7 | async-start | bytes 811008 | tf_op jit(solution)/shard_map/reduce_scatter | solution.py:90
  496.6 31.8 %copy-start.3 = (f32[2,4,32,16]{2,3,1,0:T(8,128)}, f32[2,4,32,16]{2,3,1,0:T(8,128)S(1)}, u32[]{:S(2)}) copy-start(f32[2,4,32,16]{2,3,1,0:T(8,128)S(1)} %fusion.105) | copy-start | bytes 49156
Sparse Core Ops, SparseCore 0:
  46.1 85.8 reduce-scatter.4
  168.2 84.7 reduce-scatter.6
  289.0 84.7 reduce-scatter.8
  410.2 84.7 reduce-scatter.10
where the time goes:
time: 543 us; the launch traced here: 535 us
  waiting for transfers between devices  295 us (54%)
  blocking collectives  155 us (29%)
  matrix products  31 us (6%)
  other arithmetic  27.4 us (5%)
  between operations  18.5 us (3%)
  local copies, waits for them, and re-layouts  7.82 us (1%)
    reduce_scatter x4, waiting for transfers between devices, shards(): lax.psum_scatter(total + lax.dot_general(second_table, flat_second, contr...  295 us
    all_gather x4, blocking collectives, shards(): piece = lax.all_gather(rounded, 'bl', axis=1, tiled=True)  95 us
    psum x2, blocking collectives, shards(): coefficients = lax.psum(partial_fit, 'freq')  60.5 us
  transfers between devices with their start and end apart: 4, of which 4 were waited for; matrix products, arithmetic and copies ran while one was open for 2% of the time, Pallas kernels for 0%

commit v1 on v0

v1 whole, which is shorter than its diff:
```python
import functools

import jax
import jax.numpy as jnp
import numpy as np
from jax import lax
from jax.experimental import pallas as pl
from jax.experimental.pallas import tpu as pltpu
from jax.sharding import Mesh, PartitionSpec as P

STATION_TOTAL = 512
SKY_DIRECTIONS = 4
ITERS = 2
ROUNDS = 2
LANES = 128
PARTS = STATION_TOTAL // LANES
CHUNK = 2048
f32, bf16, i32 = jnp.float32, jnp.bfloat16, jnp.int32


def basis_rows(channels):
    position = (2.0 * np.arange(channels) + 1.0) / channels - 1.0
    rows = []
    for vector in [np.ones_like(position), position, position**2, position**3]:
        for other in rows:
            vector = vector - np.sum(other * vector) * other
        rows.append(vector / np.sqrt(np.sum(vector * vector)))
    return np.stack(rows).astype(np.float32)


def lookup(parts, low, bits):
    picked = [jnp.take_along_axis(p, low, axis=1, mode="promise_in_bounds") for p in parts]
    return jnp.where(
        bits[1], jnp.where(bits[0], picked[3], picked[2]), jnp.where(bits[0], picked[1], picked[0])
    )


def column_terms(coh_re, coh_im, misc, parts_re, parts_im, sublane):
    def station(row):
        index = jnp.broadcast_to((misc[row : row + 1] + 256.0).astype(i32), (8, LANES))
        return index & (LANES - 1), index >> 7

    low_first, high_first = station(4)
    low_second, high_second = station(5)
    bits_first = ((high_first & 1) == 1, (high_first & 2) == 2)
    bits_second = ((high_second & 1) == 1, (high_second & 2) == 2)
    near_re = lookup(parts_re, low_first, bits_first)
    near_im = lookup(parts_im, low_first, bits_first)
    far_re = lookup(parts_re, low_second, bits_second)
    far_im = lookup(parts_im, low_second, bits_second)
    z_re = coh_re * far_re + coh_im * far_im
    z_im = coh_im * far_re - coh_re * far_im
    x_re = near_re * coh_re - near_im * coh_im
    x_im = near_re * coh_im + near_im * coh_re
    res_re = jnp.where(sublane < 2, misc, 0.0) - (near_re * z_re - near_im * z_im)
    res_im = jnp.where((sublane >= 2) & (sublane < 4), misc, 0.0) - (near_re * z_im + near_im * z_re)
    res_re = res_re + pltpu.roll(res_re, 4, 0)
    res_re = res_re + pltpu.roll(res_re, 2, 0)
    res_im = res_im + pltpu.roll(res_im, 4, 0)
    res_im = res_im + pltpu.roll(res_im, 2, 0)
    first = jnp.concatenate([res_re * z_re + res_im * z_im, res_im * z_re - res_re * z_im], 0)
    second = jnp.concatenate([res_re * x_re + res_im * x_im, res_re * x_im - res_im * x_re], 0)
    first_norm = z_re * z_re + z_im * z_im
    second_norm = x_re * x_re + x_im * x_im
    twice = lambda a: jnp.concatenate([a, a], 0).astype(bf16)
    return (
        (first.astype(bf16), twice(first_norm), low_first, high_first),
        (second.astype(bf16), twice(second_norm), low_second, high_second),
    )


def operands(term, station_rows, half_rows):
    pair, norm, low, high = term
    zero = jnp.zeros_like(pair)
    high = jnp.broadcast_to(high[:1].astype(f32), (16, LANES)).astype(bf16)
    rows = [jnp.where(high == float(h), pair, zero) for h in range(PARTS)]
    rows += [jnp.where(high == half_rows + float(h), norm, zero) for h in range(0, PARTS, 2)]
    low = jnp.broadcast_to(low[:1].astype(f32), (LANES, LANES)).astype(bf16)
    table = jnp.where(station_rows == low, jnp.ones_like(low), jnp.zeros_like(low))
    return jnp.concatenate(rows, 0), table


def accumulate(data_ref, gains_re, gains_im, sums_ref, acc_ref):
    sources, _, width = data_ref.shape
    chunk = min(CHUNK, width)
    per_source = width // chunk
    rounded_re = gains_re.astype(bf16).astype(f32)
    rounded_im = gains_im.astype(bf16).astype(f32)
    parts_re = [rounded_re[:, h * LANES : (h + 1) * LANES] for h in range(PARTS)]
    parts_im = [rounded_im[:, h * LANES : (h + 1) * LANES] for h in range(PARTS)]
    station_rows = lax.broadcasted_iota(i32, (LANES, LANES), 0).astype(f32).astype(bf16)
    half_rows = (lax.broadcasted_iota(i32, (16, LANES), 0) >> 3).astype(f32).astype(bf16)
    sublane = lax.broadcasted_iota(i32, (8, LANES), 0)
    acc_ref[...] = jnp.zeros_like(acc_ref)

    def step(index, carry):
        source = lax.div(index, per_source)
        offset = pl.multiple_of(lax.rem(index, per_source) * chunk, chunk)
        left, right = [], []
        for column in range(chunk // LANES):
            lanes = pl.ds(offset + column * LANES, LANES)
            coh_re = data_ref[source, 0:8, lanes].astype(f32)
            coh_im = data_ref[source, 8:16, lanes].astype(f32)
            misc = data_ref[source, 16:24, lanes].astype(f32)
            for term in column_terms(coh_re, coh_im, misc, parts_re, parts_im, sublane):
                rows, table = operands(term, station_rows, half_rows)
                left.append(rows)
                right.append(table)
        acc_ref[...] += lax.dot_general(
            jnp.concatenate(left, 1),
            jnp.concatenate(right, 1),
            (((1,), (1,)), ((), ())),
            preferred_element_type=f32,
        )
        return carry

    lax.fori_loop(0, sources * per_source, step, 0)
    acc = acc_ref[...]
    base = 16 * PARTS
    sums_ref[0] = jnp.concatenate([acc[16 * h : 16 * h + 8] for h in range(PARTS)], 1)
    sums_ref[1] = jnp.concatenate([acc[16 * h + 8 : 16 * h + 16] for h in range(PARTS)], 1)
    sums_ref[2] = jnp.concatenate([acc[base + 8 * h : base + 8 * h + 8] for h in range(PARTS)], 1)


def advance(gains, sums, target, penalty_weight):
    return gains + (sums[0:2] + penalty_weight * (target - gains)) / (
        2.0 * sums[2] + penalty_weight
    )


def sweep_kernel(data_ref, gains_ref, sums_ref, acc_ref):
    accumulate(data_ref, gains_ref[0], gains_ref[1], sums_ref, acc_ref)


def step_kernel(
    weight, data_ref, mine_ref, other_ref, gains_ref, target_ref, sums_ref, new_ref, acc_ref
):
    sums = mine_ref[...] + other_ref[...]
    gains = advance(gains_ref[...], sums, target_ref[...], weight)
    new_ref[...] = gains
    accumulate(data_ref, gains[0], gains[1], sums_ref, acc_ref)


def call(kernel, data, operands_in, out_shape, name):
    baselines = data.shape[0] * data.shape[2]
    whole = pl.BlockSpec(memory_space=pltpu.VMEM)
    return pl.pallas_call(
        kernel,
        out_shape=out_shape,
        in_specs=[whole] * (1 + len(operands_in)),
        out_specs=jax.tree.map(lambda _: whole, out_shape),
        scratch_shapes=[pltpu.VMEM((24 * PARTS, LANES), f32)],
        cost_estimate=pl.CostEstimate(
            flops=baselines * 24 * 2 * STATION_TOTAL * 2, bytes_accessed=data.size * 2, transcendentals=0
        ),
        name=name,
    )(data, *operands_in)


def shards(vis, coherency, gains_init, station_pairs):
    channels_dev = vis.shape[1]
    rows_dev = vis.shape[2]
    owned = gains_init.shape[3]
    pairs = lax.axis_size("pair")
    bands = lax.axis_size("freq")
    held = channels_dev // pairs
    assert held == 2 and STATION_TOTAL == 2 * owned * pairs
    stations = 2 * owned
    comps = 2 * SKY_DIRECTIONS * held
    weight = 2.0 * rows_dev * pairs * 2 / STATION_TOTAL
    swap = [(0, 1), (1, 0)]
    core = lax.axis_index("core")

    whole_basis = jnp.asarray(basis_rows(channels_dev * bands))
    local_basis = lax.dynamic_slice_in_dim(
        whole_basis, lax.axis_index("freq") * channels_dev, channels_dev, 1
    ).reshape(4, pairs, 1, 1, held, 1)

    def to_pairs(block):
        return lax.all_to_all(block, "pair", 0, 0, tiled=True)

    with jax.named_scope("pack"):
        gains_other = lax.ppermute(gains_init, "core", swap)
        gains_pair = jnp.where(
            core == 0,
            jnp.concatenate([gains_init, gains_other], 3),
            jnp.concatenate([gains_other, gains_init], 3),
        )
        gains_pair = gains_pair.reshape(2, SKY_DIRECTIONS, pairs, held, stations)
        gains_pair = gains_pair.transpose(2, 0, 1, 3, 4).reshape(pairs, comps * stations)
        upper = lax.reduce_precision(gains_pair, 8, 7)
        middle = lax.reduce_precision(gains_pair - upper, 8, 7)
        lower = gains_pair - upper - middle
        start = jnp.concatenate([upper, middle, lower], 1).astype(bf16)
        start = jnp.pad(start, ((0, 0), (0, 2 * rows_dev - start.shape[1]))).reshape(pairs, 2, rows_dev)
        coh = coherency.reshape(2, SKY_DIRECTIONS, pairs, held, rows_dev)
        coh = coh.transpose(2, 0, 1, 3, 4).reshape(pairs, comps, rows_dev)
        seen = vis.astype(bf16).reshape(2, pairs, held, rows_dev)
        seen = seen.transpose(1, 0, 2, 3).reshape(pairs, 2 * held, rows_dev)
        codes = (station_pairs - STATION_TOTAL // 2).astype(bf16)
        codes = jnp.broadcast_to(codes, (pairs, 2, rows_dev))
        packed = jnp.concatenate([coh, seen, codes, start], 1)
    with jax.named_scope("regroup"):
        data = to_pairs(packed)
    with jax.named_scope("unpack"):
        start = data[:, 22:24].reshape(pairs, 2 * rows_dev)[:, : 3 * comps * stations]
        start = start.astype(f32).reshape(pairs, 3, comps, stations)
        start = start[:, 0] + start[:, 1] + start[:, 2]

    def by_channel(block):
        return block.transpose(1, 0, 2).reshape(2, comps // 2, STATION_TOTAL)

    def by_station(values):
        block = values.reshape(comps, pairs, stations).transpose(1, 0, 2)
        block = to_pairs(block)
        return block.reshape(pairs, 2, SKY_DIRECTIONS, held, stations)

    sums_shape = jax.ShapeDtypeStruct((3, comps // 2, STATION_TOTAL), f32)
    gains_shape = jax.ShapeDtypeStruct((2, comps // 2, STATION_TOTAL), f32)

    gains = by_channel(start)
    target = gains
    dual = jnp.zeros_like(gains)
    owner_dual = jnp.zeros((pairs, 2, SKY_DIRECTIONS, held, stations), f32)
    partial = call(sweep_kernel, data, (gains,), sums_shape, "sweep")
    for round_index in range(ROUNDS):
        for step_index in range(ITERS):
            other = lax.ppermute(partial, "core", swap)
            if step_index < ITERS - 1:
                partial, gains = call(
                    functools.partial(step_kernel, weight),
                    data,
                    (partial, other, gains, target),
                    (sums_shape, gains_shape),
                    "step",
                )
            else:
                gains = advance(gains, partial + other, target, weight)
        last = round_index == ROUNDS - 1
        if not last:
            partial = call(sweep_kernel, data, (gains,), sums_shape, "sweep")
        with jax.named_scope("fit"):
            owner_gains = by_station(gains)
            blend = owner_gains + owner_dual
            part = jnp.sum(local_basis * blend[None], axis=(1, 4)).reshape(1, 8, LANES)
            part = jnp.broadcast_to(part, (bands, 8, LANES))
            part = lax.all_to_all(part, "freq", 0, 0, tiled=True)
            coefficients = jnp.sum(part, 0).reshape(4, 1, 2, SKY_DIRECTIONS, 1, stations)
            owner_consensus = jnp.sum(local_basis * coefficients, axis=0)
        if not last:
            with jax.named_scope("spread"):
                owner_dual = owner_dual + owner_gains - owner_consensus
                consensus = by_channel(to_pairs(owner_consensus.reshape(pairs, comps, stations)))
                dual = dual + gains - consensus
                target = consensus - dual

    def placed(block):
        block = block.transpose(1, 2, 0, 3, 4).reshape(2, SKY_DIRECTIONS, channels_dev, stations)
        return lax.dynamic_slice_in_dim(block, core * owned, owned, 3)

    return (placed(owner_gains), placed(owner_consensus))


def solution(mesh):
    split = Mesh(
        mesh.devices.reshape(mesh.shape["freq"], mesh.shape["bl"] // 2, 2), ("freq", "pair", "core")
    )
    bl = ("pair", "core")
    placed = (
        P(None, "freq", bl),
        P(None, None, "freq", bl),
        P(None, None, "freq", bl),
        P(None, bl),
    )
    return jax.shard_map(
        shards,
        mesh=split,
        in_specs=placed,
        out_specs=(P(None, None, "freq", bl), P(None, None, "freq", bl)),
        check_vma=False,
    )
```

time: 543 us -> 160 us (0.29); the launches traced: 535 us -> 159 us
  waiting for transfers between devices: 295 us -> 17.2 us
  blocking collectives: 155 us -> 59 us
  Pallas kernels: 0 us -> 44.9 us
  matrix products: 31 us -> 0 us
  other arithmetic: 27.4 us -> 9.03 us
  between operations: 18.5 us -> 1.03 us
  starting transfers between devices: 0.16 us -> 13.6 us
  local copies, waits for them, and re-layouts: 7.82 us -> 14.5 us
    reduce_scatter x4 -> x0, waiting for transfers between devices: 295 us -> none  [shards(): lax.psum_scatter(total + lax.dot_general(second_table, flat_second, contr...]
    all_gather x4 -> x0, blocking collectives: 95 us -> none  [shards(): piece = lax.all_gather(rounded, 'bl', axis=1, tiled=True)]
    psum x2 -> x0, blocking collectives: 60.5 us -> none  [shards(): coefficients = lax.psum(partial_fit, 'freq')]
    all_to_all x0 -> x3, blocking collectives: none -> 59 us  [the longest x2 42.7 us: to_pairs(): return lax.all_to_all(block, 'pair', 0, 0, tiled=True)]
    pallas_call x0 -> x4, Pallas kernels: none -> 44.9 us  [call(): pl.pallas_call(kernel, out_shape=out_shape, in_specs=[whole] * (1 + len(o...]
    dot_general x20 -> x0, matrix products: 31 us -> none  [the longest x4 10.4 us: shards(): lax.dot_general(first_table, flat_first, contract_rows, preferred_element...]
    all_to_all x0 -> x3, waiting for transfers between devices: none -> 13.4 us  [the longest x1 7.86 us: shards(): part = lax.all_to_all(part, 'freq', 0, 0, tiled=True)]
    all_to_all x0 -> x3, starting transfers between devices: none -> 12.8 us  [the longest x2 9.49 us: to_pairs(): return lax.all_to_all(block, 'pair', 0, 0, tiled=True)]
  transfers between devices with their start and end apart: 4 -> 8, of which waited for: 4 -> 5; matrix products, arithmetic and copies ran while one was open for 2% -> 5% of each run, Pallas kernels for 0% -> 7%
where the time goes in v1:
time: 160 us; the launch traced here: 159 us
  blocking collectives  59 us (37%)
  Pallas kernels  44.9 us (28%)
  waiting for transfers between devices  17.2 us (11%)
  local copies, waits for them, and re-layouts  14.5 us (9%)
  starting transfers between devices  13.6 us (8%)
  other arithmetic  9.03 us (6%)
    pallas_call x4, Pallas kernels, call(): pl.pallas_call(kernel, out_shape=out_shape, in_specs=[whole] * (1 + len(o...  44.9 us
    all_to_all x2, blocking collectives, to_pairs(): return lax.all_to_all(block, 'pair', 0, 0, tiled=True)  42.7 us
    all_to_all x1, blocking collectives, shards(): part = lax.all_to_all(part, 'freq', 0, 0, tiled=True)  16.3 us
    all_to_all x2, starting transfers between devices, to_pairs(): return lax.all_to_all(block, 'pair', 0, 0, tiled=True)  9.49 us
    all_to_all x1, waiting for transfers between devices, shards(): part = lax.all_to_all(part, 'freq', 0, 0, tiled=True)  7.86 us
    unnamed x24, local copies, waits for them, and re-layouts  6.12 us
    all_to_all x2, waiting for transfers between devices, to_pairs(): return lax.all_to_all(block, 'pair', 0, 0, tiled=True)  5.49 us
    ppermute x4, waiting for transfers between devices, shards(): other = lax.ppermute(partial, 'core', swap)  3.81 us
  transfers between devices with their start and end apart: 8, of which 5 were waited for; matrix products, arithmetic and copies ran while one was open for 5% of the time, Pallas kernels for 7%

profile of v1, /device:TPU:2, one launch (start us, length us, event | category | flops | bytes accessed | tf_op | source)
XLA Modules:
  0.0 159.3 jit_solution(6209429212010053086)
XLA Ops:
  0.6 0.9 copy.56
  1.7 0.7 add_convert_fusion
  2.4 1.7 %reshape.87 = bf16[2,4,16,2,2048]{4,3,2,1,0:T(2,128)(2,1)S(1)} reshape(bf16[2,4,32,2048]{3,2,1,0:T(8,128)(2,1)} %param.6) | data formatting | bytes 2097152 | tf_op jit(solution)/shard_map/pack/reshape | solution.py:196
  4.2 1.1 copy.77
  5.3 0.4 reshape.88
  5.7 0.6 copy-done.1
  6.4 0.2 reshape.89
  6.6 0.2 copy.78
  6.9 0.3 fusion.6
  7.3 0.2 reshape.91
  7.7 0.5 pad_maximum_fusion
  8.2 29.4 %all_to_all.30.data_ref = bf16[16,24,2048]{2,1,0:T(8,128)(2,1)S(1)} all-to-all(bf16[16,24,2048]{2,1,0:T(8,128)(2,1)S(1)} %pad_maximum_fusion), channel_id=1, replica_groups=mesh['freq'=8,'pair'=16,'core'=2] {'pair'}, dimensions={0} | all-to-all | bytes 3145728 | tf_op jit(solution)/shard_map/regroup/all_to_all | solution.py:180
  38.0 0.7 reshape.96.gains_ref.target_ref
  38.8 11.2 %sweep.2.mine_ref = f32[3,8,512]{2,1,0:T(8,128)} custom-call(bf16[16,24,2048]{2,1,0:T(8,128)(2,1)} %copy-done, f32[2,8,512]{2,1,0:T(8,128)} %reshape.96.gains_ref.target_ref), custom_call_target="tpu_custom_call" | custom-call | flops 1610612736 | bytes 1572864 | tf_op jit(solution)/shard_map/sweep/pallas_call | solution.py:147
  50.0 1.4 collective-permute-done.1.other_ref
  51.4 0.6 copy-done.6
  52.0 11.3 %step.2 = (f32[3,8,512]{2,1,0:T(8,128)}, f32[2,8,512]{2,1,0:T(8,128)}) custom-call(bf16[16,24,2048]{2,1,0:T(8,128)(2,1)} %copy-done, f32[3,8,512]{2,1,0:T(8,128)} %sweep.2.mine_ref, f32[3,8,512]{2,1,0:T(8,128)} %copy-done.6, f32[2,8,512]{2,1,0:T(8,128)} %reshape.96.gains_ref.target_ref, f32[2,8,512]{2,1,0:T(8,128)} %reshape.96.gains_ref.target_ref), custom_call_target="tpu_custom_call" | custom-call | flops 1610612736 | bytes 1572864 | tf_op jit(solution)/shard_map/step/pallas_call | solution.py:147
  63.3 0.2 collective-permute-start.2
  63.4 1.3 collective-permute-done.2
  64.7 0.8 add.56
  65.5 0.8 fusion.11.gains_ref
  66.5 0.7 reshape.107
  67.2 4.7 %all-to-all-start.1 = ((f32[16,1,512]{2,1,0:T(1,128)}), f32[16,1,512]{2,1,0:T(1,128)S(1)}, u32[]{:S(2)}, u32[]{:S(2)}) async-start(f32[16,1,512]{2,1,0:T(1,128)} %reshape.107), calls=%async_computation.1 | async-start | bytes 65536 | tf_op jit(solution)/shard_map/fit/all_to_all | solution.py:180
  72.0 0.7 constant_dynamic-slice_fusion.2
  72.8 5.5 %all-to-all-done.1 = f32[16,1,512]{2,1,0:T(1,128)S(1)} async-done(((f32[16,1,512]{2,1,0:T(1,128)}), f32[16,1,512]{2,1,0:T(1,128)S(1)}, u32[]{:S(2)}, u32[]{:S(2)}) %all-to-all-start.1) | async-done | bytes 32800 | tf_op jit(solution)/shard_map/fit/all_to_all | solution.py:180
  78.3 0.6 broadcast.38
  78.8 0.8 reduce
  79.7 0.2 multiply_reduce_fusion.3
  80.0 16.3 %all_to_all.31 = f32[8,8,128]{2,1,0:T(8,128)S(1)} all-to-all(f32[8,8,128]{2,1,0:T(8,128)S(1)} %broadcast_in_dim.22), channel_id=1, replica_groups=mesh['freq'=8,'pair'=16,'core'=2] {'freq'}, dimensions={0} | all-to-all | bytes 65536 | tf_op jit(solution)/shard_map/fit/all_to_all | solution.py:247
  96.5 0.7 reshape.109
  97.3 4.7 %all-to-all-start.3 = ((f32[16,1,512]{2,1,0:T(1,128)}), f32[16,1,512]{2,1,0:T(1,128)S(1)}, u32[]{:S(2)}, u32[]{:S(2)}) async-start(f32[16,1,512]{2,1,0:T(1,128)} %reshape.109), calls=%async_computation.3 | async-start | bytes 65536 | tf_op jit(solution)/shard_map/spread/all_to_all | solution.py:180
  102.0 11.2 %sweep.3.mine_ref = f32[3,8,512]{2,1,0:T(8,128)} custom-call(bf16[16,24,2048]{2,1,0:T(8,128)(2,1)} %copy-done, f32[2,8,512]{2,1,0:T(8,128)} %copy-done.2), custom_call_target="tpu_custom_call" | custom-call | flops 1610612736 | bytes 1572864 | tf_op jit(solution)/shard_map/sweep/pallas_call | solution.py:147
  113.2 0.8 reduce.1
  114.3 1.4 subtract_subtract_fusion.target_ref
  115.6 0.6 copy-done.5
  116.3 11.3 %step.3 = (f32[3,8,512]{2,1,0:T(8,128)}, f32[2,8,512]{2,1,0:T(8,128)}) custom-call(bf16[16,24,2048]{2,1,0:T(8,128)(2,1)} %copy-done, f32[3,8,512]{2,1,0:T(8,128)} %sweep.3.mine_ref, f32[3,8,512]{2,1,0:T(8,128)} %copy-done.5, f32[2,8,512]{2,1,0:T(8,128)} %copy-done.2, f32[2,8,512]{2,1,0:T(8,128)} %subtract_subtract_fusion.target_ref), custom_call_target="tpu_custom_call" | custom-call | flops 1610612736 | bytes 1572864 | tf_op jit(solution)/shard_map/step/pallas_call | solution.py:147
  127.5 0.5 collective-permute-start.4
  128.0 1.1 collective-permute-done.4
  129.1 0.8 add.61
  129.9 0.8 fusion.9
  131.0 13.3 %all_to_all.32 = f32[16,1,512]{2,1,0:T(1,128)S(1)} all-to-all(f32[16,1,512]{2,1,0:T(1,128)S(1)} %reshape.111), channel_id=1, replica_groups=mesh['freq'=8,'pair'=16,'core'=2] {'pair'}, dimensions={0} | all-to-all | bytes 65536 | tf_op jit(solution)/shard_map/fit/all_to_all | solution.py:180
  144.3 0.8 reduce.2
  145.3 0.2 multiply_reduce_fusion.1
  145.5 0.6 broadcast_in_dim.24
  146.1 3.3 %all-to-all-start.5 = ((f32[8,8,128]{2,1,0:T(8,128)}), f32[8,8,128]{2,1,0:T(8,128)S(1)}, u32[]{:S(2)}, u32[]{:S(2)}) async-start(f32[8,8,128]{2,1,0:T(8,128)} %broadcast_in_dim.24), calls=%async_computation.5 | async-start | bytes 65536 | tf_op jit(solution)/shard_map/fit/all_to_all | solution.py:247
  149.6 7.9 %all-to-all-done.5 = f32[8,8,128]{2,1,0:T(8,128)S(1)} async-done(((f32[8,8,128]{2,1,0:T(8,128)}), f32[8,8,128]{2,1,0:T(8,128)S(1)}, u32[]{:S(2)}, u32[]{:S(2)}) %all-to-all-start.5) | async-done | bytes 32800 | tf_op jit(solution)/shard_map/fit/all_to_all | solution.py:247
  157.9 0.7 copy.69
  158.6 0.7 copy.70
  (59 shorter events, 2.8 us)
Async XLA Ops:
  1.6 5.4 %collective-permute-start = (f32[2,4,32,16]{3,2,1,0:T(8,128)S(1)}, f32[2,4,32,16]{3,2,1,0:T(8,128)S(1)}, u32[]{:S(2)}, u32[]{:S(2)}) collective-permute-start(f32[2,4,32,16]{3,2,1,0:T(8,128)S(1)} %copy.56), channel_id=1, source_target_pairs={{0,1},{1,0},{2,3},{3,2},{4,5},{5,4},{6,7},{7,6},{8,9},{9,8},{10,11... | collective-permute-start | bytes 49160 | tf_op jit(solution)/shard_map/pack/ppermute | solution.py:183
  5.3 1.0 copy-start.1
  37.6 1.2 copy-start
  50.0 15.6 %copy-start.3 = (f32[2,8,512]{2,1,0:T(8,128)S(1)}, f32[2,8,512]{2,1,0:T(8,128)}, u32[]{:S(2)}) copy-start(f32[2,8,512]{2,1,0:T(8,128)} %reshape.96.gains_ref.target_ref) | copy-start | bytes 98308
  50.0 1.4 collective-permute-start.1
  51.4 0.6 copy-start.6
  63.3 1.4 collective-permute-start.2
  66.3 35.7 %copy-start.2 = (f32[2,8,512]{2,1,0:T(8,128)}, f32[2,8,512]{2,1,0:T(8,128)S(1)}, u32[]{:S(2)}) copy-start(f32[2,8,512]{2,1,0:T(8,128)S(1)} %fusion.11.gains_ref) | copy-start | bytes 98308
  67.2 11.1 %all-to-all-start.1 = ((f32[16,1,512]{2,1,0:T(1,128)}), f32[16,1,512]{2,1,0:T(1,128)S(1)}, u32[]{:S(2)}, u32[]{:S(2)}) async-start(f32[16,1,512]{2,1,0:T(1,128)} %reshape.107), calls=%async_computation.1 | async-start | bytes 65536 | tf_op jit(solution)/shard_map/fit/all_to_all | solution.py:180
  97.3 16.0 %all-to-all-start.3 = ((f32[16,1,512]{2,1,0:T(1,128)}), f32[16,1,512]{2,1,0:T(1,128)S(1)}, u32[]{:S(2)}, u32[]{:S(2)}) async-start(f32[16,1,512]{2,1,0:T(1,128)} %reshape.109), calls=%async_computation.3 | async-start | bytes 65536 | tf_op jit(solution)/shard_map/spread/all_to_all | solution.py:180
  113.2 2.4 %collective-permute-start.3 = (f32[3,8,512]{2,1,0:T(8,128)}, f32[3,8,512]{2,1,0:T(8,128)S(1)}, u32[]{:S(2)}, u32[]{:S(2)}) collective-permute-start(f32[3,8,512]{2,1,0:T(8,128)} %sweep.3.mine_ref), channel_id=1, source_target_pairs={{0,1},{1,0},{2,3},{3,2},{4,5},{5,4},{6,7},{7,6},{8,9},{9,8},{10,11... | collective-permute-start | bytes 147464 | tf_op jit(solution)/shard_map/ppermute | solution.py:228
  115.6 14.3 %copy-start.4 = (f32[2,8,512]{2,1,0:T(8,128)S(1)}, f32[2,8,512]{2,1,0:T(8,128)}, u32[]{:S(2)}) copy-start(f32[2,8,512]{2,1,0:T(8,128)} %subtract_subtract_fusion.target_ref) | copy-start | bytes 98308
  115.6 0.6 copy-start.5
  127.5 1.6 %collective-permute-start.4 = (f32[3,8,512]{2,1,0:T(8,128)}, f32[3,8,512]{2,1,0:T(8,128)S(1)}, u32[]{:S(2)}, u32[]{:S(2)}) collective-permute-start(f32[3,8,512]{2,1,0:T(8,128)} %get-tuple-element.9), channel_id=1, source_target_pairs={{0,1},{1,0},{2,3},{3,2},{4,5},{5,4},{6,7},{7,6},{8,9},{9,8},{10,11... | collective-permute-start | bytes 147464 | tf_op jit(solution)/shard_map/ppermute | solution.py:228
  146.1 11.3 %all-to-all-start.5 = ((f32[8,8,128]{2,1,0:T(8,128)}), f32[8,8,128]{2,1,0:T(8,128)S(1)}, u32[]{:S(2)}, u32[]{:S(2)}) async-start(f32[8,8,128]{2,1,0:T(8,128)} %broadcast_in_dim.24), calls=%async_computation.5 | async-start | bytes 65536 | tf_op jit(solution)/shard_map/fit/all_to_all | solution.py:247

commit v2 on v1

v2 whole, which is shorter than its diff:
```python
import functools

import jax
import jax.numpy as jnp
import numpy as np
from jax import lax
from jax.experimental import pallas as pl
from jax.experimental.pallas import tpu as pltpu
from jax.sharding import Mesh, PartitionSpec as P

STATION_TOTAL = 512
SKY_DIRECTIONS = 4
ITERS = 2
ROUNDS = 2
LANES = 128
PARTS = STATION_TOTAL // LANES
UNROLL = 2
VMEM_LIMIT = 24 * 1024 * 1024
f32, bf16, i32 = jnp.float32, jnp.bfloat16, jnp.int32


def basis_rows(channels):
    position = (2.0 * np.arange(channels) + 1.0) / channels - 1.0
    rows = []
    for vector in [np.ones_like(position), position, position**2, position**3]:
        for other in rows:
            vector = vector - np.sum(other * vector) * other
        rows.append(vector / np.sqrt(np.sum(vector * vector)))
    return np.stack(rows).astype(np.float32)


def lanes_of(rows):
    return {"re": 0, "im": rows, "misc": 2 * rows, "low": 3 * rows, "start": 3 * rows + rows // 2}


def pick_channel_pair(by_direction, pair):
    return jnp.concatenate([block[2 * pair : 2 * pair + 2] for block in by_direction], 0)


def pack_kernel(core_ref, coh_ref, vis_ref, pairs_ref, mine_ref, other_ref, out_ref):
    rows = vis_ref.shape[2]
    count = out_ref.shape[0]
    at = lanes_of(rows)
    half = rows // 2

    def columns(index, carry):
        early = pl.multiple_of(index * LANES, LANES)
        late = pl.multiple_of(half + index * LANES, LANES)
        lower = []
        for offset in (early, late):
            lanes = pl.ds(offset, LANES)
            for part in range(2):
                blocks = [coh_ref[part, d, :, lanes].astype(f32) for d in range(SKY_DIRECTIONS)]
                place = pl.multiple_of(offset + part * rows, LANES)
                for p in range(count):
                    out_ref[p, :, pl.ds(place, LANES)] = pick_channel_pair(blocks, p).astype(bf16)
            upper = []
            for part in range(2):
                seen = vis_ref[part, :, lanes]
                rounded = seen.astype(bf16).astype(f32)
                upper.append(rounded)
                lower.append(seen - rounded)
            codes = (pairs_ref[:, lanes] - STATION_TOTAL // 2).astype(f32)
            tail = jnp.concatenate([codes, jnp.zeros((2, LANES), f32)], 0)
            place = pl.multiple_of(offset + at["misc"], LANES)
            for p in range(count):
                block = jnp.concatenate([upper[0][2 * p : 2 * p + 2], upper[1][2 * p : 2 * p + 2], tail], 0)
                out_ref[p, :, pl.ds(place, LANES)] = block.astype(bf16)
        place = pl.multiple_of(early + at["low"], LANES)
        for p in range(count):
            out_ref[p, :, pl.ds(place, LANES)] = pick_channel_pair(lower, p).astype(bf16)
        return carry

    lax.fori_loop(0, half // LANES, columns, 0)
    is_first = core_ref[0] == 0
    for part in range(2):
        mine = jnp.concatenate([mine_ref[part, d] for d in range(SKY_DIRECTIONS)], 1)
        other = jnp.concatenate([other_ref[part, d] for d in range(SKY_DIRECTIONS)], 1)
        start = jnp.concatenate([jnp.where(is_first, mine, other), jnp.where(is_first, other, mine)], 0)
        upper = start.astype(bf16).astype(f32)
        middle = (start - upper).astype(bf16).astype(f32)
        lower = start - upper - middle
        square = jnp.concatenate([upper, middle, lower, jnp.zeros_like(start)], 0).T
        blocks = [square[d * 2 * count : (d + 1) * 2 * count] for d in range(SKY_DIRECTIONS)]
        place = at["start"] + part * LANES
        for p in range(count):
            out_ref[p, :, place : place + LANES] = pick_channel_pair(blocks, p).astype(bf16)


def stations_in_lanes(pieces):
    lane = lax.broadcasted_iota(i32, (8, LANES), 1)
    tiles = []
    for q in range(0, len(pieces), 4):
        tile = pieces[q]
        for k in range(1, 4):
            moved = pltpu.roll(pieces[q + k], 32 * k, 1)
            tile = jnp.where(lane >= 32 * k, moved, tile)
        tiles.append(tile)
    return jnp.concatenate(tiles, 1)


def starting_gains(data_ref):
    at = lanes_of((data_ref.shape[2] - 2 * LANES) * 2 // 7)["start"]
    parts = []
    for part in range(2):
        pieces = []
        for p in range(data_ref.shape[0]):
            piece = data_ref[p, :, at + part * LANES : at + (part + 1) * LANES].astype(f32)
            piece = piece + pltpu.roll(piece, LANES - 32, 1) + pltpu.roll(piece, LANES - 64, 1)
            pieces.append(piece)
        parts.append(stations_in_lanes(pieces))
    return parts


def lookup(parts, low, bits):
    picked = [jnp.take_along_axis(p, low, axis=1, mode="promise_in_bounds") for p in parts]
    return jnp.where(
        bits[1], jnp.where(bits[0], picked[3], picked[2]), jnp.where(bits[0], picked[1], picked[0])
    )


def column_terms(coh_re, coh_im, misc, low, low_row, parts_re, parts_im, sublane):
    def station(row):
        index = jnp.broadcast_to((misc[row : row + 1] + 256.0).astype(i32), (8, LANES))
        return index & (LANES - 1), index >> 7

    low_first, high_first = station(4)
    low_second, high_second = station(5)
    bits_first = ((high_first & 1) == 1, (high_first & 2) == 2)
    bits_second = ((high_second & 1) == 1, (high_second & 2) == 2)
    near_re = lookup(parts_re, low_first, bits_first)
    near_im = lookup(parts_im, low_first, bits_first)
    far_re = lookup(parts_re, low_second, bits_second)
    far_im = lookup(parts_im, low_second, bits_second)
    z_re = coh_re * far_re + coh_im * far_im
    z_im = coh_im * far_re - coh_re * far_im
    x_re = near_re * coh_re - near_im * coh_im
    x_im = near_re * coh_im + near_im * coh_re
    inside = lambda row: (sublane >= row) & (sublane < row + 2)
    vis_re = jnp.where(inside(0), misc, jnp.where(inside(low_row), low, 0.0))
    vis_im = jnp.where(inside(2), misc, jnp.where(inside(low_row + 2), low, 0.0))
    if low_row == 0:
        vis_re = jnp.where(inside(0), misc + low, 0.0)
        vis_im = jnp.where(inside(2), misc + low, 0.0)
    res_re = vis_re - (near_re * z_re - near_im * z_im)
    res_im = vis_im - (near_re * z_im + near_im * z_re)
    res_re = res_re + pltpu.roll(res_re, 4, 0)
    res_re = res_re + pltpu.roll(res_re, 2, 0)
    res_im = res_im + pltpu.roll(res_im, 4, 0)
    res_im = res_im + pltpu.roll(res_im, 2, 0)
    first = jnp.concatenate([res_re * z_re + res_im * z_im, res_im * z_re - res_re * z_im], 0)
    second = jnp.concatenate([res_re * x_re + res_im * x_im, res_re * x_im - res_im * x_re], 0)
    first_norm = z_re * z_re + z_im * z_im
    second_norm = x_re * x_re + x_im * x_im
    twice = lambda a: jnp.concatenate([a, a], 0).astype(bf16)
    return (
        (first.astype(bf16), twice(first_norm), low_first, high_first),
        (second.astype(bf16), twice(second_norm), low_second, high_second),
    )


def operands(term, station_rows, half_rows):
    pair, norm, low, high = term
    zero = jnp.zeros_like(pair)
    high = jnp.broadcast_to(high[:1].astype(f32), (16, LANES)).astype(bf16)
    rows = [jnp.where(high == float(h), pair, zero) for h in range(PARTS)]
    rows += [jnp.where(high == half_rows + float(h), norm, zero) for h in range(0, PARTS, 2)]
    low = jnp.broadcast_to(low[:1].astype(f32), (LANES, LANES)).astype(bf16)
    table = jnp.where(station_rows == low, jnp.ones_like(low), jnp.zeros_like(low))
    return jnp.concatenate(rows, 0), table


def accumulate(data_ref, first, count, gains_re, gains_im, sums_ref, acc_ref, before=None):
    rows = (data_ref.shape[2] - 2 * LANES) * 2 // 7
    at = lanes_of(rows)
    half = rows // 2
    rounded_re = gains_re.astype(bf16).astype(f32)
    rounded_im = gains_im.astype(bf16).astype(f32)
    parts_re = [rounded_re[:, h * LANES : (h + 1) * LANES] for h in range(PARTS)]
    parts_im = [rounded_im[:, h * LANES : (h + 1) * LANES] for h in range(PARTS)]
    station_rows = lax.broadcasted_iota(i32, (LANES, LANES), 0).astype(f32).astype(bf16)
    half_rows = (lax.broadcasted_iota(i32, (16, LANES), 0) >> 3).astype(f32).astype(bf16)
    sublane = lax.broadcasted_iota(i32, (8, LANES), 0)
    acc_ref[...] = jnp.zeros_like(acc_ref)

    def step(source, carry):
        left, right = [], []
        for offset in range(0, rows, LANES):
            load = lambda start: data_ref[source, :, start : start + LANES].astype(f32)
            low = load(at["low"] + offset % half)
            terms = column_terms(
                load(at["re"] + offset),
                load(at["im"] + offset),
                load(at["misc"] + offset),
                low,
                4 * (offset // half),
                parts_re,
                parts_im,
                sublane,
            )
            (rows_first, table_first), (rows_second, table_second) = [
                operands(term, station_rows, half_rows) for term in terms
            ]
            left.append(jnp.concatenate([rows_first, rows_second], 0))
            right.append(jnp.concatenate([table_first, table_second], 0))
        acc_ref[...] += lax.dot_general(
            jnp.concatenate(left, 1),
            jnp.concatenate(right, 1),
            (((1,), (1,)), ((), ())),
            preferred_element_type=f32,
        )
        return carry

    lax.fori_loop(first, first + count, step, 0, unroll=UNROLL)
    tall = 24 * PARTS
    acc = acc_ref[0:tall, 0:LANES] + acc_ref[tall : 2 * tall, LANES : 2 * LANES]
    base = 16 * PARTS
    sums = [
        jnp.concatenate([acc[16 * h : 16 * h + 8] for h in range(PARTS)], 1),
        jnp.concatenate([acc[16 * h + 8 : 16 * h + 16] for h in range(PARTS)], 1),
        jnp.concatenate([acc[base + 8 * h : base + 8 * h + 8] for h in range(PARTS)], 1),
    ]
    for k in range(3):
        sums_ref[k] = sums[k] if before is None else before[k] + sums[k]


def advance(gains, sums, target, penalty_weight):
    return gains + (sums[0:2] + penalty_weight * (target - gains)) / (
        2.0 * sums[2] + penalty_weight
    )


def first_kernel(data_ref, sums_ref, gains_ref, acc_ref):
    gains = starting_gains(data_ref)
    gains_ref[0], gains_ref[1] = gains
    accumulate(data_ref, 0, data_ref.shape[0], *gains, sums_ref, acc_ref)


def early_kernel(data_ref, gains_ref, sums_ref, acc_ref):
    accumulate(data_ref, 0, data_ref.shape[0] // 2, gains_ref[0], gains_ref[1], sums_ref, acc_ref)


def late_kernel(data_ref, gains_ref, before_ref, sums_ref, acc_ref):
    half = data_ref.shape[0] // 2
    accumulate(data_ref, half, half, gains_ref[0], gains_ref[1], sums_ref, acc_ref, before_ref)


def step_kernel(weight, data_ref, mine_ref, other_ref, gains_ref, sums_ref, new_ref, acc_ref):
    gains = gains_ref[...]
    gains = advance(gains, mine_ref[...] + other_ref[...], gains, weight)
    new_ref[...] = gains
    accumulate(data_ref, 0, data_ref.shape[0], gains[0], gains[1], sums_ref, acc_ref)


def retarget_kernel(
    weight, data_ref, mine_ref, other_ref, gains_ref, fit_ref, sums_ref, new_ref, target_ref, acc_ref
):
    consensus = by_channel(fit_ref)
    gains = gains_ref[...]
    target = consensus - (gains - consensus)
    target_ref[...] = target
    gains = advance(gains, mine_ref[...] + other_ref[...], target, weight)
    new_ref[...] = gains
    accumulate(data_ref, 0, data_ref.shape[0], gains[0], gains[1], sums_ref, acc_ref)


def by_channel(block_ref):
    pieces = [block_ref[p] for p in range(block_ref.shape[0])]
    turned = [pltpu.roll(piece, LANES - 32, 1) for piece in pieces]
    return jnp.stack([stations_in_lanes(pieces), stations_in_lanes(turned)])


def finish_kernel(weight, mine_ref, other_ref, gains_ref, target_ref, new_ref, block_ref):
    gains = advance(gains_ref[...], mine_ref[...] + other_ref[...], target_ref[...], weight)
    new_ref[...] = gains
    lane = lax.broadcasted_iota(i32, (8, LANES), 1)
    for p in range(block_ref.shape[0]):
        tile = slice(p // 4 * LANES, (p // 4 + 1) * LANES)
        shift = 32 * (p % 4)
        real = pltpu.roll(gains[0][:, tile], (LANES - shift) % LANES, 1)
        imag = pltpu.roll(gains[1][:, tile], (LANES + 32 - shift) % LANES, 1)
        block_ref[p] = jnp.where(lane < 32, real, imag)


def is_even(shape):
    return (lax.broadcasted_iota(i32, shape, 0) & 1) == 0


def basis_column(basis_ref, row, source):
    even = is_even((8, LANES))
    return jnp.where(even, basis_ref[row, 2 * source], basis_ref[row, 2 * source + 1])


def fit_kernel(basis_ref, *refs):
    *block_refs, out_ref = refs
    even = is_even((8, LANES))
    blocks = []
    for p in range(block_refs[0].shape[0]):
        blend = block_refs[0][p]
        if len(block_refs) > 1:
            blend = blend + block_refs[1][p]
        blocks.append(blend)
    totals = []
    for row in range(4):
        total = sum(basis_column(basis_ref, row, p) * block for p, block in enumerate(blocks))
        totals.append(total + jnp.where(even, pltpu.roll(total, 7, 0), pltpu.roll(total, 1, 0)))
    lane = lax.broadcasted_iota(i32, (8, LANES), 1)
    early = jnp.where(even, totals[0], totals[1])
    late = jnp.where(even, totals[2], totals[3])
    packed = jnp.where(lane < LANES // 2, early, pltpu.roll(late, LANES // 2, 1))
    for f in range(out_ref.shape[0]):
        out_ref[f] = packed


def consensus_blocks(basis_ref, parts_ref, count):
    even = is_even((8, LANES))
    total = parts_ref[0]
    for f in range(1, parts_ref.shape[0]):
        total = total + parts_ref[f]
    rows = []
    for half in (total, pltpu.roll(total, LANES // 2, 1)):
        rows.append(jnp.where(even, half, pltpu.roll(half, 1, 0)))
        rows.append(jnp.where(even, pltpu.roll(half, 7, 0), half))
    return [
        sum(basis_column(basis_ref, row, p) * rows[row] for row in range(4)) for p in range(count)
    ]


def spread_kernel(basis_ref, parts_ref, gains_ref, out_ref, dual_ref):
    for p, block in enumerate(consensus_blocks(basis_ref, parts_ref, out_ref.shape[0])):
        out_ref[p] = block
        dual_ref[p] = gains_ref[p] - block


def write_owned(blocks, is_first, out_ref):
    owned = out_ref.shape[2]
    channels = 2 * len(blocks)
    rows = [block[2 * d : 2 * d + 2] for d in range(SKY_DIRECTIONS) for block in blocks]
    turned = jnp.concatenate(rows, 0).T
    for part in range(2):
        both = turned[part * 2 * owned : (part + 1) * 2 * owned]
        mine = jnp.where(is_first, both[:owned], both[owned:])
        for d in range(SKY_DIRECTIONS):
            out_ref[part, d] = mine[:, d * channels : (d + 1) * channels]


def place_kernel(core_ref, blocks_ref, out_ref):
    write_owned([blocks_ref[p] for p in range(blocks_ref.shape[0])], core_ref[0] == 0, out_ref)


def final_kernel(basis_ref, core_ref, parts_ref, out_ref):
    count = out_ref.shape[3] // 2
    write_owned(consensus_blocks(basis_ref, parts_ref, count), core_ref[0] == 0, out_ref)


def call(name, kernel, out_shape, *inputs, scalars=0, flops=0, scratch=()):
    whole = pl.BlockSpec(memory_space=pltpu.VMEM)
    specs = [pl.BlockSpec(memory_space=pltpu.SMEM)] * scalars + [whole] * (len(inputs) - scalars)
    return pl.pallas_call(
        kernel,
        out_shape=out_shape,
        in_specs=specs,
        out_specs=jax.tree.map(lambda _: whole, out_shape),
        scratch_shapes=list(scratch),
        compiler_params=pltpu.CompilerParams(vmem_limit_bytes=VMEM_LIMIT),
        cost_estimate=pl.CostEstimate(
            flops=flops, bytes_accessed=sum(x.size * x.dtype.itemsize for x in inputs), transcendentals=0
        ),
        name=name,
    )(*inputs)


def shards(vis, coherency, gains_init, station_pairs):
    channels_dev = vis.shape[1]
    rows_dev = vis.shape[2]
    owned = gains_init.shape[3]
    pairs = lax.axis_size("pair")
    bands = lax.axis_size("freq")
    assert channels_dev == 2 * pairs and owned == 16 and STATION_TOTAL == 2 * owned * pairs
    assert ROUNDS == 2 and ITERS == 2
    weight = 2.0 * rows_dev * pairs * 2 / STATION_TOTAL
    swap = [(0, 1), (1, 0)]
    core = lax.axis_index("core").astype(i32).reshape(1)
    basis = lax.dynamic_slice_in_dim(
        jnp.asarray(basis_rows(channels_dev * bands)),
        lax.axis_index("freq") * channels_dev,
        channels_dev,
        1,
    )
    shape = jax.ShapeDtypeStruct
    gains_shape = shape((2, 8, STATION_TOTAL), f32)
    sums_shape = shape((3, 8, STATION_TOTAL), f32)
    block_shape = shape((pairs, 8, LANES), f32)
    parts_shape = shape((bands, 8, LANES), f32)
    out_shape = shape((2, SKY_DIRECTIONS, owned, channels_dev), f32)
    width = 7 * rows_dev // 2 + 2 * LANES
    flops = 2 * rows_dev * pairs * 192 * 256
    scratch = [pltpu.VMEM((48 * PARTS, 2 * LANES), f32)]
    sweep = functools.partial(call, flops=flops, scratch=scratch)
    half_sweep = functools.partial(call, flops=flops // 2, scratch=scratch)

    def exchange(partial):
        return lax.ppermute(partial, "core", swap)

    def to_pairs(block):
        return lax.all_to_all(block, "pair", 0, 0, tiled=True)

    def over_bands(block):
        return lax.all_to_all(block, "freq", 0, 0, tiled=True)

    start = gains_init.transpose(0, 1, 3, 2)
    packed = call(
        "pack",
        pack_kernel,
        shape((pairs, 8, width), bf16),
        core,
        coherency,
        vis,
        station_pairs,
        start,
        exchange(start),
        scalars=1,
    )
    data = to_pairs(packed)

    sums, gains = sweep("first", first_kernel, (sums_shape, gains_shape), data)
    target = gains
    sums, gains = sweep(
        "step",
        functools.partial(step_kernel, weight),
        (sums_shape, gains_shape),
        data,
        sums,
        exchange(sums),
        gains,
    )
    finish = functools.partial(finish_kernel, weight)
    gains, block = call("finish", finish, (gains_shape, block_shape), sums, exchange(sums), gains, target)
    owner_gains = to_pairs(block)
    sums = half_sweep("early", early_kernel, sums_shape, data, gains)
    parts = over_bands(call("fit", fit_kernel, parts_shape, basis, owner_gains, scalars=1))
    sums = half_sweep("late", late_kernel, sums_shape, data, gains, sums)
    block, owner_dual = call(
        "spread", spread_kernel, (block_shape, block_shape), basis, parts, owner_gains, scalars=1
    )
    fit = to_pairs(block)

    sums, gains, target = sweep(
        "retarget",
        functools.partial(retarget_kernel, weight),
        (sums_shape, gains_shape, gains_shape),
        data,
        sums,
        exchange(sums),
        gains,
        fit,
    )
    gains, block = call("finish", finish, (gains_shape, block_shape), sums, exchange(sums), gains, target)
    owner_gains = to_pairs(block)
    parts = over_bands(call("fit", fit_kernel, parts_shape, basis, owner_gains, owner_dual, scalars=1))
    final_gains = call("place", place_kernel, out_shape, core, owner_gains, scalars=1)
    final_consensus = call("final", final_kernel, out_shape, basis, core, parts, scalars=2)
    return (final_gains.transpose(0, 1, 3, 2), final_consensus.transpose(0, 1, 3, 2))


def solution(mesh):
    split = Mesh(
        mesh.devices.reshape(mesh.shape["freq"], mesh.shape["bl"] // 2, 2), ("freq", "pair", "core")
    )
    bl = ("pair", "core")
    placed = (
        P(None, "freq", bl),
        P(None, None, "freq", bl),
        P(None, None, "freq", bl),
        P(None, bl),
    )
    return jax.shard_map(
        shards,
        mesh=split,
        in_specs=placed,
        out_specs=(P(None, None, "freq", bl), P(None, None, "freq", bl)),
        check_vma=False,
    )
```

time: 160 us -> 140 us (0.88)
  blocking collectives: 59 us -> 45.1 us
  local copies, waits for them, and re-layouts: 14.5 us -> 3.9 us
  other arithmetic: 9.03 us -> 0 us
  starting transfers between devices: 13.6 us -> 22 us
  waiting for transfers between devices: 17.2 us -> 24.2 us
  Pallas kernels: 44.9 us -> 43 us
    all_to_all x1 -> x0, blocking collectives: 16.3 us -> none  [shards(): part = lax.all_to_all(part, 'freq', 0, 0, tiled=True)]
    all_to_all x1 -> x2, starting transfers between devices: 3.34 us -> 11.9 us  [over_bands(): return lax.all_to_all(block, 'freq', 0, 0, tiled=True)]
    reshape x16 -> x0, local copies, waits for them, and re-layouts: 5.38 us -> none  [the longest x2 2.87 us: shards(): coh = coherency.reshape(2, SKY_DIRECTIONS, pairs, held, rows_dev)]
    add x5 -> x0, other arithmetic: 3.21 us -> none  [the longest x2 1.61 us: shards(): gains = advance(gains, partial + other, target, weight)]
    all_to_all x1 -> x2, waiting for transfers between devices: 7.86 us -> 11 us  [over_bands(): return lax.all_to_all(block, 'freq', 0, 0, tiled=True)]
    all_to_all x2, blocking collectives: 42.7 us -> 45.1 us  [to_pairs(): return lax.all_to_all(block, 'pair', 0, 0, tiled=True)]
    ppermute x5, waiting for transfers between devices: 3.82 us -> 6.16 us  [exchange(): return lax.ppermute(partial, 'core', swap)]
    unnamed x24 -> x10, local copies, waits for them, and re-layouts: 6.12 us -> 3.83 us
  transfers between devices with their start and end apart: 8 -> 9, of which waited for: 5 -> 9; matrix products, arithmetic and copies ran while one was open for 5% -> 0% of each run, Pallas kernels for 7% -> 7%
where the time goes in v2:
time: 140 us; the launch traced here: 139 us
  blocking collectives  45.1 us (32%)
  Pallas kernels  43 us (31%)
  waiting for transfers between devices  24.2 us (17%)
  starting transfers between devices  22 us (16%)
  local copies, waits for them, and re-layouts  3.9 us (3%)
    all_to_all x2, blocking collectives, to_pairs(): return lax.all_to_all(block, 'pair', 0, 0, tiled=True)  45.1 us
    pallas_call x13, Pallas kernels, call(): pl.pallas_call(kernel, out_shape=out_shape, in_specs=specs, out_specs=jax...  43 us
    all_to_all x2, starting transfers between devices, over_bands(): return lax.all_to_all(block, 'freq', 0, 0, tiled=True)  11.9 us
    all_to_all x2, waiting for transfers between devices, over_bands(): return lax.all_to_all(block, 'freq', 0, 0, tiled=True)  11 us
    all_to_all x2, starting transfers between devices, to_pairs(): return lax.all_to_all(block, 'pair', 0, 0, tiled=True)  9.5 us
    all_to_all x2, waiting for transfers between devices, to_pairs(): return lax.all_to_all(block, 'pair', 0, 0, tiled=True)  7.07 us
    ppermute x5, waiting for transfers between devices, exchange(): return lax.ppermute(partial, 'core', swap)  6.16 us
    unnamed x10, local copies, waits for them, and re-layouts  3.83 us
  transfers between devices with their start and end apart: 9, of which 9 were waited for; matrix products, arithmetic and copies ran while one was open for 0% of the time, Pallas kernels for 7%

profile of v2, /device:TPU:2, one launch (start us, length us, event | category | flops | bytes accessed | tf_op | source)
XLA Modules:
  0.0 138.9 jit_solution(14568200402260816253)
XLA Ops:
  0.6 0.1 collective-permute-start
  0.7 1.4 %collective-permute-done.other_ref = f32[2,4,16,32]{3,2,1,0:T(8,128)S(1)} collective-permute-done((f32[2,4,16,32]{3,2,1,0:T(8,128)}, f32[2,4,16,32]{3,2,1,0:T(8,128)S(1)}, u32[]{:S(2)}, u32[]{:S(2)}) %collective-permute-start) | collective-permute-done | bytes 16416 | tf_op jit(solution)/shard_map/ppermute | solution.py:403
  2.2 0.0 copy-start
  2.2 1.2 copy-done
  3.4 0.0 copy-start.1
  3.4 1.0 copy-done.1
  4.5 0.0 copy-start.2
  4.5 0.8 copy-done.2
  5.3 0.0 copy-start.3
  5.3 0.7 copy-done.3
  6.0 1.2 pack.1
  7.2 32.5 %all_to_all.30.data_ref = bf16[16,8,7424]{2,1,0:T(8,128)(2,1)S(1)} all-to-all(bf16[16,8,7424]{2,1,0:T(8,128)(2,1)S(1)} %pack.1), channel_id=1, replica_groups=mesh['freq'=8,'pair'=16,'core'=2] {'pair'}, dimensions={0} | all-to-all | bytes 3801088 | tf_op jit(solution)/shard_map/all_to_all | solution.py:406
  39.7 8.7 %first.1 = (f32[3,8,512]{2,1,0:T(8,128)S(1)}, f32[2,8,512]{2,1,0:T(8,128)S(1)}) custom-call(bf16[16,8,7424]{2,1,0:T(8,128)(2,1)S(1)} %all_to_all.30.data_ref), custom_call_target="tpu_custom_call" | custom-call | flops 3221225472 | bytes 1900544 | tf_op jit(solution)/shard_map/first/pallas_call | solution.py:359
  48.3 0.1 collective-permute-start.1
  48.4 1.2 collective-permute-done.1.other_ref
  49.7 0.0 copy-start.4
  49.7 8.5 %step.1 = (f32[3,8,512]{2,1,0:T(8,128)S(1)}, f32[2,8,512]{2,1,0:T(8,128)S(1)}) custom-call(bf16[16,8,7424]{2,1,0:T(8,128)(2,1)S(1)} %all_to_all.30.data_ref, f32[3,8,512]{2,1,0:T(8,128)S(1)} %get-tuple-element.14.mine_ref, f32[3,8,512]{2,1,0:T(8,128)S(1)} %collective-permute-done.1.other_ref, f32[2,8,512]{2,1,0:T(8,128)S(1)} %get-tuple-element.15.gains_ref.target_ref), custom_call_target="tpu_custom_call" | custom-call | flops 3221225472 | bytes 2031616 | tf_op jit(solution)/shard_map/step/pallas_call | solution.py:359
  58.2 0.3 collective-permute-start.2
  58.4 1.1 collective-permute-done.2.other_ref
  59.5 0.7 finish.2
  60.2 4.8 %all-to-all-start.1 = ((f32[16,8,128]{2,1,0:T(8,128)}), f32[16,8,128]{2,1,0:T(8,128)S(1)}, u32[]{:S(2)}, u32[]{:S(2)}) async-start(f32[16,8,128]{2,1,0:T(8,128)} %get-tuple-element.19), calls=%async_computation.1 | async-start | bytes 131072 | tf_op jit(solution)/shard_map/all_to_all | solution.py:406
  65.0 0.0 copy-done.4
  65.0 0.1 constant_dynamic-slice_fusion.basis_ref
  65.0 6.3 %all-to-all-done.1.refs_0_.gains_ref = f32[16,8,128]{2,1,0:T(8,128)S(1)} async-done(((f32[16,8,128]{2,1,0:T(8,128)}), f32[16,8,128]{2,1,0:T(8,128)S(1)}, u32[]{:S(2)}, u32[]{:S(2)}) %all-to-all-start.1) | async-done | bytes 65568 | tf_op jit(solution)/shard_map/all_to_all | solution.py:406
  71.3 1.3 fit.2
  72.6 8.5 %all-to-all-start.2 = ((f32[8,8,128]{2,1,0:T(8,128)}), f32[8,8,128]{2,1,0:T(8,128)S(1)}, u32[]{:S(2)}, u32[]{:S(2)}) async-start(f32[8,8,128]{2,1,0:T(8,128)} %fit.2), calls=%async_computation.2 | async-start | bytes 65536 | tf_op jit(solution)/shard_map/all_to_all | solution.py:409
  81.1 4.3 %early.1.before_ref = f32[3,8,512]{2,1,0:T(8,128)S(1)} custom-call(bf16[16,8,7424]{2,1,0:T(8,128)(2,1)S(1)} %all_to_all.30.data_ref, f32[2,8,512]{2,1,0:T(8,128)S(1)} %get-tuple-element.18.gains_ref), custom_call_target="tpu_custom_call" | custom-call | flops 1610612736 | bytes 1933312 | tf_op jit(solution)/shard_map/early/pallas_call | solution.py:359
  85.4 3.8 %all-to-all-done.2.parts_ref = f32[8,8,128]{2,1,0:T(8,128)S(1)} async-done(((f32[8,8,128]{2,1,0:T(8,128)}), f32[8,8,128]{2,1,0:T(8,128)S(1)}, u32[]{:S(2)}, u32[]{:S(2)}) %all-to-all-start.2) | async-done | bytes 32800 | tf_op jit(solution)/shard_map/all_to_all | solution.py:409
  89.1 1.3 spread.1
  90.4 4.7 %all-to-all-start.3 = ((f32[16,8,128]{2,1,0:T(8,128)}), f32[16,8,128]{2,1,0:T(8,128)S(1)}, u32[]{:S(2)}, u32[]{:S(2)}) async-start(f32[16,8,128]{2,1,0:T(8,128)} %get-tuple-element.20), calls=%async_computation.3 | async-start | bytes 131072 | tf_op jit(solution)/shard_map/all_to_all | solution.py:406
  95.2 4.3 %late.1.mine_ref = f32[3,8,512]{2,1,0:T(8,128)S(1)} custom-call(bf16[16,8,7424]{2,1,0:T(8,128)(2,1)S(1)} %all_to_all.30.data_ref, f32[2,8,512]{2,1,0:T(8,128)S(1)} %get-tuple-element.18.gains_ref, f32[3,8,512]{2,1,0:T(8,128)S(1)} %early.1.before_ref), custom_call_target="tpu_custom_call" | custom-call | flops 1610612736 | bytes 1982464 | tf_op jit(solution)/shard_map/late/pallas_call | solution.py:359
  99.4 0.1 collective-permute-start.3
  99.5 1.2 collective-permute-done.3.other_ref
  100.7 0.8 all-to-all-done.3.fit_ref
  101.5 8.6 %retarget.1 = (f32[3,8,512]{2,1,0:T(8,128)S(1)}, f32[2,8,512]{2,1,0:T(8,128)S(1)}, f32[2,8,512]{2,1,0:T(8,128)S(1)}) custom-call(bf16[16,8,7424]{2,1,0:T(8,128)(2,1)S(1)} %all_to_all.30.data_ref, f32[3,8,512]{2,1,0:T(8,128)S(1)} %late.1.mine_ref, f32[3,8,512]{2,1,0:T(8,128)S(1)} %collective-permute-done.3.other_ref, ...), custom_call_target="tpu_custom_call" | custom-call | flops 3221225472 | bytes 2097152 | tf_op jit(solution)/shard_map/retarget/pallas_call | solution.py:359
  110.2 0.1 collective-permute-start.4
  110.3 1.2 collective-permute-done.4.other_ref
  111.5 0.6 finish.3
  112.1 12.6 %all_to_all.31.blocks_ref.refs_0_ = f32[16,8,128]{2,1,0:T(8,128)S(1)} all-to-all(f32[16,8,128]{2,1,0:T(8,128)S(1)} %get-tuple-element.24), channel_id=1, replica_groups=mesh['freq'=8,'pair'=16,'core'=2] {'pair'}, dimensions={0} | all-to-all | bytes 131072 | tf_op jit(solution)/shard_map/all_to_all | solution.py:406
  124.7 1.3 fit.3
  126.0 3.5 %all-to-all-start.5 = ((f32[8,8,128]{2,1,0:T(8,128)}), f32[8,8,128]{2,1,0:T(8,128)S(1)}, u32[]{:S(2)}, u32[]{:S(2)}) async-start(f32[8,8,128]{2,1,0:T(8,128)} %fit.3), calls=%async_computation.5 | async-start | bytes 65536 | tf_op jit(solution)/shard_map/all_to_all | solution.py:409
  129.5 0.8 place.1
  130.3 7.2 %all-to-all-done.5.parts_ref = f32[8,8,128]{2,1,0:T(8,128)S(1)} async-done(((f32[8,8,128]{2,1,0:T(8,128)}), f32[8,8,128]{2,1,0:T(8,128)S(1)}, u32[]{:S(2)}, u32[]{:S(2)}) %all-to-all-start.5) | async-done | bytes 32800 | tf_op jit(solution)/shard_map/all_to_all | solution.py:409
  137.5 1.4 %final.1 = f32[2,4,16,32]{3,2,1,0:T(8,128)} custom-call(f32[4,32]{1,0:T(4,128)S(1)} %constant_dynamic-slice_fusion.basis_ref, s32[1]{0:T(128)} %bitcast.core_ref, f32[8,8,128]{2,1,0:T(8,128)S(1)} %all-to-all-done.5.parts_ref), custom_call_target="tpu_custom_call" | custom-call | bytes 33284 | tf_op jit(solution)/shard_map/final/pallas_call | solution.py:359
Async XLA Ops:
  0.6 1.6 %collective-permute-start = (f32[2,4,16,32]{3,2,1,0:T(8,128)}, f32[2,4,16,32]{3,2,1,0:T(8,128)S(1)}, u32[]{:S(2)}, u32[]{:S(2)}) collective-permute-start(f32[2,4,16,32]{3,2,1,0:T(8,128)} %bitcast.4), channel_id=1, source_target_pairs={{0,1},{1,0},{2,3},{3,2},{4,5},{5,4},{6,7},{7,6},{8,9},{9,8},{10,11... | collective-permute-start | bytes 49160 | tf_op jit(solution)/shard_map/ppermute | solution.py:403
  2.2 1.2 copy-start
  3.4 1.0 copy-start.1
  4.5 0.8 copy-start.2
  5.3 0.7 copy-start.3
  48.3 1.3 collective-permute-start.1
  49.7 15.3 %copy-start.4 = (f32[4,256]{1,0:T(4,128)S(1)}, f32[4,256]{1,0:T(4,128)}, u32[]{:S(2)}) copy-start(f32[4,256]{1,0:T(4,128)} %constant.18.clone) | copy-start | bytes 12292
  58.2 1.3 collective-permute-start.2
  60.2 11.1 %all-to-all-start.1 = ((f32[16,8,128]{2,1,0:T(8,128)}), f32[16,8,128]{2,1,0:T(8,128)S(1)}, u32[]{:S(2)}, u32[]{:S(2)}) async-start(f32[16,8,128]{2,1,0:T(8,128)} %get-tuple-element.19), calls=%async_computation.1 | async-start | bytes 131072 | tf_op jit(solution)/shard_map/all_to_all | solution.py:406
  72.6 16.5 %all-to-all-start.2 = ((f32[8,8,128]{2,1,0:T(8,128)}), f32[8,8,128]{2,1,0:T(8,128)S(1)}, u32[]{:S(2)}, u32[]{:S(2)}) async-start(f32[8,8,128]{2,1,0:T(8,128)} %fit.2), calls=%async_computation.2 | async-start | bytes 65536 | tf_op jit(solution)/shard_map/all_to_all | solution.py:409
  90.4 11.1 %all-to-all-start.3 = ((f32[16,8,128]{2,1,0:T(8,128)}), f32[16,8,128]{2,1,0:T(8,128)S(1)}, u32[]{:S(2)}, u32[]{:S(2)}) async-start(f32[16,8,128]{2,1,0:T(8,128)} %get-tuple-element.20), calls=%async_computation.3 | async-start | bytes 131072 | tf_op jit(solution)/shard_map/all_to_all | solution.py:406
  99.4 1.3 collective-permute-start.3
  110.2 1.3 collective-permute-start.4
  126.0 11.5 %all-to-all-start.5 = ((f32[8,8,128]{2,1,0:T(8,128)}), f32[8,8,128]{2,1,0:T(8,128)S(1)}, u32[]{:S(2)}, u32[]{:S(2)}) async-start(f32[8,8,128]{2,1,0:T(8,128)} %fit.3), calls=%async_computation.5 | async-start | bytes 65536 | tf_op jit(solution)/shard_map/all_to_all | solution.py:409

commit v3 on v2

--- a/solution.py
+++ b/solution.py
@@ -15,6 +15,8 @@
 LANES = 128
 PARTS = STATION_TOTAL // LANES
 UNROLL = 2
+COPIES = 4
+PACK_VMEM_LIMIT = 58 * 1024 * 1024
 VMEM_LIMIT = 24 * 1024 * 1024
 f32, bf16, i32 = jnp.float32, jnp.bfloat16, jnp.int32
 
@@ -37,11 +39,31 @@
     return jnp.concatenate([block[2 * pair : 2 * pair + 2] for block in by_direction], 0)
 
 
-def pack_kernel(core_ref, coh_ref, vis_ref, pairs_ref, mine_ref, other_ref, out_ref):
+def pack_kernel(
+    core_ref, coh_hbm, vis_hbm, pairs_ref, mine_ref, other_ref, out_ref, coh_ref, vis_ref, coh_sem, vis_sem
+):
     rows = vis_ref.shape[2]
     count = out_ref.shape[0]
     at = lanes_of(rows)
     half = rows // 2
+    piece = half // COPIES
+    copies = []
+    for index in range(COPIES):
+        group = []
+        for side in range(2):
+            lanes = pl.ds(side * half + index * piece, piece)
+            slot = 2 * index + side
+            group.append(
+                pltpu.make_async_copy(
+                    coh_hbm.at[:, :, :, lanes], coh_ref.at[:, :, :, lanes], coh_sem.at[slot]
+                )
+            )
+            group.append(
+                pltpu.make_async_copy(vis_hbm.at[:, :, lanes], vis_ref.at[:, :, lanes], vis_sem.at[slot])
+            )
+        for copy in group:
+            copy.start()
+        copies.append(group)
 
     def columns(index, carry):
         early = pl.multiple_of(index * LANES, LANES)
@@ -71,7 +93,6 @@
             out_ref[p, :, pl.ds(place, LANES)] = pick_channel_pair(lower, p).astype(bf16)
         return carry
 
-    lax.fori_loop(0, half // LANES, columns, 0)
     is_first = core_ref[0] == 0
     for part in range(2):
         mine = jnp.concatenate([mine_ref[part, d] for d in range(SKY_DIRECTIONS)], 1)
@@ -85,6 +106,11 @@
         place = at["start"] + part * LANES
         for p in range(count):
             out_ref[p, :, place : place + LANES] = pick_channel_pair(blocks, p).astype(bf16)
+    step = piece // LANES
+    for index, group in enumerate(copies):
+        for copy in group:
+            copy.wait()
+        lax.fori_loop(index * step, (index + 1) * step, columns, 0)
 
 
 def stations_in_lanes(pieces):
@@ -287,8 +313,7 @@
 
 
 def basis_column(basis_ref, row, source):
-    even = is_even((8, LANES))
-    return jnp.where(even, basis_ref[row, 2 * source], basis_ref[row, 2 * source + 1])
+    return basis_ref[row, source]
 
 
 def fit_kernel(basis_ref, *refs):
@@ -348,21 +373,25 @@
     write_owned([blocks_ref[p] for p in range(blocks_ref.shape[0])], core_ref[0] == 0, out_ref)
 
 
-def final_kernel(basis_ref, core_ref, parts_ref, out_ref):
+def final_kernel(core_ref, basis_ref, parts_ref, out_ref):
     count = out_ref.shape[3] // 2
     write_owned(consensus_blocks(basis_ref, parts_ref, count), core_ref[0] == 0, out_ref)
 
 
-def call(name, kernel, out_shape, *inputs, scalars=0, flops=0, scratch=()):
+def call(
+    name, kernel, out_shape, *inputs, scalars=0, held=0, flops=0, scratch=(), limit=VMEM_LIMIT
+):
     whole = pl.BlockSpec(memory_space=pltpu.VMEM)
-    specs = [pl.BlockSpec(memory_space=pltpu.SMEM)] * scalars + [whole] * (len(inputs) - scalars)
+    specs = [pl.BlockSpec(memory_space=pltpu.SMEM)] * scalars
+    specs += [pl.BlockSpec(memory_space=pltpu.HBM)] * held
+    specs += [whole] * (len(inputs) - len(specs))
     return pl.pallas_call(
         kernel,
         out_shape=out_shape,
         in_specs=specs,
         out_specs=jax.tree.map(lambda _: whole, out_shape),
         scratch_shapes=list(scratch),
-        compiler_params=pltpu.CompilerParams(vmem_limit_bytes=VMEM_LIMIT),
+        compiler_params=pltpu.CompilerParams(vmem_limit_bytes=limit),
         cost_estimate=pl.CostEstimate(
             flops=flops, bytes_accessed=sum(x.size * x.dtype.itemsize for x in inputs), transcendentals=0
         ),
@@ -387,6 +416,8 @@
         channels_dev,
         1,
     )
+    basis = basis.reshape(4, pairs, 1, 2, 1)
+    basis = jnp.broadcast_to(basis, (4, pairs, SKY_DIRECTIONS, 2, LANES)).reshape(4, pairs, 8, LANES)
     shape = jax.ShapeDtypeStruct
     gains_shape = shape((2, 8, STATION_TOTAL), f32)
     sums_shape = shape((3, 8, STATION_TOTAL), f32)
@@ -420,6 +451,14 @@
         start,
         exchange(start),
         scalars=1,
+        held=2,
+        limit=PACK_VMEM_LIMIT,
+        scratch=[
+            pltpu.VMEM(coherency.shape, bf16),
+            pltpu.VMEM(vis.shape, f32),
+            pltpu.SemaphoreType.DMA((2 * COPIES,)),
+            pltpu.SemaphoreType.DMA((2 * COPIES,)),
+        ],
     )
     data = to_pairs(packed)
 
@@ -438,10 +477,12 @@
     gains, block = call("finish", finish, (gains_shape, block_shape), sums, exchange(sums), gains, target)
     owner_gains = to_pairs(block)
     sums = half_sweep("early", early_kernel, sums_shape, data, gains)
-    parts = over_bands(call("fit", fit_kernel, parts_shape, basis, owner_gains, scalars=1))
+    owner_gains, sums = lax.optimization_barrier((owner_gains, sums))
+    parts = over_bands(call("fit", fit_kernel, parts_shape, basis, owner_gains))
     sums = half_sweep("late", late_kernel, sums_shape, data, gains, sums)
+    parts, sums = lax.optimization_barrier((parts, sums))
     block, owner_dual = call(
-        "spread", spread_kernel, (block_shape, block_shape), basis, parts, owner_gains, scalars=1
+        "spread", spread_kernel, (block_shape, block_shape), basis, parts, owner_gains
     )
     fit = to_pairs(block)
 
@@ -457,9 +498,9 @@
     )
     gains, block = call("finish", finish, (gains_shape, block_shape), sums, exchange(sums), gains, target)
     owner_gains = to_pairs(block)
-    parts = over_bands(call("fit", fit_kernel, parts_shape, basis, owner_gains, owner_dual, scalars=1))
+    parts = over_bands(call("fit", fit_kernel, parts_shape, basis, owner_gains, owner_dual))
     final_gains = call("place", place_kernel, out_shape, core, owner_gains, scalars=1)
-    final_consensus = call("final", final_kernel, out_shape, basis, core, parts, scalars=2)
+    final_consensus = call("final", final_kernel, out_shape, core, basis, parts, scalars=1)
     return (final_gains.transpose(0, 1, 3, 2), final_consensus.transpose(0, 1, 3, 2))
 
 

time: 140 us -> 136 us (0.971)
  local copies, waits for them, and re-layouts: 3.9 us -> 1.65 us
  blocking collectives: 45.1 us -> 43.5 us
    unnamed x10 -> x2, local copies, waits for them, and re-layouts: 3.83 us -> 0.63 us
    all_to_all x2, blocking collectives: 45.1 us -> 43.5 us  [to_pairs(): return lax.all_to_all(block, 'pair', 0, 0, tiled=True)]
  transfers between devices with their start and end apart: 9 -> 9, of which waited for: 9 -> 9; matrix products, arithmetic and copies ran while one was open for 0% -> 1% of each run, Pallas kernels for 7% -> 7%
where the time goes in v3:
time: 136 us
  Pallas kernels  43.8 us (32%)
  blocking collectives  43.5 us (32%)
  waiting for transfers between devices  23.4 us (17%)
  starting transfers between devices  22.4 us (16%)
  local copies, waits for them, and re-layouts  1.65 us (1%)
    pallas_call x13, Pallas kernels, call(): pl.pallas_call(kernel, out_shape=out_shape, in_specs=specs, out_specs=jax...  43.8 us
    all_to_all x2, blocking collectives, to_pairs(): return lax.all_to_all(block, 'pair', 0, 0, tiled=True)  43.5 us
    all_to_all x2, starting transfers between devices, over_bands(): return lax.all_to_all(block, 'freq', 0, 0, tiled=True)  11.9 us
    all_to_all x2, waiting for transfers between devices, over_bands(): return lax.all_to_all(block, 'freq', 0, 0, tiled=True)  11 us
    all_to_all x2, starting transfers between devices, to_pairs(): return lax.all_to_all(block, 'pair', 0, 0, tiled=True)  9.95 us
    all_to_all x2, waiting for transfers between devices, to_pairs(): return lax.all_to_all(block, 'pair', 0, 0, tiled=True)  7.17 us
    ppermute x5, waiting for transfers between devices, exchange(): return lax.ppermute(partial, 'core', swap)  5.27 us
  transfers between devices with their start and end apart: 9, of which 9 were waited for; matrix products, arithmetic and copies ran while one was open for 1% of the time, Pallas kernels for 7%

profile of v3, /device:TPU:2, one launch (start us, length us, event | category | flops | bytes accessed | tf_op | source)
XLA Modules:
  0.0 135.5 jit_solution(12064858556280477668)
XLA Ops:
  0.6 0.1 collective-permute-start
  0.7 1.4 %collective-permute-done.other_ref = f32[2,4,16,32]{3,2,1,0:T(8,128)S(1)} collective-permute-done((f32[2,4,16,32]{3,2,1,0:T(8,128)}, f32[2,4,16,32]{3,2,1,0:T(8,128)S(1)}, u32[]{:S(2)}, u32[]{:S(2)}) %collective-permute-start) | collective-permute-done | bytes 16416 | tf_op jit(solution)/shard_map/ppermute | solution.py:434
  2.2 0.0 copy-start
  2.2 0.6 copy-done
  2.8 4.3 %pack.1 = bf16[16,8,7424]{2,1,0:T(8,128)(2,1)} custom-call(s32[1]{0:T(128)} %bitcast.core_ref, bf16[2,4,32,2048]{3,2,1,0:T(8,128)(2,1)} %coh_hbm.1, f32[2,32,2048]{2,1,0:T(8,128)} %vis_hbm.1, s32[2,2048]{1,0:T(2,128)} %pairs_ref.1, f32[2,4,16,32]{3,2,1,0:T(8,128)} %bitcast.7, f32[2,4,16,32]{3,2,1,0:T(8,128)} %copy-done), custom_call_target="tpu_custom_call" | custom-call | bytes 1622020 | tf_op jit(solution)/shard_map/pack/pallas_call | solution.py:388
  7.1 32.7 %all_to_all.30.data_ref = bf16[16,8,7424]{2,1,0:T(8,128)(2,1)S(1)} all-to-all(bf16[16,8,7424]{2,1,0:T(8,128)(2,1)} %pack.1), channel_id=1, replica_groups=mesh['freq'=8,'pair'=16,'core'=2] {'pair'}, dimensions={0} | all-to-all | bytes 3801088 | tf_op jit(solution)/shard_map/all_to_all | solution.py:437
  39.9 8.7 %first.1 = (f32[3,8,512]{2,1,0:T(8,128)S(1)}, f32[2,8,512]{2,1,0:T(8,128)S(1)}) custom-call(bf16[16,8,7424]{2,1,0:T(8,128)(2,1)S(1)} %all_to_all.30.data_ref), custom_call_target="tpu_custom_call" | custom-call | flops 3221225472 | bytes 1900544 | tf_op jit(solution)/shard_map/first/pallas_call | solution.py:388
  48.5 0.1 collective-permute-start.1
  48.6 1.2 collective-permute-done.1.other_ref
  49.8 8.5 %step.1 = (f32[3,8,512]{2,1,0:T(8,128)S(1)}, f32[2,8,512]{2,1,0:T(8,128)S(1)}) custom-call(bf16[16,8,7424]{2,1,0:T(8,128)(2,1)S(1)} %all_to_all.30.data_ref, f32[3,8,512]{2,1,0:T(8,128)S(1)} %get-tuple-element.18.mine_ref, f32[3,8,512]{2,1,0:T(8,128)S(1)} %collective-permute-done.1.other_ref, f32[2,8,512]{2,1,0:T(8,128)S(1)} %get-tuple-element.19.gains_ref.target_ref), custom_call_target="tpu_custom_call" | custom-call | flops 3221225472 | bytes 2031616 | tf_op jit(solution)/shard_map/step/pallas_call | solution.py:388
  58.3 0.2 collective-permute-start.2
  58.6 0.7 constant_dynamic-slice_fusion
  59.3 0.1 copy.8
  59.4 0.1 copy.9
  59.5 0.2 collective-permute-done.2.other_ref
  59.6 0.7 finish.2
  60.4 4.8 %all-to-all-start.1 = ((f32[16,8,128]{2,1,0:T(8,128)}), f32[16,8,128]{2,1,0:T(8,128)S(1)}, u32[]{:S(2)}, u32[]{:S(2)}) async-start(f32[16,8,128]{2,1,0:T(8,128)} %get-tuple-element.22), calls=%async_computation.1 | async-start | bytes 131072 | tf_op jit(solution)/shard_map/all_to_all | solution.py:437
  65.1 4.3 %early.1.before_ref = f32[3,8,512]{2,1,0:T(8,128)S(1)} custom-call(bf16[16,8,7424]{2,1,0:T(8,128)(2,1)S(1)} %all_to_all.30.data_ref, f32[2,8,512]{2,1,0:T(8,128)S(1)} %get-tuple-element.23.gains_ref), custom_call_target="tpu_custom_call" | custom-call | flops 1610612736 | bytes 1933312 | tf_op jit(solution)/shard_map/early/pallas_call | solution.py:388
  69.4 2.1 %all-to-all-done.1.refs_0_.gains_ref = f32[16,8,128]{2,1,0:T(8,128)S(1)} async-done(((f32[16,8,128]{2,1,0:T(8,128)}), f32[16,8,128]{2,1,0:T(8,128)S(1)}, u32[]{:S(2)}, u32[]{:S(2)}) %all-to-all-start.1) | async-done | bytes 65568 | tf_op jit(solution)/shard_map/all_to_all | solution.py:437
  71.5 0.1 broadcast_in_dim.14.basis_ref
  71.6 0.7 fit.2
  72.4 8.5 %all-to-all-start.2 = ((f32[8,8,128]{2,1,0:T(8,128)}), f32[8,8,128]{2,1,0:T(8,128)S(1)}, u32[]{:S(2)}, u32[]{:S(2)}) async-start(f32[8,8,128]{2,1,0:T(8,128)} %fit.2), calls=%async_computation.2 | async-start | bytes 65536 | tf_op jit(solution)/shard_map/all_to_all | solution.py:440
  80.8 4.3 %late.1.mine_ref = f32[3,8,512]{2,1,0:T(8,128)S(1)} custom-call(bf16[16,8,7424]{2,1,0:T(8,128)(2,1)S(1)} %all_to_all.30.data_ref, f32[2,8,512]{2,1,0:T(8,128)S(1)} %get-tuple-element.23.gains_ref, f32[3,8,512]{2,1,0:T(8,128)S(1)} %early.1.before_ref), custom_call_target="tpu_custom_call" | custom-call | flops 1610612736 | bytes 1982464 | tf_op jit(solution)/shard_map/late/pallas_call | solution.py:388
  85.1 3.8 %all-to-all-done.2.parts_ref = f32[8,8,128]{2,1,0:T(8,128)S(1)} async-done(((f32[8,8,128]{2,1,0:T(8,128)}), f32[8,8,128]{2,1,0:T(8,128)S(1)}, u32[]{:S(2)}, u32[]{:S(2)}) %all-to-all-start.2) | async-done | bytes 32800 | tf_op jit(solution)/shard_map/all_to_all | solution.py:440
  88.9 0.7 spread.1
  89.6 5.2 %all-to-all-start.3 = ((f32[16,8,128]{2,1,0:T(8,128)}), f32[16,8,128]{2,1,0:T(8,128)S(1)}, u32[]{:S(2)}, u32[]{:S(2)}) async-start(f32[16,8,128]{2,1,0:T(8,128)} %get-tuple-element.28), calls=%async_computation.3 | async-start | bytes 131072 | tf_op jit(solution)/shard_map/all_to_all | solution.py:437
  94.8 0.0 collective-permute-start.3
  94.8 1.2 collective-permute-done.3.other_ref
  96.0 5.1 %all-to-all-done.3.fit_ref = f32[16,8,128]{2,1,0:T(8,128)S(1)} async-done(((f32[16,8,128]{2,1,0:T(8,128)}), f32[16,8,128]{2,1,0:T(8,128)S(1)}, u32[]{:S(2)}, u32[]{:S(2)}) %all-to-all-start.3) | async-done | bytes 65568 | tf_op jit(solution)/shard_map/all_to_all | solution.py:437
  101.1 8.6 %retarget.1 = (f32[3,8,512]{2,1,0:T(8,128)S(1)}, f32[2,8,512]{2,1,0:T(8,128)S(1)}, f32[2,8,512]{2,1,0:T(8,128)S(1)}) custom-call(bf16[16,8,7424]{2,1,0:T(8,128)(2,1)S(1)} %all_to_all.30.data_ref, f32[3,8,512]{2,1,0:T(8,128)S(1)} %late.1.mine_ref, f32[3,8,512]{2,1,0:T(8,128)S(1)} %collective-permute-done.3.other_ref, ...), custom_call_target="tpu_custom_call" | custom-call | flops 3221225472 | bytes 2097152 | tf_op jit(solution)/shard_map/retarget/pallas_call | solution.py:388
  109.7 0.1 collective-permute-start.4
  109.8 1.2 collective-permute-done.4.other_ref
  111.0 0.6 finish.3
  111.7 10.8 %all_to_all.31.blocks_ref.refs_0_ = f32[16,8,128]{2,1,0:T(8,128)S(1)} all-to-all(f32[16,8,128]{2,1,0:T(8,128)S(1)} %get-tuple-element.32), channel_id=1, replica_groups=mesh['freq'=8,'pair'=16,'core'=2] {'pair'}, dimensions={0} | all-to-all | bytes 131072 | tf_op jit(solution)/shard_map/all_to_all | solution.py:437
  122.4 0.7 fit.3
  123.2 3.5 %all-to-all-start.5 = ((f32[8,8,128]{2,1,0:T(8,128)}), f32[8,8,128]{2,1,0:T(8,128)S(1)}, u32[]{:S(2)}, u32[]{:S(2)}) async-start(f32[8,8,128]{2,1,0:T(8,128)} %fit.3), calls=%async_computation.5 | async-start | bytes 65536 | tf_op jit(solution)/shard_map/all_to_all | solution.py:440
  126.6 0.8 place.1
  127.4 7.2 %all-to-all-done.5.parts_ref = f32[8,8,128]{2,1,0:T(8,128)S(1)} async-done(((f32[8,8,128]{2,1,0:T(8,128)}), f32[8,8,128]{2,1,0:T(8,128)S(1)}, u32[]{:S(2)}, u32[]{:S(2)}) %all-to-all-start.5) | async-done | bytes 32800 | tf_op jit(solution)/shard_map/all_to_all | solution.py:440
  134.7 0.9 final.1
  (1 shorter events, 0.0 us)
Async XLA Ops:
  0.6 1.6 %collective-permute-start = (f32[2,4,16,32]{3,2,1,0:T(8,128)}, f32[2,4,16,32]{3,2,1,0:T(8,128)S(1)}, u32[]{:S(2)}, u32[]{:S(2)}) collective-permute-start(f32[2,4,16,32]{3,2,1,0:T(8,128)} %bitcast.6), channel_id=1, source_target_pairs={{0,1},{1,0},{2,3},{3,2},{4,5},{5,4},{6,7},{7,6},{8,9},{9,8},{10,11... | collective-permute-start | bytes 49160 | tf_op jit(solution)/shard_map/ppermute | solution.py:434
  2.2 0.6 copy-start
  48.5 1.3 collective-permute-start.1
  58.3 1.3 collective-permute-start.2
  60.4 11.1 %all-to-all-start.1 = ((f32[16,8,128]{2,1,0:T(8,128)}), f32[16,8,128]{2,1,0:T(8,128)S(1)}, u32[]{:S(2)}, u32[]{:S(2)}) async-start(f32[16,8,128]{2,1,0:T(8,128)} %get-tuple-element.22), calls=%async_computation.1 | async-start | bytes 131072 | tf_op jit(solution)/shard_map/all_to_all | solution.py:437
  72.4 16.5 %all-to-all-start.2 = ((f32[8,8,128]{2,1,0:T(8,128)}), f32[8,8,128]{2,1,0:T(8,128)S(1)}, u32[]{:S(2)}, u32[]{:S(2)}) async-start(f32[8,8,128]{2,1,0:T(8,128)} %fit.2), calls=%async_computation.2 | async-start | bytes 65536 | tf_op jit(solution)/shard_map/all_to_all | solution.py:440
  89.6 11.5 %all-to-all-start.3 = ((f32[16,8,128]{2,1,0:T(8,128)}), f32[16,8,128]{2,1,0:T(8,128)S(1)}, u32[]{:S(2)}, u32[]{:S(2)}) async-start(f32[16,8,128]{2,1,0:T(8,128)} %get-tuple-element.28), calls=%async_computation.3 | async-start | bytes 131072 | tf_op jit(solution)/shard_map/all_to_all | solution.py:437
  94.8 1.2 collective-permute-start.3
  109.7 1.3 collective-permute-start.4
  123.2 11.5 %all-to-all-start.5 = ((f32[8,8,128]{2,1,0:T(8,128)}), f32[8,8,128]{2,1,0:T(8,128)S(1)}, u32[]{:S(2)}, u32[]{:S(2)}) async-start(f32[8,8,128]{2,1,0:T(8,128)} %fit.3), calls=%async_computation.5 | async-start | bytes 65536 | tf_op jit(solution)/shard_map/all_to_all | solution.py:440

commit v4 on v3

--- a/solution.py
+++ b/solution.py
@@ -14,11 +14,11 @@
 ROUNDS = 2
 LANES = 128
 PARTS = STATION_TOTAL // LANES
-UNROLL = 2
+UNROLL = 8
 COPIES = 4
 PACK_VMEM_LIMIT = 58 * 1024 * 1024
 VMEM_LIMIT = 24 * 1024 * 1024
-f32, bf16, i32 = jnp.float32, jnp.bfloat16, jnp.int32
+f32, bf16, i32, i16 = jnp.float32, jnp.bfloat16, jnp.int32, jnp.int16
 
 
 def basis_rows(channels):
@@ -40,13 +40,15 @@
 
 
 def pack_kernel(
-    core_ref, coh_hbm, vis_hbm, pairs_ref, mine_ref, other_ref, out_ref, coh_ref, vis_ref, coh_sem, vis_sem
+    coh_hbm, vis_hbm, pairs_hbm, out_hbm, coh_ref, vis_ref, pairs_ref, out_ref, coh_sem, vis_sem, pairs_sem, out_sem
 ):
     rows = vis_ref.shape[2]
     count = out_ref.shape[0]
     at = lanes_of(rows)
     half = rows // 2
     piece = half // COPIES
+    pairs_copy = pltpu.make_async_copy(pairs_hbm, pairs_ref, pairs_sem)
+    pairs_copy.start()
     copies = []
     for index in range(COPIES):
         group = []
@@ -93,6 +95,24 @@
             out_ref[p, :, pl.ds(place, LANES)] = pick_channel_pair(lower, p).astype(bf16)
         return carry
 
+    pairs_copy.wait()
+    step = piece // LANES
+    sent = []
+    for index, group in enumerate(copies):
+        for copy in group:
+            copy.wait()
+        lax.fori_loop(index * step, (index + 1) * step, columns, 0)
+        for start in (at["re"], at["re"] + half, at["im"], at["im"] + half, at["misc"], at["misc"] + half, at["low"]):
+            lanes = pl.ds(start + index * piece, piece)
+            copy = pltpu.make_async_copy(out_ref.at[:, :, lanes], out_hbm.at[:, :, lanes], out_sem.at[len(sent)])
+            copy.start()
+            sent.append(copy)
+    for copy in sent:
+        copy.wait()
+
+
+def seed_kernel(core_ref, mine_ref, other_ref, packed_hbm, out_hbm, block_ref, block_sem):
+    count = block_ref.shape[0]
     is_first = core_ref[0] == 0
     for part in range(2):
         mine = jnp.concatenate([mine_ref[part, d] for d in range(SKY_DIRECTIONS)], 1)
@@ -103,14 +123,13 @@
         lower = start - upper - middle
         square = jnp.concatenate([upper, middle, lower, jnp.zeros_like(start)], 0).T
         blocks = [square[d * 2 * count : (d + 1) * 2 * count] for d in range(SKY_DIRECTIONS)]
-        place = at["start"] + part * LANES
+        place = part * LANES
         for p in range(count):
-            out_ref[p, :, place : place + LANES] = pick_channel_pair(blocks, p).astype(bf16)
-    step = piece // LANES
-    for index, group in enumerate(copies):
-        for copy in group:
-            copy.wait()
-        lax.fori_loop(index * step, (index + 1) * step, columns, 0)
+            block_ref[p, :, place : place + LANES] = pick_channel_pair(blocks, p).astype(bf16)
+    width = out_hbm.shape[2]
+    copy = pltpu.make_async_copy(block_ref, out_hbm.at[:, :, width - 2 * LANES : width], block_sem)
+    copy.start()
+    copy.wait()
 
 
 def stations_in_lanes(pieces):
@@ -138,26 +157,38 @@
     return parts
 
 
-def lookup(parts, low, bits):
-    picked = [jnp.take_along_axis(p, low, axis=1, mode="promise_in_bounds") for p in parts]
-    return jnp.where(
-        bits[1], jnp.where(bits[0], picked[3], picked[2]), jnp.where(bits[0], picked[1], picked[0])
-    )
-
-
-def column_terms(coh_re, coh_im, misc, low, low_row, parts_re, parts_im, sublane):
+def lookup(words, low, high):
+    picked = [jnp.take_along_axis(w, low, axis=1, mode="promise_in_bounds") for w in words]
+    odd, upper = (high & 1) == 1, (high & 2) == 2
+    word = jnp.where(
+        upper, jnp.where(odd, picked[3], picked[2]), jnp.where(odd, picked[1], picked[0])
+    )
+    return (word >> 16).astype(f32), ((word & 65535) - 32768).astype(f32)
+
+
+def words_of(gains_re, gains_im):
+    rounded_re = gains_re.astype(bf16).astype(f32)
+    rounded_im = gains_im.astype(bf16).astype(f32)
+    peak = jnp.max(jnp.maximum(jnp.abs(rounded_re), jnp.abs(rounded_im)), axis=(0, 1), keepdims=True)
+    unit = jnp.full((1, 1), 2.0**-60, f32)
+    for power in range(-60, 60):
+        unit = jnp.where(peak > 32767.0 * 2.0**power, 2.0 ** (power + 1), unit)
+    inverse = 1.0 / unit
+    scaled_re = jnp.round(rounded_re * inverse).astype(i32)
+    scaled_im = jnp.round(rounded_im * inverse).astype(i32)
+    word = (scaled_re << 16) + (scaled_im + 32768)
+    return [word[:, h * LANES : (h + 1) * LANES] for h in range(PARTS)], unit
+
+
+def column_terms(coh_re, coh_im, misc, low, low_row, words, square, sublane):
     def station(row):
         index = jnp.broadcast_to((misc[row : row + 1] + 256.0).astype(i32), (8, LANES))
         return index & (LANES - 1), index >> 7
 
     low_first, high_first = station(4)
     low_second, high_second = station(5)
-    bits_first = ((high_first & 1) == 1, (high_first & 2) == 2)
-    bits_second = ((high_second & 1) == 1, (high_second & 2) == 2)
-    near_re = lookup(parts_re, low_first, bits_first)
-    near_im = lookup(parts_im, low_first, bits_first)
-    far_re = lookup(parts_re, low_second, bits_second)
-    far_im = lookup(parts_im, low_second, bits_second)
+    near_re, near_im = lookup(words, low_first, high_first)
+    far_re, far_im = lookup(words, low_second, high_second)
     z_re = coh_re * far_re + coh_im * far_im
     z_im = coh_im * far_re - coh_re * far_im
     x_re = near_re * coh_re - near_im * coh_im
@@ -168,8 +199,8 @@
     if low_row == 0:
         vis_re = jnp.where(inside(0), misc + low, 0.0)
         vis_im = jnp.where(inside(2), misc + low, 0.0)
-    res_re = vis_re - (near_re * z_re - near_im * z_im)
-    res_im = vis_im - (near_re * z_im + near_im * z_re)
+    res_re = vis_re - square * (near_re * z_re - near_im * z_im)
+    res_im = vis_im - square * (near_re * z_im + near_im * z_re)
     res_re = res_re + pltpu.roll(res_re, 4, 0)
     res_re = res_re + pltpu.roll(res_re, 2, 0)
     res_im = res_im + pltpu.roll(res_im, 4, 0)
@@ -188,9 +219,9 @@
 def operands(term, station_rows, half_rows):
     pair, norm, low, high = term
     zero = jnp.zeros_like(pair)
-    high = jnp.broadcast_to(high[:1].astype(f32), (16, LANES)).astype(bf16)
-    rows = [jnp.where(high == float(h), pair, zero) for h in range(PARTS)]
-    rows += [jnp.where(high == half_rows + float(h), norm, zero) for h in range(0, PARTS, 2)]
+    high = jnp.broadcast_to(high[:1], (16, LANES)).astype(i16)
+    rows = [jnp.where(high == i16(h), pair, zero) for h in range(PARTS)]
+    rows += [jnp.where(high == half_rows + i16(h), norm, zero) for h in range(0, PARTS, 2)]
     low = jnp.broadcast_to(low[:1].astype(f32), (LANES, LANES)).astype(bf16)
     table = jnp.where(station_rows == low, jnp.ones_like(low), jnp.zeros_like(low))
     return jnp.concatenate(rows, 0), table
@@ -200,12 +231,10 @@
     rows = (data_ref.shape[2] - 2 * LANES) * 2 // 7
     at = lanes_of(rows)
     half = rows // 2
-    rounded_re = gains_re.astype(bf16).astype(f32)
-    rounded_im = gains_im.astype(bf16).astype(f32)
-    parts_re = [rounded_re[:, h * LANES : (h + 1) * LANES] for h in range(PARTS)]
-    parts_im = [rounded_im[:, h * LANES : (h + 1) * LANES] for h in range(PARTS)]
+    words, unit = words_of(gains_re, gains_im)
+    square = jnp.broadcast_to(unit * unit, (8, LANES))
     station_rows = lax.broadcasted_iota(i32, (LANES, LANES), 0).astype(f32).astype(bf16)
-    half_rows = (lax.broadcasted_iota(i32, (16, LANES), 0) >> 3).astype(f32).astype(bf16)
+    half_rows = (lax.broadcasted_iota(i32, (16, LANES), 0) >> 3).astype(i16)
     sublane = lax.broadcasted_iota(i32, (8, LANES), 0)
     acc_ref[...] = jnp.zeros_like(acc_ref)
 
@@ -220,8 +249,8 @@
                 load(at["misc"] + offset),
                 low,
                 4 * (offset // half),
-                parts_re,
-                parts_im,
+                words,
+                square,
                 sublane,
             )
             (rows_first, table_first), (rows_second, table_second) = [
@@ -230,8 +259,8 @@
             left.append(jnp.concatenate([rows_first, rows_second], 0))
             right.append(jnp.concatenate([table_first, table_second], 0))
         acc_ref[...] += lax.dot_general(
+            jnp.concatenate(right, 1),
             jnp.concatenate(left, 1),
-            jnp.concatenate(right, 1),
             (((1,), (1,)), ((), ())),
             preferred_element_type=f32,
         )
@@ -239,15 +268,16 @@
 
     lax.fori_loop(first, first + count, step, 0, unroll=UNROLL)
     tall = 24 * PARTS
-    acc = acc_ref[0:tall, 0:LANES] + acc_ref[tall : 2 * tall, LANES : 2 * LANES]
+    acc = (acc_ref[0:LANES, 0:tall] + acc_ref[LANES : 2 * LANES, tall : 2 * tall]).T
     base = 16 * PARTS
     sums = [
         jnp.concatenate([acc[16 * h : 16 * h + 8] for h in range(PARTS)], 1),
         jnp.concatenate([acc[16 * h + 8 : 16 * h + 16] for h in range(PARTS)], 1),
         jnp.concatenate([acc[base + 8 * h : base + 8 * h + 8] for h in range(PARTS)], 1),
     ]
-    for k in range(3):
-        sums_ref[k] = sums[k] if before is None else before[k] + sums[k]
+    for k, factor in enumerate((unit, unit, unit * unit)):
+        part = sums[k] * factor
+        sums_ref[k] = part if before is None else before[k] + part
 
 
 def advance(gains, sums, target, penalty_weight):
@@ -379,18 +409,29 @@
 
 
 def call(
-    name, kernel, out_shape, *inputs, scalars=0, held=0, flops=0, scratch=(), limit=VMEM_LIMIT
+    name,
+    kernel,
+    out_shape,
+    *inputs,
+    scalars=0,
+    in_hbm=(),
+    out_hbm=False,
+    aliases=None,
+    flops=0,
+    scratch=(),
+    limit=VMEM_LIMIT,
 ):
     whole = pl.BlockSpec(memory_space=pltpu.VMEM)
+    outside = pl.BlockSpec(memory_space=pltpu.HBM)
     specs = [pl.BlockSpec(memory_space=pltpu.SMEM)] * scalars
-    specs += [pl.BlockSpec(memory_space=pltpu.HBM)] * held
-    specs += [whole] * (len(inputs) - len(specs))
+    specs += [outside if k in in_hbm else whole for k in range(scalars, len(inputs))]
     return pl.pallas_call(
         kernel,
         out_shape=out_shape,
         in_specs=specs,
-        out_specs=jax.tree.map(lambda _: whole, out_shape),
+        out_specs=jax.tree.map(lambda _: outside if out_hbm else whole, out_shape),
         scratch_shapes=list(scratch),
+        input_output_aliases=aliases or {},
         compiler_params=pltpu.CompilerParams(vmem_limit_bytes=limit),
         cost_estimate=pl.CostEstimate(
             flops=flops, bytes_accessed=sum(x.size * x.dtype.itemsize for x in inputs), transcendentals=0
@@ -426,7 +467,7 @@
     out_shape = shape((2, SKY_DIRECTIONS, owned, channels_dev), f32)
     width = 7 * rows_dev // 2 + 2 * LANES
     flops = 2 * rows_dev * pairs * 192 * 256
-    scratch = [pltpu.VMEM((48 * PARTS, 2 * LANES), f32)]
+    scratch = [pltpu.VMEM((2 * LANES, 48 * PARTS), f32)]
     sweep = functools.partial(call, flops=flops, scratch=scratch)
     half_sweep = functools.partial(call, flops=flops // 2, scratch=scratch)
 
@@ -440,25 +481,42 @@
         return lax.all_to_all(block, "freq", 0, 0, tiled=True)
 
     start = gains_init.transpose(0, 1, 3, 2)
+    packed_shape = shape((pairs, 8, width), bf16)
     packed = call(
         "pack",
         pack_kernel,
-        shape((pairs, 8, width), bf16),
-        core,
+        packed_shape,
         coherency,
         vis,
         station_pairs,
-        start,
-        exchange(start),
-        scalars=1,
-        held=2,
+        in_hbm=(0, 1, 2),
+        out_hbm=True,
         limit=PACK_VMEM_LIMIT,
         scratch=[
             pltpu.VMEM(coherency.shape, bf16),
             pltpu.VMEM(vis.shape, f32),
+            pltpu.VMEM(station_pairs.shape, i32),
+            pltpu.VMEM(packed_shape.shape, bf16),
             pltpu.SemaphoreType.DMA((2 * COPIES,)),
             pltpu.SemaphoreType.DMA((2 * COPIES,)),
+            pltpu.SemaphoreType.DMA,
+            pltpu.SemaphoreType.DMA((7 * COPIES,)),
         ],
+    )
+    packed = call(
+        "seed",
+        seed_kernel,
+        packed_shape,
+        core,
+        start,
+        exchange(start),
+        packed,
+        scalars=1,
+        in_hbm=(3,),
+        out_hbm=True,
+        aliases={3: 0},
+        limit=PACK_VMEM_LIMIT,
+        scratch=[pltpu.VMEM((pairs, 8, 2 * LANES), bf16), pltpu.SemaphoreType.DMA],
     )
     data = to_pairs(packed)
 

time: 136 us -> 129 us (0.949)
  Pallas kernels: 43.8 us -> 36.8 us
    pallas_call x13 -> x14, Pallas kernels: 43.8 us -> 36.8 us  [call(): pl.pallas_call(kernel, out_shape=out_shape, in_specs=specs, out_specs=jax...]
    ppermute x5, waiting for transfers between devices: 5.27 us -> 3.82 us  [exchange(): return lax.ppermute(partial, 'core', swap)]
  transfers between devices with their start and end apart: 9 -> 9, of which waited for: 9 -> 8; matrix products, arithmetic and copies ran while one was open for 1% -> 1% of each run, Pallas kernels for 7% -> 9%
where the time goes in v4:
time: 129 us
  blocking collectives  44 us (34%)
  Pallas kernels  36.8 us (29%)
  waiting for transfers between devices  23.6 us (18%)
  starting transfers between devices  21.8 us (17%)
  local copies, waits for them, and re-layouts  1.65 us (1%)
    all_to_all x2, blocking collectives, to_pairs(): return lax.all_to_all(block, 'pair', 0, 0, tiled=True)  44 us
    pallas_call x14, Pallas kernels, call(): pl.pallas_call(kernel, out_shape=out_shape, in_specs=specs, out_specs=jax...  36.8 us
    all_to_all x2, starting transfers between devices, over_bands(): return lax.all_to_all(block, 'freq', 0, 0, tiled=True)  11.8 us
    all_to_all x2, waiting for transfers between devices, over_bands(): return lax.all_to_all(block, 'freq', 0, 0, tiled=True)  11.7 us
    all_to_all x2, starting transfers between devices, to_pairs(): return lax.all_to_all(block, 'pair', 0, 0, tiled=True)  9.49 us
    all_to_all x2, waiting for transfers between devices, to_pairs(): return lax.all_to_all(block, 'pair', 0, 0, tiled=True)  8.06 us
    ppermute x5, waiting for transfers between devices, exchange(): return lax.ppermute(partial, 'core', swap)  3.82 us
  transfers between devices with their start and end apart: 9, of which 8 were waited for; matrix products, arithmetic and copies ran while one was open for 1% of the time, Pallas kernels for 9%

profile of v4, /device:TPU:2, one launch (start us, length us, event | category | flops | bytes accessed | tf_op | source)
XLA Modules:
  0.0 128.6 jit_solution(18316350703477118914)
XLA Ops:
  0.6 0.1 collective-permute-start
  0.7 3.4 %pack.1.packed_hbm = bf16[16,8,7424]{2,1,0:T(8,128)(2,1)} custom-call(bf16[2,4,32,2048]{3,2,1,0:T(8,128)(2,1)} %coh_hbm.1, f32[2,32,2048]{2,1,0:T(8,128)} %vis_hbm.1, s32[2,2048]{1,0:T(2,128)} %pairs_hbm.1), custom_call_target="tpu_custom_call" | custom-call | bytes 1589248 | tf_op jit(solution)/shard_map/pack/pallas_call | solution.py:428
  4.2 0.0 collective-permute-done.other_ref
  4.2 0.0 copy-start
  4.2 0.6 copy-done
  4.8 1.7 %seed.1 = bf16[16,8,7424]{2,1,0:T(8,128)(2,1)} custom-call(s32[1]{0:T(128)} %bitcast.core_ref, f32[2,4,16,32]{3,2,1,0:T(8,128)} %bitcast.7, f32[2,4,16,32]{3,2,1,0:T(8,128)} %copy-done, bf16[16,8,7424]{2,1,0:T(8,128)(2,1)} %pack.1.packed_hbm), custom_call_target="tpu_custom_call", output_to_operand_aliasing={{}: (3, {})} | custom-call | bytes 1933316 | tf_op jit(solution)/shard_map/seed/pallas_call | solution.py:428
  6.6 33.1 %all_to_all.30.data_ref = bf16[16,8,7424]{2,1,0:T(8,128)(2,1)S(1)} all-to-all(bf16[16,8,7424]{2,1,0:T(8,128)(2,1)} %seed.1), channel_id=1, replica_groups=mesh['freq'=8,'pair'=16,'core'=2] {'pair'}, dimensions={0} | all-to-all | bytes 3801088 | tf_op jit(solution)/shard_map/all_to_all | solution.py:478
  39.7 6.6 %first.1 = (f32[3,8,512]{2,1,0:T(8,128)S(1)}, f32[2,8,512]{2,1,0:T(8,128)S(1)}) custom-call(bf16[16,8,7424]{2,1,0:T(8,128)(2,1)S(1)} %all_to_all.30.data_ref), custom_call_target="tpu_custom_call" | custom-call | flops 3221225472 | bytes 1900544 | tf_op jit(solution)/shard_map/first/pallas_call | solution.py:428
  46.3 0.1 collective-permute-start.1
  46.4 1.2 collective-permute-done.1.other_ref
  47.6 6.4 %step.1 = (f32[3,8,512]{2,1,0:T(8,128)S(1)}, f32[2,8,512]{2,1,0:T(8,128)S(1)}) custom-call(bf16[16,8,7424]{2,1,0:T(8,128)(2,1)S(1)} %all_to_all.30.data_ref, f32[3,8,512]{2,1,0:T(8,128)S(1)} %get-tuple-element.18.mine_ref, f32[3,8,512]{2,1,0:T(8,128)S(1)} %collective-permute-done.1.other_ref, f32[2,8,512]{2,1,0:T(8,128)S(1)} %get-tuple-element.19.gains_ref.target_ref), custom_call_target="tpu_custom_call" | custom-call | flops 3221225472 | bytes 2031616 | tf_op jit(solution)/shard_map/step/pallas_call | solution.py:428
  54.0 0.3 collective-permute-start.2
  54.3 0.7 constant_dynamic-slice_fusion
  55.0 0.1 copy.9
  55.1 0.1 copy.10
  55.2 0.2 collective-permute-done.2.other_ref
  55.3 0.7 finish.2
  56.1 4.7 %all-to-all-start.1 = ((f32[16,8,128]{2,1,0:T(8,128)}), f32[16,8,128]{2,1,0:T(8,128)S(1)}, u32[]{:S(2)}, u32[]{:S(2)}) async-start(f32[16,8,128]{2,1,0:T(8,128)} %get-tuple-element.22), calls=%async_computation.1 | async-start | bytes 131072 | tf_op jit(solution)/shard_map/all_to_all | solution.py:478
  60.8 3.4 %early.1.before_ref = f32[3,8,512]{2,1,0:T(8,128)S(1)} custom-call(bf16[16,8,7424]{2,1,0:T(8,128)(2,1)S(1)} %all_to_all.30.data_ref, f32[2,8,512]{2,1,0:T(8,128)S(1)} %get-tuple-element.23.gains_ref), custom_call_target="tpu_custom_call" | custom-call | flops 1610612736 | bytes 1933312 | tf_op jit(solution)/shard_map/early/pallas_call | solution.py:428
  64.3 2.9 %all-to-all-done.1.refs_0_.gains_ref = f32[16,8,128]{2,1,0:T(8,128)S(1)} async-done(((f32[16,8,128]{2,1,0:T(8,128)}), f32[16,8,128]{2,1,0:T(8,128)S(1)}, u32[]{:S(2)}, u32[]{:S(2)}) %all-to-all-start.1) | async-done | bytes 65568 | tf_op jit(solution)/shard_map/all_to_all | solution.py:478
  67.2 0.1 broadcast_in_dim.14.basis_ref
  67.3 0.7 fit.2
  68.0 8.5 %all-to-all-start.2 = ((f32[8,8,128]{2,1,0:T(8,128)}), f32[8,8,128]{2,1,0:T(8,128)S(1)}, u32[]{:S(2)}, u32[]{:S(2)}) async-start(f32[8,8,128]{2,1,0:T(8,128)} %fit.2), calls=%async_computation.2 | async-start | bytes 65536 | tf_op jit(solution)/shard_map/all_to_all | solution.py:481
  76.5 3.4 %late.1.mine_ref = f32[3,8,512]{2,1,0:T(8,128)S(1)} custom-call(bf16[16,8,7424]{2,1,0:T(8,128)(2,1)S(1)} %all_to_all.30.data_ref, f32[2,8,512]{2,1,0:T(8,128)S(1)} %get-tuple-element.23.gains_ref, f32[3,8,512]{2,1,0:T(8,128)S(1)} %early.1.before_ref), custom_call_target="tpu_custom_call" | custom-call | flops 1610612736 | bytes 1982464 | tf_op jit(solution)/shard_map/late/pallas_call | solution.py:428
  80.0 4.6 %all-to-all-done.2.parts_ref = f32[8,8,128]{2,1,0:T(8,128)S(1)} async-done(((f32[8,8,128]{2,1,0:T(8,128)}), f32[8,8,128]{2,1,0:T(8,128)S(1)}, u32[]{:S(2)}, u32[]{:S(2)}) %all-to-all-start.2) | async-done | bytes 32800 | tf_op jit(solution)/shard_map/all_to_all | solution.py:481
  84.5 0.7 spread.1
  85.3 4.7 %all-to-all-start.3 = ((f32[16,8,128]{2,1,0:T(8,128)}), f32[16,8,128]{2,1,0:T(8,128)S(1)}, u32[]{:S(2)}, u32[]{:S(2)}) async-start(f32[16,8,128]{2,1,0:T(8,128)} %get-tuple-element.28), calls=%async_computation.3 | async-start | bytes 131072 | tf_op jit(solution)/shard_map/all_to_all | solution.py:478
  90.0 0.0 collective-permute-start.3
  90.0 1.2 collective-permute-done.3.other_ref
  91.2 5.1 %all-to-all-done.3.fit_ref = f32[16,8,128]{2,1,0:T(8,128)S(1)} async-done(((f32[16,8,128]{2,1,0:T(8,128)}), f32[16,8,128]{2,1,0:T(8,128)S(1)}, u32[]{:S(2)}, u32[]{:S(2)}) %all-to-all-start.3) | async-done | bytes 65568 | tf_op jit(solution)/shard_map/all_to_all | solution.py:478
  96.4 6.6 %retarget.1 = (f32[3,8,512]{2,1,0:T(8,128)S(1)}, f32[2,8,512]{2,1,0:T(8,128)S(1)}, f32[2,8,512]{2,1,0:T(8,128)S(1)}) custom-call(bf16[16,8,7424]{2,1,0:T(8,128)(2,1)S(1)} %all_to_all.30.data_ref, f32[3,8,512]{2,1,0:T(8,128)S(1)} %late.1.mine_ref, f32[3,8,512]{2,1,0:T(8,128)S(1)} %collective-permute-done.3.other_ref, ...), custom_call_target="tpu_custom_call" | custom-call | flops 3221225472 | bytes 2097152 | tf_op jit(solution)/shard_map/retarget/pallas_call | solution.py:428
  103.0 0.1 collective-permute-start.4
  103.1 1.2 collective-permute-done.4.other_ref
  104.3 0.6 finish.3
  104.9 10.8 %all_to_all.31.blocks_ref.refs_0_ = f32[16,8,128]{2,1,0:T(8,128)S(1)} all-to-all(f32[16,8,128]{2,1,0:T(8,128)S(1)} %get-tuple-element.32), channel_id=1, replica_groups=mesh['freq'=8,'pair'=16,'core'=2] {'pair'}, dimensions={0} | all-to-all | bytes 131072 | tf_op jit(solution)/shard_map/all_to_all | solution.py:478
  115.7 0.7 fit.3
  116.4 3.3 %all-to-all-start.5 = ((f32[8,8,128]{2,1,0:T(8,128)}), f32[8,8,128]{2,1,0:T(8,128)S(1)}, u32[]{:S(2)}, u32[]{:S(2)}) async-start(f32[8,8,128]{2,1,0:T(8,128)} %fit.3), calls=%async_computation.5 | async-start | bytes 65536 | tf_op jit(solution)/shard_map/all_to_all | solution.py:481
  119.8 0.8 place.1
  120.6 7.1 %all-to-all-done.5.parts_ref = f32[8,8,128]{2,1,0:T(8,128)S(1)} async-done(((f32[8,8,128]{2,1,0:T(8,128)}), f32[8,8,128]{2,1,0:T(8,128)S(1)}, u32[]{:S(2)}, u32[]{:S(2)}) %all-to-all-start.5) | async-done | bytes 32800 | tf_op jit(solution)/shard_map/all_to_all | solution.py:481
  127.7 0.9 final.1
  (1 shorter events, 0.0 us)
Async XLA Ops:
  0.6 3.5 %collective-permute-start = (f32[2,4,16,32]{3,2,1,0:T(8,128)}, f32[2,4,16,32]{3,2,1,0:T(8,128)S(1)}, u32[]{:S(2)}, u32[]{:S(2)}) collective-permute-start(f32[2,4,16,32]{3,2,1,0:T(8,128)} %bitcast.6), channel_id=1, source_target_pairs={{0,1},{1,0},{2,3},{3,2},{4,5},{5,4},{6,7},{7,6},{8,9},{9,8},{10,11... | collective-permute-start | bytes 49160 | tf_op jit(solution)/shard_map/ppermute | solution.py:475
  4.2 0.6 copy-start
  46.3 1.3 %collective-permute-start.1 = (f32[3,8,512]{2,1,0:T(8,128)S(1)}, f32[3,8,512]{2,1,0:T(8,128)S(1)}, u32[]{:S(2)}, u32[]{:S(2)}) collective-permute-start(f32[3,8,512]{2,1,0:T(8,128)S(1)} %get-tuple-element.18.mine_ref), channel_id=1, source_target_pairs={{0,1},{1,0},{2,3},{3,2},{4,5},{5,4},{6,7},{7,6},{8,9},{9,8},{10,11... | collective-permute-start | bytes 147464 | tf_op jit(solution)/shard_map/ppermute | solution.py:475
  54.0 1.3 %collective-permute-start.2 = (f32[3,8,512]{2,1,0:T(8,128)S(1)}, f32[3,8,512]{2,1,0:T(8,128)S(1)}, u32[]{:S(2)}, u32[]{:S(2)}) collective-permute-start(f32[3,8,512]{2,1,0:T(8,128)S(1)} %get-tuple-element.20.mine_ref), channel_id=1, source_target_pairs={{0,1},{1,0},{2,3},{3,2},{4,5},{5,4},{6,7},{7,6},{8,9},{9,8},{10,11... | collective-permute-start | bytes 147464 | tf_op jit(solution)/shard_map/ppermute | solution.py:475
  56.1 11.1 %all-to-all-start.1 = ((f32[16,8,128]{2,1,0:T(8,128)}), f32[16,8,128]{2,1,0:T(8,128)S(1)}, u32[]{:S(2)}, u32[]{:S(2)}) async-start(f32[16,8,128]{2,1,0:T(8,128)} %get-tuple-element.22), calls=%async_computation.1 | async-start | bytes 131072 | tf_op jit(solution)/shard_map/all_to_all | solution.py:478
  68.0 16.5 %all-to-all-start.2 = ((f32[8,8,128]{2,1,0:T(8,128)}), f32[8,8,128]{2,1,0:T(8,128)S(1)}, u32[]{:S(2)}, u32[]{:S(2)}) async-start(f32[8,8,128]{2,1,0:T(8,128)} %fit.2), calls=%async_computation.2 | async-start | bytes 65536 | tf_op jit(solution)/shard_map/all_to_all | solution.py:481
  85.3 11.1 %all-to-all-start.3 = ((f32[16,8,128]{2,1,0:T(8,128)}), f32[16,8,128]{2,1,0:T(8,128)S(1)}, u32[]{:S(2)}, u32[]{:S(2)}) async-start(f32[16,8,128]{2,1,0:T(8,128)} %get-tuple-element.28), calls=%async_computation.3 | async-start | bytes 131072 | tf_op jit(solution)/shard_map/all_to_all | solution.py:478
  90.0 1.2 collective-permute-start.3
  103.0 1.3 %collective-permute-start.4 = (f32[3,8,512]{2,1,0:T(8,128)S(1)}, f32[3,8,512]{2,1,0:T(8,128)S(1)}, u32[]{:S(2)}, u32[]{:S(2)}) collective-permute-start(f32[3,8,512]{2,1,0:T(8,128)S(1)} %get-tuple-element.29.mine_ref), channel_id=1, source_target_pairs={{0,1},{1,0},{2,3},{3,2},{4,5},{5,4},{6,7},{7,6},{8,9},{9,8},{10,11... | collective-permute-start | bytes 147464 | tf_op jit(solution)/shard_map/ppermute | solution.py:475
  116.4 11.3 %all-to-all-start.5 = ((f32[8,8,128]{2,1,0:T(8,128)}), f32[8,8,128]{2,1,0:T(8,128)S(1)}, u32[]{:S(2)}, u32[]{:S(2)}) async-start(f32[8,8,128]{2,1,0:T(8,128)} %fit.3), calls=%async_computation.5 | async-start | bytes 65536 | tf_op jit(solution)/shard_map/all_to_all | solution.py:481

commit v5 on v4

--- a/solution.py
+++ b/solution.py
@@ -15,8 +15,12 @@
 LANES = 128
 PARTS = STATION_TOTAL // LANES
 UNROLL = 8
+COH_STEPS = 4096.0
+GAIN_STEPS = 4096.0
+REST_STEPS = 2.0**27
 COPIES = 4
 PACK_VMEM_LIMIT = 58 * 1024 * 1024
+SEED_VMEM_LIMIT = 53 * 1024 * 1024
 VMEM_LIMIT = 24 * 1024 * 1024
 f32, bf16, i32, i16 = jnp.float32, jnp.bfloat16, jnp.int32, jnp.int16
 
@@ -32,7 +36,15 @@
 
 
 def lanes_of(rows):
-    return {"re": 0, "im": rows, "misc": 2 * rows, "low": 3 * rows, "start": 3 * rows + rows // 2}
+    return {"re": 0, "im": rows, "misc": 2 * rows, "start": 3 * rows}
+
+
+def rows_of(data_ref):
+    return (data_ref.shape[2] - LANES) // 3
+
+
+def coded(values):
+    return jnp.round(values).astype(i32).astype(i16)
 
 
 def pick_channel_pair(by_direction, pair):
@@ -44,6 +56,7 @@
 ):
     rows = vis_ref.shape[2]
     count = out_ref.shape[0]
+    channels = vis_ref.shape[1]
     at = lanes_of(rows)
     half = rows // 2
     piece = half // COPIES
@@ -63,46 +76,53 @@
             group.append(
                 pltpu.make_async_copy(vis_hbm.at[:, :, lanes], vis_ref.at[:, :, lanes], vis_sem.at[slot])
             )
-        for copy in group:
-            copy.start()
         copies.append(group)
+    for kind in (1, 0):
+        for group in copies:
+            for copy in group[kind::2]:
+                copy.start()
+    for group in copies:
+        for copy in group[1::2]:
+            copy.wait()
+    peak = jnp.zeros((channels, LANES), f32)
+    for start in range(0, rows, LANES):
+        for part in range(2):
+            peak = jnp.maximum(peak, jnp.abs(vis_ref[part, :, start : start + LANES]))
+    peak = jnp.max(peak, axis=(0, 1), keepdims=True)
+    exponent = jnp.full((1, 1), -60.0, f32)
+    inverse = jnp.full((1, 1), 2.0**60, f32)
+    for power in range(-60, -8):
+        over = peak > 32767.0 * 2.0**power
+        exponent = jnp.where(over, power + 1.0, exponent)
+        inverse = jnp.where(over, 2.0 ** (-power - 1), inverse)
+    exponent = jnp.broadcast_to(exponent, (2, LANES))
 
     def columns(index, carry):
         early = pl.multiple_of(index * LANES, LANES)
         late = pl.multiple_of(half + index * LANES, LANES)
-        lower = []
         for offset in (early, late):
             lanes = pl.ds(offset, LANES)
             for part in range(2):
-                blocks = [coh_ref[part, d, :, lanes].astype(f32) for d in range(SKY_DIRECTIONS)]
+                blocks = [coh_ref[part, d, :, lanes].astype(f32) * COH_STEPS for d in range(SKY_DIRECTIONS)]
                 place = pl.multiple_of(offset + part * rows, LANES)
                 for p in range(count):
-                    out_ref[p, :, pl.ds(place, LANES)] = pick_channel_pair(blocks, p).astype(bf16)
-            upper = []
-            for part in range(2):
-                seen = vis_ref[part, :, lanes]
-                rounded = seen.astype(bf16).astype(f32)
-                upper.append(rounded)
-                lower.append(seen - rounded)
-            codes = (pairs_ref[:, lanes] - STATION_TOTAL // 2).astype(f32)
-            tail = jnp.concatenate([codes, jnp.zeros((2, LANES), f32)], 0)
+                    out_ref[p, :, pl.ds(place, LANES)] = coded(pick_channel_pair(blocks, p))
+            seen = [vis_ref[part, :, lanes] * inverse for part in range(2)]
+            tail = jnp.concatenate([pairs_ref[:, lanes].astype(f32), exponent], 0)
             place = pl.multiple_of(offset + at["misc"], LANES)
             for p in range(count):
-                block = jnp.concatenate([upper[0][2 * p : 2 * p + 2], upper[1][2 * p : 2 * p + 2], tail], 0)
-                out_ref[p, :, pl.ds(place, LANES)] = block.astype(bf16)
-        place = pl.multiple_of(early + at["low"], LANES)
-        for p in range(count):
-            out_ref[p, :, pl.ds(place, LANES)] = pick_channel_pair(lower, p).astype(bf16)
+                block = jnp.concatenate([seen[0][2 * p : 2 * p + 2], seen[1][2 * p : 2 * p + 2], tail], 0)
+                out_ref[p, :, pl.ds(place, LANES)] = coded(block)
         return carry
 
     pairs_copy.wait()
     step = piece // LANES
     sent = []
     for index, group in enumerate(copies):
-        for copy in group:
+        for copy in group[0::2]:
             copy.wait()
         lax.fori_loop(index * step, (index + 1) * step, columns, 0)
-        for start in (at["re"], at["re"] + half, at["im"], at["im"] + half, at["misc"], at["misc"] + half, at["low"]):
+        for start in (at["re"], at["re"] + half, at["im"], at["im"] + half, at["misc"], at["misc"] + half):
             lanes = pl.ds(start + index * piece, piece)
             copy = pltpu.make_async_copy(out_ref.at[:, :, lanes], out_hbm.at[:, :, lanes], out_sem.at[len(sent)])
             copy.start()
@@ -114,20 +134,19 @@
 def seed_kernel(core_ref, mine_ref, other_ref, packed_hbm, out_hbm, block_ref, block_sem):
     count = block_ref.shape[0]
     is_first = core_ref[0] == 0
+    parts = []
     for part in range(2):
         mine = jnp.concatenate([mine_ref[part, d] for d in range(SKY_DIRECTIONS)], 1)
         other = jnp.concatenate([other_ref[part, d] for d in range(SKY_DIRECTIONS)], 1)
         start = jnp.concatenate([jnp.where(is_first, mine, other), jnp.where(is_first, other, mine)], 0)
-        upper = start.astype(bf16).astype(f32)
-        middle = (start - upper).astype(bf16).astype(f32)
-        lower = start - upper - middle
-        square = jnp.concatenate([upper, middle, lower, jnp.zeros_like(start)], 0).T
-        blocks = [square[d * 2 * count : (d + 1) * 2 * count] for d in range(SKY_DIRECTIONS)]
-        place = part * LANES
-        for p in range(count):
-            block_ref[p, :, place : place + LANES] = pick_channel_pair(blocks, p).astype(bf16)
+        coarse = jnp.round(start * GAIN_STEPS)
+        parts += [coarse, jnp.round((start - coarse * (1.0 / GAIN_STEPS)) * REST_STEPS)]
+    square = jnp.concatenate(parts, 0).T
+    blocks = [square[d * 2 * count : (d + 1) * 2 * count] for d in range(SKY_DIRECTIONS)]
+    for p in range(count):
+        block_ref[p] = coded(pick_channel_pair(blocks, p))
     width = out_hbm.shape[2]
-    copy = pltpu.make_async_copy(block_ref, out_hbm.at[:, :, width - 2 * LANES : width], block_sem)
+    copy = pltpu.make_async_copy(block_ref, out_hbm.at[:, :, width - LANES : width], block_sem)
     copy.start()
     copy.wait()
 
@@ -145,13 +164,15 @@
 
 
 def starting_gains(data_ref):
-    at = lanes_of((data_ref.shape[2] - 2 * LANES) * 2 // 7)["start"]
+    at = lanes_of(rows_of(data_ref))["start"]
     parts = []
     for part in range(2):
         pieces = []
         for p in range(data_ref.shape[0]):
-            piece = data_ref[p, :, at + part * LANES : at + (part + 1) * LANES].astype(f32)
-            piece = piece + pltpu.roll(piece, LANES - 32, 1) + pltpu.roll(piece, LANES - 64, 1)
+            piece = data_ref[p, :, at : at + LANES].astype(i32).astype(f32)
+            if part:
+                piece = pltpu.roll(piece, LANES - 64, 1)
+            piece = piece * (1.0 / GAIN_STEPS) + pltpu.roll(piece, LANES - 32, 1) * (1.0 / REST_STEPS)
             pieces.append(piece)
         parts.append(stations_in_lanes(pieces))
     return parts
@@ -180,9 +201,9 @@
     return [word[:, h * LANES : (h + 1) * LANES] for h in range(PARTS)], unit
 
 
-def column_terms(coh_re, coh_im, misc, low, low_row, words, square, sublane):
+def column_terms(coh_re, coh_im, misc, vis_unit, words, square, sublane):
     def station(row):
-        index = jnp.broadcast_to((misc[row : row + 1] + 256.0).astype(i32), (8, LANES))
+        index = jnp.broadcast_to(misc[row : row + 1], (8, LANES))
         return index & (LANES - 1), index >> 7
 
     low_first, high_first = station(4)
@@ -193,12 +214,9 @@
     z_im = coh_im * far_re - coh_re * far_im
     x_re = near_re * coh_re - near_im * coh_im
     x_im = near_re * coh_im + near_im * coh_re
-    inside = lambda row: (sublane >= row) & (sublane < row + 2)
-    vis_re = jnp.where(inside(0), misc, jnp.where(inside(low_row), low, 0.0))
-    vis_im = jnp.where(inside(2), misc, jnp.where(inside(low_row + 2), low, 0.0))
-    if low_row == 0:
-        vis_re = jnp.where(inside(0), misc + low, 0.0)
-        vis_im = jnp.where(inside(2), misc + low, 0.0)
+    seen = misc.astype(f32) * vis_unit
+    vis_re = jnp.where(sublane < 2, seen, 0.0)
+    vis_im = jnp.where((sublane >= 2) & (sublane < 4), seen, 0.0)
     res_re = vis_re - square * (near_re * z_re - near_im * z_im)
     res_im = vis_im - square * (near_re * z_im + near_im * z_re)
     res_re = res_re + pltpu.roll(res_re, 4, 0)
@@ -228,11 +246,11 @@
 
 
 def accumulate(data_ref, first, count, gains_re, gains_im, sums_ref, acc_ref, before=None):
-    rows = (data_ref.shape[2] - 2 * LANES) * 2 // 7
+    rows = rows_of(data_ref)
     at = lanes_of(rows)
-    half = rows // 2
     words, unit = words_of(gains_re, gains_im)
-    square = jnp.broadcast_to(unit * unit, (8, LANES))
+    square = jnp.broadcast_to(unit * unit * (1.0 / COH_STEPS), (8, LANES))
+    unit = unit * (1.0 / COH_STEPS)
     station_rows = lax.broadcasted_iota(i32, (LANES, LANES), 0).astype(f32).astype(bf16)
     half_rows = (lax.broadcasted_iota(i32, (16, LANES), 0) >> 3).astype(i16)
     sublane = lax.broadcasted_iota(i32, (8, LANES), 0)
@@ -240,15 +258,15 @@
 
     def step(source, carry):
         left, right = [], []
+        exponent = data_ref[source, :, at["misc"] : at["misc"] + LANES].astype(i32).astype(f32)
+        vis_unit = jnp.exp2(jnp.broadcast_to(exponent[6:7], (8, LANES)))
         for offset in range(0, rows, LANES):
-            load = lambda start: data_ref[source, :, start : start + LANES].astype(f32)
-            low = load(at["low"] + offset % half)
+            load = lambda start: data_ref[source, :, start : start + LANES].astype(i32)
             terms = column_terms(
-                load(at["re"] + offset),
-                load(at["im"] + offset),
+                load(at["re"] + offset).astype(f32),
+                load(at["im"] + offset).astype(f32),
                 load(at["misc"] + offset),
-                low,
-                4 * (offset // half),
+                vis_unit,
                 words,
                 square,
                 sublane,
@@ -465,7 +483,7 @@
     block_shape = shape((pairs, 8, LANES), f32)
     parts_shape = shape((bands, 8, LANES), f32)
     out_shape = shape((2, SKY_DIRECTIONS, owned, channels_dev), f32)
-    width = 7 * rows_dev // 2 + 2 * LANES
+    width = 3 * rows_dev + LANES
     flops = 2 * rows_dev * pairs * 192 * 256
     scratch = [pltpu.VMEM((2 * LANES, 48 * PARTS), f32)]
     sweep = functools.partial(call, flops=flops, scratch=scratch)
@@ -481,7 +499,7 @@
         return lax.all_to_all(block, "freq", 0, 0, tiled=True)
 
     start = gains_init.transpose(0, 1, 3, 2)
-    packed_shape = shape((pairs, 8, width), bf16)
+    packed_shape = shape((pairs, 8, width), i16)
     packed = call(
         "pack",
         pack_kernel,
@@ -496,11 +514,11 @@
             pltpu.VMEM(coherency.shape, bf16),
             pltpu.VMEM(vis.shape, f32),
             pltpu.VMEM(station_pairs.shape, i32),
-            pltpu.VMEM(packed_shape.shape, bf16),
+            pltpu.VMEM(packed_shape.shape, i16),
             pltpu.SemaphoreType.DMA((2 * COPIES,)),
             pltpu.SemaphoreType.DMA((2 * COPIES,)),
             pltpu.SemaphoreType.DMA,
-            pltpu.SemaphoreType.DMA((7 * COPIES,)),
+            pltpu.SemaphoreType.DMA((6 * COPIES,)),
         ],
     )
     packed = call(
@@ -515,8 +533,8 @@
         in_hbm=(3,),
         out_hbm=True,
         aliases={3: 0},
-        limit=PACK_VMEM_LIMIT,
-        scratch=[pltpu.VMEM((pairs, 8, 2 * LANES), bf16), pltpu.SemaphoreType.DMA],
+        limit=SEED_VMEM_LIMIT,
+        scratch=[pltpu.VMEM((pairs, 8, LANES), i16), pltpu.SemaphoreType.DMA],
     )
     data = to_pairs(packed)
 

time: 129 us -> 125 us (0.969)
  blocking collectives: 44 us -> 40.9 us
    all_to_all x2, blocking collectives: 44 us -> 40.9 us  [to_pairs(): return lax.all_to_all(block, 'pair', 0, 0, tiled=True)]
where the time goes in v5:
time: 125 us; the launch traced here: 124 us
  blocking collectives  40.9 us (33%)
  Pallas kernels  36.4 us (29%)
  waiting for transfers between devices  23.5 us (19%)
  starting transfers between devices  21.8 us (17%)
    all_to_all x2, blocking collectives, to_pairs(): return lax.all_to_all(block, 'pair', 0, 0, tiled=True)  40.9 us
    pallas_call x14, Pallas kernels, call(): pl.pallas_call(kernel, out_shape=out_shape, in_specs=specs, out_specs=jax...  36.4 us
    all_to_all x2, starting transfers between devices, over_bands(): return lax.all_to_all(block, 'freq', 0, 0, tiled=True)  11.8 us
    all_to_all x2, waiting for transfers between devices, over_bands(): return lax.all_to_all(block, 'freq', 0, 0, tiled=True)  11.7 us
    all_to_all x2, starting transfers between devices, to_pairs(): return lax.all_to_all(block, 'pair', 0, 0, tiled=True)  9.5 us
    all_to_all x2, waiting for transfers between devices, to_pairs(): return lax.all_to_all(block, 'pair', 0, 0, tiled=True)  8.02 us
    ppermute x5, waiting for transfers between devices, exchange(): return lax.ppermute(partial, 'core', swap)  3.83 us
  transfers between devices with their start and end apart: 9, of which 8 were waited for; matrix products, arithmetic and copies ran while one was open for 1% of the time, Pallas kernels for 9%

profile of v5, /device:TPU:2, one launch (start us, length us, event | category | flops | bytes accessed | tf_op | source)
XLA Modules:
  0.0 124.5 jit_solution(4051309631463050335)
XLA Ops:
  0.6 0.0 copy-start
  0.6 0.1 collective-permute-start
  0.7 3.7 %pack.1.packed_hbm = s16[16,8,6272]{2,1,0:T(8,128)(2,1)} custom-call(bf16[2,4,32,2048]{3,2,1,0:T(8,128)(2,1)} %coh_hbm.1, f32[2,32,2048]{2,1,0:T(8,128)} %vis_hbm.1, s32[2,2048]{1,0:T(2,128)} %pairs_hbm.1), custom_call_target="tpu_custom_call" | custom-call | bytes 1589248 | tf_op jit(solution)/shard_map/pack/pallas_call | solution.py:446
  4.5 0.0 collective-permute-done.other_ref
  4.5 0.0 copy-done
  4.5 0.8 seed.1
  5.3 30.1 %all_to_all.30.data_ref = s16[16,8,6272]{2,1,0:T(8,128)(2,1)S(1)} all-to-all(s16[16,8,6272]{2,1,0:T(8,128)(2,1)} %seed.1), channel_id=1, replica_groups=mesh['freq'=8,'pair'=16,'core'=2] {'pair'}, dimensions={0} | all-to-all | bytes 3211264 | tf_op jit(solution)/shard_map/all_to_all | solution.py:496
  35.4 6.7 %first.1 = (f32[3,8,512]{2,1,0:T(8,128)S(1)}, f32[2,8,512]{2,1,0:T(8,128)S(1)}) custom-call(s16[16,8,6272]{2,1,0:T(8,128)(2,1)S(1)} %all_to_all.30.data_ref), custom_call_target="tpu_custom_call" | custom-call | flops 3221225472 | bytes 1605632 | tf_op jit(solution)/shard_map/first/pallas_call | solution.py:446
  42.1 0.1 collective-permute-start.1
  42.2 1.2 collective-permute-done.1.other_ref
  43.4 6.5 %step.1 = (f32[3,8,512]{2,1,0:T(8,128)S(1)}, f32[2,8,512]{2,1,0:T(8,128)S(1)}) custom-call(s16[16,8,6272]{2,1,0:T(8,128)(2,1)S(1)} %all_to_all.30.data_ref, f32[3,8,512]{2,1,0:T(8,128)S(1)} %get-tuple-element.18.mine_ref, f32[3,8,512]{2,1,0:T(8,128)S(1)} %collective-permute-done.1.other_ref, f32[2,8,512]{2,1,0:T(8,128)S(1)} %get-tuple-element.19.gains_ref.target_ref), custom_call_target="tpu_custom_call" | custom-call | flops 3221225472 | bytes 1736704 | tf_op jit(solution)/shard_map/step/pallas_call | solution.py:446
  49.9 0.2 collective-permute-start.2
  50.1 0.7 constant_dynamic-slice_fusion
  50.9 0.1 copy.9
  51.0 0.1 copy.10
  51.0 0.2 collective-permute-done.2.other_ref
  51.2 0.7 finish.2
  51.9 4.8 %all-to-all-start.1 = ((f32[16,8,128]{2,1,0:T(8,128)}), f32[16,8,128]{2,1,0:T(8,128)S(1)}, u32[]{:S(2)}, u32[]{:S(2)}) async-start(f32[16,8,128]{2,1,0:T(8,128)} %get-tuple-element.22), calls=%async_computation.1 | async-start | bytes 131072 | tf_op jit(solution)/shard_map/all_to_all | solution.py:496
  56.7 3.5 %early.1.before_ref = f32[3,8,512]{2,1,0:T(8,128)S(1)} custom-call(s16[16,8,6272]{2,1,0:T(8,128)(2,1)S(1)} %all_to_all.30.data_ref, f32[2,8,512]{2,1,0:T(8,128)S(1)} %get-tuple-element.23.gains_ref), custom_call_target="tpu_custom_call" | custom-call | flops 1610612736 | bytes 1638400 | tf_op jit(solution)/shard_map/early/pallas_call | solution.py:446
  60.2 2.9 %all-to-all-done.1.refs_0_.gains_ref = f32[16,8,128]{2,1,0:T(8,128)S(1)} async-done(((f32[16,8,128]{2,1,0:T(8,128)}), f32[16,8,128]{2,1,0:T(8,128)S(1)}, u32[]{:S(2)}, u32[]{:S(2)}) %all-to-all-start.1) | async-done | bytes 65568 | tf_op jit(solution)/shard_map/all_to_all | solution.py:496
  63.1 0.1 broadcast_in_dim.14.basis_ref
  63.2 0.7 fit.2
  63.9 8.5 %all-to-all-start.2 = ((f32[8,8,128]{2,1,0:T(8,128)}), f32[8,8,128]{2,1,0:T(8,128)S(1)}, u32[]{:S(2)}, u32[]{:S(2)}) async-start(f32[8,8,128]{2,1,0:T(8,128)} %fit.2), calls=%async_computation.2 | async-start | bytes 65536 | tf_op jit(solution)/shard_map/all_to_all | solution.py:499
  72.4 3.5 %late.1.mine_ref = f32[3,8,512]{2,1,0:T(8,128)S(1)} custom-call(s16[16,8,6272]{2,1,0:T(8,128)(2,1)S(1)} %all_to_all.30.data_ref, f32[2,8,512]{2,1,0:T(8,128)S(1)} %get-tuple-element.23.gains_ref, f32[3,8,512]{2,1,0:T(8,128)S(1)} %early.1.before_ref), custom_call_target="tpu_custom_call" | custom-call | flops 1610612736 | bytes 1687552 | tf_op jit(solution)/shard_map/late/pallas_call | solution.py:446
  75.9 4.5 %all-to-all-done.2.parts_ref = f32[8,8,128]{2,1,0:T(8,128)S(1)} async-done(((f32[8,8,128]{2,1,0:T(8,128)}), f32[8,8,128]{2,1,0:T(8,128)S(1)}, u32[]{:S(2)}, u32[]{:S(2)}) %all-to-all-start.2) | async-done | bytes 32800 | tf_op jit(solution)/shard_map/all_to_all | solution.py:499
  80.4 0.7 spread.1
  81.1 4.7 %all-to-all-start.3 = ((f32[16,8,128]{2,1,0:T(8,128)}), f32[16,8,128]{2,1,0:T(8,128)S(1)}, u32[]{:S(2)}, u32[]{:S(2)}) async-start(f32[16,8,128]{2,1,0:T(8,128)} %get-tuple-element.28), calls=%async_computation.3 | async-start | bytes 131072 | tf_op jit(solution)/shard_map/all_to_all | solution.py:496
  85.9 0.0 collective-permute-start.3
  85.9 1.2 collective-permute-done.3.other_ref
  87.1 5.1 %all-to-all-done.3.fit_ref = f32[16,8,128]{2,1,0:T(8,128)S(1)} async-done(((f32[16,8,128]{2,1,0:T(8,128)}), f32[16,8,128]{2,1,0:T(8,128)S(1)}, u32[]{:S(2)}, u32[]{:S(2)}) %all-to-all-start.3) | async-done | bytes 65568 | tf_op jit(solution)/shard_map/all_to_all | solution.py:496
  92.2 6.6 %retarget.1 = (f32[3,8,512]{2,1,0:T(8,128)S(1)}, f32[2,8,512]{2,1,0:T(8,128)S(1)}, f32[2,8,512]{2,1,0:T(8,128)S(1)}) custom-call(s16[16,8,6272]{2,1,0:T(8,128)(2,1)S(1)} %all_to_all.30.data_ref, f32[3,8,512]{2,1,0:T(8,128)S(1)} %late.1.mine_ref, f32[3,8,512]{2,1,0:T(8,128)S(1)} %collective-permute-done.3.other_ref, ...), custom_call_target="tpu_custom_call" | custom-call | flops 3221225472 | bytes 1802240 | tf_op jit(solution)/shard_map/retarget/pallas_call | solution.py:446
  98.9 0.1 collective-permute-start.4
  99.0 1.2 collective-permute-done.4.other_ref
  100.2 0.6 finish.3
  100.8 10.8 %all_to_all.31.blocks_ref.refs_0_ = f32[16,8,128]{2,1,0:T(8,128)S(1)} all-to-all(f32[16,8,128]{2,1,0:T(8,128)S(1)} %get-tuple-element.32), channel_id=1, replica_groups=mesh['freq'=8,'pair'=16,'core'=2] {'pair'}, dimensions={0} | all-to-all | bytes 131072 | tf_op jit(solution)/shard_map/all_to_all | solution.py:496
  111.6 0.7 fit.3
  112.3 3.3 %all-to-all-start.5 = ((f32[8,8,128]{2,1,0:T(8,128)}), f32[8,8,128]{2,1,0:T(8,128)S(1)}, u32[]{:S(2)}, u32[]{:S(2)}) async-start(f32[8,8,128]{2,1,0:T(8,128)} %fit.3), calls=%async_computation.5 | async-start | bytes 65536 | tf_op jit(solution)/shard_map/all_to_all | solution.py:499
  115.7 0.8 place.1
  116.5 7.1 %all-to-all-done.5.parts_ref = f32[8,8,128]{2,1,0:T(8,128)S(1)} async-done(((f32[8,8,128]{2,1,0:T(8,128)}), f32[8,8,128]{2,1,0:T(8,128)S(1)}, u32[]{:S(2)}, u32[]{:S(2)}) %all-to-all-start.5) | async-done | bytes 32800 | tf_op jit(solution)/shard_map/all_to_all | solution.py:499
  123.6 0.9 final.1
  (1 shorter events, 0.0 us)
Async XLA Ops:
  0.6 3.9 %copy-start = (f32[2,4,32,16]{2,3,1,0:T(8,128)S(1)}, f32[2,4,32,16]{2,3,1,0:T(8,128)}, u32[]{:S(2)}) copy-start(f32[2,4,32,16]{2,3,1,0:T(8,128)} %param.7) | copy-start | bytes 49156
  0.6 3.8 %collective-permute-start = (f32[2,4,16,32]{3,2,1,0:T(8,128)}, f32[2,4,16,32]{3,2,1,0:T(8,128)S(1)}, u32[]{:S(2)}, u32[]{:S(2)}) collective-permute-start(f32[2,4,16,32]{3,2,1,0:T(8,128)} %bitcast.6), channel_id=1, source_target_pairs={{0,1},{1,0},{2,3},{3,2},{4,5},{5,4},{6,7},{7,6},{8,9},{9,8},{10,11... | collective-permute-start | bytes 49160 | tf_op jit(solution)/shard_map/ppermute | solution.py:493
  42.1 1.3 %collective-permute-start.1 = (f32[3,8,512]{2,1,0:T(8,128)S(1)}, f32[3,8,512]{2,1,0:T(8,128)S(1)}, u32[]{:S(2)}, u32[]{:S(2)}) collective-permute-start(f32[3,8,512]{2,1,0:T(8,128)S(1)} %get-tuple-element.18.mine_ref), channel_id=1, source_target_pairs={{0,1},{1,0},{2,3},{3,2},{4,5},{5,4},{6,7},{7,6},{8,9},{9,8},{10,11... | collective-permute-start | bytes 147464 | tf_op jit(solution)/shard_map/ppermute | solution.py:493
  49.9 1.3 %collective-permute-start.2 = (f32[3,8,512]{2,1,0:T(8,128)S(1)}, f32[3,8,512]{2,1,0:T(8,128)S(1)}, u32[]{:S(2)}, u32[]{:S(2)}) collective-permute-start(f32[3,8,512]{2,1,0:T(8,128)S(1)} %get-tuple-element.20.mine_ref), channel_id=1, source_target_pairs={{0,1},{1,0},{2,3},{3,2},{4,5},{5,4},{6,7},{7,6},{8,9},{9,8},{10,11... | collective-permute-start | bytes 147464 | tf_op jit(solution)/shard_map/ppermute | solution.py:493
  51.9 11.1 %all-to-all-start.1 = ((f32[16,8,128]{2,1,0:T(8,128)}), f32[16,8,128]{2,1,0:T(8,128)S(1)}, u32[]{:S(2)}, u32[]{:S(2)}) async-start(f32[16,8,128]{2,1,0:T(8,128)} %get-tuple-element.22), calls=%async_computation.1 | async-start | bytes 131072 | tf_op jit(solution)/shard_map/all_to_all | solution.py:496
  63.9 16.5 %all-to-all-start.2 = ((f32[8,8,128]{2,1,0:T(8,128)}), f32[8,8,128]{2,1,0:T(8,128)S(1)}, u32[]{:S(2)}, u32[]{:S(2)}) async-start(f32[8,8,128]{2,1,0:T(8,128)} %fit.2), calls=%async_computation.2 | async-start | bytes 65536 | tf_op jit(solution)/shard_map/all_to_all | solution.py:499
  81.1 11.1 %all-to-all-start.3 = ((f32[16,8,128]{2,1,0:T(8,128)}), f32[16,8,128]{2,1,0:T(8,128)S(1)}, u32[]{:S(2)}, u32[]{:S(2)}) async-start(f32[16,8,128]{2,1,0:T(8,128)} %get-tuple-element.28), calls=%async_computation.3 | async-start | bytes 131072 | tf_op jit(solution)/shard_map/all_to_all | solution.py:496
  85.9 1.2 collective-permute-start.3
  98.9 1.3 %collective-permute-start.4 = (f32[3,8,512]{2,1,0:T(8,128)S(1)}, f32[3,8,512]{2,1,0:T(8,128)S(1)}, u32[]{:S(2)}, u32[]{:S(2)}) collective-permute-start(f32[3,8,512]{2,1,0:T(8,128)S(1)} %get-tuple-element.29.mine_ref), channel_id=1, source_target_pairs={{0,1},{1,0},{2,3},{3,2},{4,5},{5,4},{6,7},{7,6},{8,9},{9,8},{10,11... | collective-permute-start | bytes 147464 | tf_op jit(solution)/shard_map/ppermute | solution.py:493
  112.3 11.3 %all-to-all-start.5 = ((f32[8,8,128]{2,1,0:T(8,128)}), f32[8,8,128]{2,1,0:T(8,128)S(1)}, u32[]{:S(2)}, u32[]{:S(2)}) async-start(f32[8,8,128]{2,1,0:T(8,128)} %fit.3), calls=%async_computation.5 | async-start | bytes 65536 | tf_op jit(solution)/shard_map/all_to_all | solution.py:499

commit v6 on v5

--- a/solution.py
+++ b/solution.py
@@ -19,8 +19,6 @@
 GAIN_STEPS = 4096.0
 REST_STEPS = 2.0**27
 COPIES = 4
-PACK_VMEM_LIMIT = 58 * 1024 * 1024
-SEED_VMEM_LIMIT = 53 * 1024 * 1024
 VMEM_LIMIT = 24 * 1024 * 1024
 f32, bf16, i32, i16 = jnp.float32, jnp.bfloat16, jnp.int32, jnp.int16
 
@@ -52,7 +50,7 @@
 
 
 def pack_kernel(
-    coh_hbm, vis_hbm, pairs_hbm, out_hbm, coh_ref, vis_ref, pairs_ref, out_ref, coh_sem, vis_sem, pairs_sem, out_sem
+    coh_hbm, vis_hbm, pairs_hbm, out_ref, coh_ref, vis_ref, pairs_ref, coh_sem, vis_sem, pairs_sem
 ):
     rows = vis_ref.shape[2]
     count = out_ref.shape[0]
@@ -117,21 +115,13 @@
 
     pairs_copy.wait()
     step = piece // LANES
-    sent = []
     for index, group in enumerate(copies):
         for copy in group[0::2]:
             copy.wait()
         lax.fori_loop(index * step, (index + 1) * step, columns, 0)
-        for start in (at["re"], at["re"] + half, at["im"], at["im"] + half, at["misc"], at["misc"] + half):
-            lanes = pl.ds(start + index * piece, piece)
-            copy = pltpu.make_async_copy(out_ref.at[:, :, lanes], out_hbm.at[:, :, lanes], out_sem.at[len(sent)])
-            copy.start()
-            sent.append(copy)
-    for copy in sent:
-        copy.wait()
-
-
-def seed_kernel(core_ref, mine_ref, other_ref, packed_hbm, out_hbm, block_ref, block_sem):
+
+
+def seed_kernel(core_ref, mine_ref, other_ref, packed_ref, out_ref, block_ref, block_sem):
     count = block_ref.shape[0]
     is_first = core_ref[0] == 0
     parts = []
@@ -145,8 +135,8 @@
     blocks = [square[d * 2 * count : (d + 1) * 2 * count] for d in range(SKY_DIRECTIONS)]
     for p in range(count):
         block_ref[p] = coded(pick_channel_pair(blocks, p))
-    width = out_hbm.shape[2]
-    copy = pltpu.make_async_copy(block_ref, out_hbm.at[:, :, width - LANES : width], block_sem)
+    width = out_ref.shape[2]
+    copy = pltpu.make_async_copy(block_ref, out_ref.at[:, :, width - LANES : width], block_sem)
     copy.start()
     copy.wait()
 
@@ -432,25 +422,23 @@
     out_shape,
     *inputs,
     scalars=0,
-    in_hbm=(),
-    out_hbm=False,
+    outside=(),
     aliases=None,
     flops=0,
     scratch=(),
-    limit=VMEM_LIMIT,
 ):
     whole = pl.BlockSpec(memory_space=pltpu.VMEM)
-    outside = pl.BlockSpec(memory_space=pltpu.HBM)
+    anywhere = pl.BlockSpec(memory_space=pl.ANY)
     specs = [pl.BlockSpec(memory_space=pltpu.SMEM)] * scalars
-    specs += [outside if k in in_hbm else whole for k in range(scalars, len(inputs))]
+    specs += [anywhere if k in outside else whole for k in range(scalars, len(inputs))]
     return pl.pallas_call(
         kernel,
         out_shape=out_shape,
         in_specs=specs,
-        out_specs=jax.tree.map(lambda _: outside if out_hbm else whole, out_shape),
+        out_specs=jax.tree.map(lambda _: anywhere if aliases else whole, out_shape),
         scratch_shapes=list(scratch),
         input_output_aliases=aliases or {},
-        compiler_params=pltpu.CompilerParams(vmem_limit_bytes=limit),
+        compiler_params=pltpu.CompilerParams(vmem_limit_bytes=VMEM_LIMIT),
         cost_estimate=pl.CostEstimate(
             flops=flops, bytes_accessed=sum(x.size * x.dtype.itemsize for x in inputs), transcendentals=0
         ),
@@ -489,6 +477,9 @@
     sweep = functools.partial(call, flops=flops, scratch=scratch)
     half_sweep = functools.partial(call, flops=flops // 2, scratch=scratch)
 
+    def in_hbm(array):
+        return pltpu.with_memory_space_constraint(array, pltpu.HBM)
+
     def exchange(partial):
         return lax.ppermute(partial, "core", swap)
 
@@ -504,21 +495,17 @@
         "pack",
         pack_kernel,
         packed_shape,
-        coherency,
-        vis,
-        station_pairs,
-        in_hbm=(0, 1, 2),
-        out_hbm=True,
-        limit=PACK_VMEM_LIMIT,
+        in_hbm(coherency),
+        in_hbm(vis),
+        in_hbm(station_pairs),
+        outside=(0, 1, 2),
         scratch=[
             pltpu.VMEM(coherency.shape, bf16),
             pltpu.VMEM(vis.shape, f32),
             pltpu.VMEM(station_pairs.shape, i32),
-            pltpu.VMEM(packed_shape.shape, i16),
             pltpu.SemaphoreType.DMA((2 * COPIES,)),
             pltpu.SemaphoreType.DMA((2 * COPIES,)),
             pltpu.SemaphoreType.DMA,
-            pltpu.SemaphoreType.DMA((6 * COPIES,)),
         ],
     )
     packed = call(
@@ -530,10 +517,8 @@
         exchange(start),
         packed,
         scalars=1,
-        in_hbm=(3,),
-        out_hbm=True,
+        outside=(3,),
         aliases={3: 0},
-        limit=SEED_VMEM_LIMIT,
         scratch=[pltpu.VMEM((pairs, 8, LANES), i16), pltpu.SemaphoreType.DMA],
     )
     data = to_pairs(packed)

time: 125 us -> 123 us (0.984)
  Pallas kernels: 36.4 us -> 34.8 us
    pallas_call x14, Pallas kernels: 36.4 us -> 34.8 us  [call(): pl.pallas_call(kernel, out_shape=out_shape, in_specs=specs, out_specs=jax...]
where the time goes in v6:
time: 123 us
  blocking collectives  40.7 us (33%)
  Pallas kernels  34.8 us (28%)
  waiting for transfers between devices  23.5 us (19%)
  starting transfers between devices  21.8 us (18%)
    all_to_all x2, blocking collectives, to_pairs(): return lax.all_to_all(block, 'pair', 0, 0, tiled=True)  40.7 us
    pallas_call x14, Pallas kernels, call(): pl.pallas_call(kernel, out_shape=out_shape, in_specs=specs, out_specs=jax...  34.8 us
    all_to_all x2, starting transfers between devices, over_bands(): return lax.all_to_all(block, 'freq', 0, 0, tiled=True)  11.8 us
    all_to_all x2, waiting for transfers between devices, over_bands(): return lax.all_to_all(block, 'freq', 0, 0, tiled=True)  11.7 us
    all_to_all x2, starting transfers between devices, to_pairs(): return lax.all_to_all(block, 'pair', 0, 0, tiled=True)  9.5 us
    all_to_all x2, waiting for transfers between devices, to_pairs(): return lax.all_to_all(block, 'pair', 0, 0, tiled=True)  8.02 us
    ppermute x5, waiting for transfers between devices, exchange(): return lax.ppermute(partial, 'core', swap)  3.83 us
  transfers between devices with their start and end apart: 9, of which 8 were waited for; matrix products, arithmetic and copies ran while one was open for 1% of the time, Pallas kernels for 9%

profile of v6, /device:TPU:2, one launch (start us, length us, event | category | flops | bytes accessed | tf_op | source)
XLA Modules:
  0.0 122.7 jit_solution(12924402285153957340)
XLA Ops:
  0.6 0.0 copy-start
  0.6 0.1 collective-permute-start
  0.7 2.7 %pack.1.packed_ref = s16[16,8,6272]{2,1,0:T(8,128)(2,1)S(1)} custom-call(bf16[2,4,32,2048]{3,2,1,0:T(8,128)(2,1)} %coh_hbm.1, f32[2,32,2048]{2,1,0:T(8,128)} %vis_hbm.1, s32[2,2048]{1,0:T(2,128)} %pairs_hbm.1), custom_call_target="tpu_custom_call" | custom-call | bytes 1589248 | tf_op jit(solution)/shard_map/pack/pallas_call | solution.py:434
  3.5 0.0 collective-permute-done.other_ref
  3.5 0.0 copy-done
  3.5 0.2 seed.1
  3.7 29.9 %all_to_all.30.data_ref = s16[16,8,6272]{2,1,0:T(8,128)(2,1)S(1)} all-to-all(s16[16,8,6272]{2,1,0:T(8,128)(2,1)S(1)} %seed.1), channel_id=1, replica_groups=mesh['freq'=8,'pair'=16,'core'=2] {'pair'}, dimensions={0} | all-to-all | bytes 3211264 | tf_op jit(solution)/shard_map/all_to_all | solution.py:487
  33.6 6.7 %first.1 = (f32[3,8,512]{2,1,0:T(8,128)S(1)}, f32[2,8,512]{2,1,0:T(8,128)S(1)}) custom-call(s16[16,8,6272]{2,1,0:T(8,128)(2,1)S(1)} %all_to_all.30.data_ref), custom_call_target="tpu_custom_call" | custom-call | flops 3221225472 | bytes 1605632 | tf_op jit(solution)/shard_map/first/pallas_call | solution.py:434
  40.3 0.1 collective-permute-start.1
  40.4 1.2 collective-permute-done.1.other_ref
  41.6 6.5 %step.1 = (f32[3,8,512]{2,1,0:T(8,128)S(1)}, f32[2,8,512]{2,1,0:T(8,128)S(1)}) custom-call(s16[16,8,6272]{2,1,0:T(8,128)(2,1)S(1)} %all_to_all.30.data_ref, f32[3,8,512]{2,1,0:T(8,128)S(1)} %get-tuple-element.18.mine_ref, f32[3,8,512]{2,1,0:T(8,128)S(1)} %collective-permute-done.1.other_ref, f32[2,8,512]{2,1,0:T(8,128)S(1)} %get-tuple-element.19.gains_ref.target_ref), custom_call_target="tpu_custom_call" | custom-call | flops 3221225472 | bytes 1736704 | tf_op jit(solution)/shard_map/step/pallas_call | solution.py:434
  48.1 0.2 collective-permute-start.2
  48.3 0.7 constant_dynamic-slice_fusion
  49.0 0.1 copy.9
  49.1 0.1 copy.10
  49.2 0.2 collective-permute-done.2.other_ref
  49.4 0.7 finish.2
  50.1 4.8 %all-to-all-start.1 = ((f32[16,8,128]{2,1,0:T(8,128)}), f32[16,8,128]{2,1,0:T(8,128)S(1)}, u32[]{:S(2)}, u32[]{:S(2)}) async-start(f32[16,8,128]{2,1,0:T(8,128)} %get-tuple-element.22), calls=%async_computation.1 | async-start | bytes 131072 | tf_op jit(solution)/shard_map/all_to_all | solution.py:487
  54.9 3.5 %early.1.before_ref = f32[3,8,512]{2,1,0:T(8,128)S(1)} custom-call(s16[16,8,6272]{2,1,0:T(8,128)(2,1)S(1)} %all_to_all.30.data_ref, f32[2,8,512]{2,1,0:T(8,128)S(1)} %get-tuple-element.23.gains_ref), custom_call_target="tpu_custom_call" | custom-call | flops 1610612736 | bytes 1638400 | tf_op jit(solution)/shard_map/early/pallas_call | solution.py:434
  58.4 2.9 %all-to-all-done.1.refs_0_.gains_ref = f32[16,8,128]{2,1,0:T(8,128)S(1)} async-done(((f32[16,8,128]{2,1,0:T(8,128)}), f32[16,8,128]{2,1,0:T(8,128)S(1)}, u32[]{:S(2)}, u32[]{:S(2)}) %all-to-all-start.1) | async-done | bytes 65568 | tf_op jit(solution)/shard_map/all_to_all | solution.py:487
  61.2 0.1 broadcast_in_dim.14.basis_ref
  61.4 0.7 fit.2
  62.1 8.5 %all-to-all-start.2 = ((f32[8,8,128]{2,1,0:T(8,128)}), f32[8,8,128]{2,1,0:T(8,128)S(1)}, u32[]{:S(2)}, u32[]{:S(2)}) async-start(f32[8,8,128]{2,1,0:T(8,128)} %fit.2), calls=%async_computation.2 | async-start | bytes 65536 | tf_op jit(solution)/shard_map/all_to_all | solution.py:490
  70.6 3.5 %late.1.mine_ref = f32[3,8,512]{2,1,0:T(8,128)S(1)} custom-call(s16[16,8,6272]{2,1,0:T(8,128)(2,1)S(1)} %all_to_all.30.data_ref, f32[2,8,512]{2,1,0:T(8,128)S(1)} %get-tuple-element.23.gains_ref, f32[3,8,512]{2,1,0:T(8,128)S(1)} %early.1.before_ref), custom_call_target="tpu_custom_call" | custom-call | flops 1610612736 | bytes 1687552 | tf_op jit(solution)/shard_map/late/pallas_call | solution.py:434
  74.0 4.5 %all-to-all-done.2.parts_ref = f32[8,8,128]{2,1,0:T(8,128)S(1)} async-done(((f32[8,8,128]{2,1,0:T(8,128)}), f32[8,8,128]{2,1,0:T(8,128)S(1)}, u32[]{:S(2)}, u32[]{:S(2)}) %all-to-all-start.2) | async-done | bytes 32800 | tf_op jit(solution)/shard_map/all_to_all | solution.py:490
  78.6 0.7 spread.1
  79.3 4.7 %all-to-all-start.3 = ((f32[16,8,128]{2,1,0:T(8,128)}), f32[16,8,128]{2,1,0:T(8,128)S(1)}, u32[]{:S(2)}, u32[]{:S(2)}) async-start(f32[16,8,128]{2,1,0:T(8,128)} %get-tuple-element.28), calls=%async_computation.3 | async-start | bytes 131072 | tf_op jit(solution)/shard_map/all_to_all | solution.py:487
  84.0 0.0 collective-permute-start.3
  84.1 1.2 collective-permute-done.3.other_ref
  85.3 5.1 %all-to-all-done.3.fit_ref = f32[16,8,128]{2,1,0:T(8,128)S(1)} async-done(((f32[16,8,128]{2,1,0:T(8,128)}), f32[16,8,128]{2,1,0:T(8,128)S(1)}, u32[]{:S(2)}, u32[]{:S(2)}) %all-to-all-start.3) | async-done | bytes 65568 | tf_op jit(solution)/shard_map/all_to_all | solution.py:487
  90.4 6.6 %retarget.1 = (f32[3,8,512]{2,1,0:T(8,128)S(1)}, f32[2,8,512]{2,1,0:T(8,128)S(1)}, f32[2,8,512]{2,1,0:T(8,128)S(1)}) custom-call(s16[16,8,6272]{2,1,0:T(8,128)(2,1)S(1)} %all_to_all.30.data_ref, f32[3,8,512]{2,1,0:T(8,128)S(1)} %late.1.mine_ref, f32[3,8,512]{2,1,0:T(8,128)S(1)} %collective-permute-done.3.other_ref, ...), custom_call_target="tpu_custom_call" | custom-call | flops 3221225472 | bytes 1802240 | tf_op jit(solution)/shard_map/retarget/pallas_call | solution.py:434
  97.0 0.1 collective-permute-start.4
  97.1 1.2 collective-permute-done.4.other_ref
  98.3 0.6 finish.3
  99.0 10.8 %all_to_all.31.blocks_ref.refs_0_ = f32[16,8,128]{2,1,0:T(8,128)S(1)} all-to-all(f32[16,8,128]{2,1,0:T(8,128)S(1)} %get-tuple-element.32), channel_id=1, replica_groups=mesh['freq'=8,'pair'=16,'core'=2] {'pair'}, dimensions={0} | all-to-all | bytes 131072 | tf_op jit(solution)/shard_map/all_to_all | solution.py:487
  109.8 0.7 fit.3
  110.5 3.3 %all-to-all-start.5 = ((f32[8,8,128]{2,1,0:T(8,128)}), f32[8,8,128]{2,1,0:T(8,128)S(1)}, u32[]{:S(2)}, u32[]{:S(2)}) async-start(f32[8,8,128]{2,1,0:T(8,128)} %fit.3), calls=%async_computation.5 | async-start | bytes 65536 | tf_op jit(solution)/shard_map/all_to_all | solution.py:490
  113.9 0.8 place.1
  114.7 7.1 %all-to-all-done.5.parts_ref = f32[8,8,128]{2,1,0:T(8,128)S(1)} async-done(((f32[8,8,128]{2,1,0:T(8,128)}), f32[8,8,128]{2,1,0:T(8,128)S(1)}, u32[]{:S(2)}, u32[]{:S(2)}) %all-to-all-start.5) | async-done | bytes 32800 | tf_op jit(solution)/shard_map/all_to_all | solution.py:490
  121.8 0.9 final.1
  (1 shorter events, 0.0 us)
Async XLA Ops:
  0.6 2.8 %copy-start = (f32[2,4,32,16]{2,3,1,0:T(8,128)S(1)}, f32[2,4,32,16]{2,3,1,0:T(8,128)}, u32[]{:S(2)}) copy-start(f32[2,4,32,16]{2,3,1,0:T(8,128)} %param.7) | copy-start | bytes 49156
  0.6 2.8 %collective-permute-start = (f32[2,4,16,32]{3,2,1,0:T(8,128)}, f32[2,4,16,32]{3,2,1,0:T(8,128)S(1)}, u32[]{:S(2)}, u32[]{:S(2)}) collective-permute-start(f32[2,4,16,32]{3,2,1,0:T(8,128)} %bitcast.6), channel_id=1, source_target_pairs={{0,1},{1,0},{2,3},{3,2},{4,5},{5,4},{6,7},{7,6},{8,9},{9,8},{10,11... | collective-permute-start | bytes 49160 | tf_op jit(solution)/shard_map/ppermute | solution.py:484
  40.3 1.3 %collective-permute-start.1 = (f32[3,8,512]{2,1,0:T(8,128)S(1)}, f32[3,8,512]{2,1,0:T(8,128)S(1)}, u32[]{:S(2)}, u32[]{:S(2)}) collective-permute-start(f32[3,8,512]{2,1,0:T(8,128)S(1)} %get-tuple-element.18.mine_ref), channel_id=1, source_target_pairs={{0,1},{1,0},{2,3},{3,2},{4,5},{5,4},{6,7},{7,6},{8,9},{9,8},{10,11... | collective-permute-start | bytes 147464 | tf_op jit(solution)/shard_map/ppermute | solution.py:484
  48.1 1.3 %collective-permute-start.2 = (f32[3,8,512]{2,1,0:T(8,128)S(1)}, f32[3,8,512]{2,1,0:T(8,128)S(1)}, u32[]{:S(2)}, u32[]{:S(2)}) collective-permute-start(f32[3,8,512]{2,1,0:T(8,128)S(1)} %get-tuple-element.20.mine_ref), channel_id=1, source_target_pairs={{0,1},{1,0},{2,3},{3,2},{4,5},{5,4},{6,7},{7,6},{8,9},{9,8},{10,11... | collective-permute-start | bytes 147464 | tf_op jit(solution)/shard_map/ppermute | solution.py:484
  50.1 11.1 %all-to-all-start.1 = ((f32[16,8,128]{2,1,0:T(8,128)}), f32[16,8,128]{2,1,0:T(8,128)S(1)}, u32[]{:S(2)}, u32[]{:S(2)}) async-start(f32[16,8,128]{2,1,0:T(8,128)} %get-tuple-element.22), calls=%async_computation.1 | async-start | bytes 131072 | tf_op jit(solution)/shard_map/all_to_all | solution.py:487
  62.1 16.5 %all-to-all-start.2 = ((f32[8,8,128]{2,1,0:T(8,128)}), f32[8,8,128]{2,1,0:T(8,128)S(1)}, u32[]{:S(2)}, u32[]{:S(2)}) async-start(f32[8,8,128]{2,1,0:T(8,128)} %fit.2), calls=%async_computation.2 | async-start | bytes 65536 | tf_op jit(solution)/shard_map/all_to_all | solution.py:490
  79.3 11.1 %all-to-all-start.3 = ((f32[16,8,128]{2,1,0:T(8,128)}), f32[16,8,128]{2,1,0:T(8,128)S(1)}, u32[]{:S(2)}, u32[]{:S(2)}) async-start(f32[16,8,128]{2,1,0:T(8,128)} %get-tuple-element.28), calls=%async_computation.3 | async-start | bytes 131072 | tf_op jit(solution)/shard_map/all_to_all | solution.py:487
  84.0 1.2 %collective-permute-start.3 = (f32[3,8,512]{2,1,0:T(8,128)S(1)}, f32[3,8,512]{2,1,0:T(8,128)S(1)}, u32[]{:S(2)}, u32[]{:S(2)}) collective-permute-start(f32[3,8,512]{2,1,0:T(8,128)S(1)} %late.1.mine_ref), channel_id=1, source_target_pairs={{0,1},{1,0},{2,3},{3,2},{4,5},{5,4},{6,7},{7,6},{8,9},{9,8},{10,11... | collective-permute-start | bytes 147464 | tf_op jit(solution)/shard_map/ppermute | solution.py:484
  97.0 1.3 %collective-permute-start.4 = (f32[3,8,512]{2,1,0:T(8,128)S(1)}, f32[3,8,512]{2,1,0:T(8,128)S(1)}, u32[]{:S(2)}, u32[]{:S(2)}) collective-permute-start(f32[3,8,512]{2,1,0:T(8,128)S(1)} %get-tuple-element.29.mine_ref), channel_id=1, source_target_pairs={{0,1},{1,0},{2,3},{3,2},{4,5},{5,4},{6,7},{7,6},{8,9},{9,8},{10,11... | collective-permute-start | bytes 147464 | tf_op jit(solution)/shard_map/ppermute | solution.py:484
  110.5 11.3 %all-to-all-start.5 = ((f32[8,8,128]{2,1,0:T(8,128)}), f32[8,8,128]{2,1,0:T(8,128)S(1)}, u32[]{:S(2)}, u32[]{:S(2)}) async-start(f32[8,8,128]{2,1,0:T(8,128)} %fit.3), calls=%async_computation.5 | async-start | bytes 65536 | tf_op jit(solution)/shard_map/all_to_all | solution.py:490

commit v7 on v6

--- a/solution.py
+++ b/solution.py
@@ -34,11 +34,12 @@
 
 
 def lanes_of(rows):
-    return {"re": 0, "im": rows, "misc": 2 * rows, "start": 3 * rows}
+    start = 2 * rows + 3 * rows // 4
+    return {"re": 0, "im": rows, "misc": 2 * rows, "start": start, "scale": start + LANES}
 
 
 def rows_of(data_ref):
-    return (data_ref.shape[2] - LANES) // 3
+    return (data_ref.shape[2] - 2 * LANES) * 4 // 11
 
 
 def coded(values):
@@ -93,7 +94,24 @@
         over = peak > 32767.0 * 2.0**power
         exponent = jnp.where(over, power + 1.0, exponent)
         inverse = jnp.where(over, 2.0 ** (-power - 1), inverse)
-    exponent = jnp.broadcast_to(exponent, (2, LANES))
+    exponent = coded(jnp.broadcast_to(exponent, (8, LANES)))
+    for p in range(count):
+        out_ref[p, :, at["scale"] : at["scale"] + LANES] = exponent
+    pairs_copy.wait()
+
+    def misc(group, carry):
+        columns = [pl.ds(pl.multiple_of((4 * group + k) * LANES, LANES), LANES) for k in range(4)]
+        stations = coded(jnp.concatenate([pairs_ref[:, lanes].astype(f32) for lanes in columns], 0))
+        seen = [[vis_ref[part, :, lanes] * inverse for lanes in columns] for part in range(2)]
+        place = at["misc"] + 3 * LANES * group
+        places = [pl.ds(pl.multiple_of(place + k * LANES, LANES), LANES) for k in range(3)]
+        for p in range(count):
+            out_ref[p, :, places[0]] = coded(pick_channel_pair(seen[0], p))
+            out_ref[p, :, places[1]] = coded(pick_channel_pair(seen[1], p))
+            out_ref[p, :, places[2]] = stations
+        return carry
+
+    lax.fori_loop(0, rows // (4 * LANES), misc, 0)
 
     def columns(index, carry):
         early = pl.multiple_of(index * LANES, LANES)
@@ -105,15 +123,8 @@
                 place = pl.multiple_of(offset + part * rows, LANES)
                 for p in range(count):
                     out_ref[p, :, pl.ds(place, LANES)] = coded(pick_channel_pair(blocks, p))
-            seen = [vis_ref[part, :, lanes] * inverse for part in range(2)]
-            tail = jnp.concatenate([pairs_ref[:, lanes].astype(f32), exponent], 0)
-            place = pl.multiple_of(offset + at["misc"], LANES)
-            for p in range(count):
-                block = jnp.concatenate([seen[0][2 * p : 2 * p + 2], seen[1][2 * p : 2 * p + 2], tail], 0)
-                out_ref[p, :, pl.ds(place, LANES)] = coded(block)
         return carry
 
-    pairs_copy.wait()
     step = piece // LANES
     for index, group in enumerate(copies):
         for copy in group[0::2]:
@@ -136,7 +147,7 @@
     for p in range(count):
         block_ref[p] = coded(pick_channel_pair(blocks, p))
     width = out_ref.shape[2]
-    copy = pltpu.make_async_copy(block_ref, out_ref.at[:, :, width - LANES : width], block_sem)
+    copy = pltpu.make_async_copy(block_ref, out_ref.at[:, :, width - 2 * LANES : width - LANES], block_sem)
     copy.start()
     copy.wait()
 
@@ -191,22 +202,22 @@
     return [word[:, h * LANES : (h + 1) * LANES] for h in range(PARTS)], unit
 
 
-def column_terms(coh_re, coh_im, misc, vis_unit, words, square, sublane):
+def column_terms(coh_re, coh_im, seen_re, seen_im, stations, place, words, square, sublane):
     def station(row):
-        index = jnp.broadcast_to(misc[row : row + 1], (8, LANES))
+        index = jnp.broadcast_to(stations[row : row + 1], (8, LANES))
         return index & (LANES - 1), index >> 7
 
-    low_first, high_first = station(4)
-    low_second, high_second = station(5)
+    low_first, high_first = station(2 * place)
+    low_second, high_second = station(2 * place + 1)
     near_re, near_im = lookup(words, low_first, high_first)
     far_re, far_im = lookup(words, low_second, high_second)
     z_re = coh_re * far_re + coh_im * far_im
     z_im = coh_im * far_re - coh_re * far_im
     x_re = near_re * coh_re - near_im * coh_im
     x_im = near_re * coh_im + near_im * coh_re
-    seen = misc.astype(f32) * vis_unit
-    vis_re = jnp.where(sublane < 2, seen, 0.0)
-    vis_im = jnp.where((sublane >= 2) & (sublane < 4), seen, 0.0)
+    inside = (sublane >> 1) == place
+    vis_re = jnp.where(inside, seen_re, 0.0)
+    vis_im = jnp.where(inside, seen_im, 0.0)
     res_re = vis_re - square * (near_re * z_re - near_im * z_im)
     res_im = vis_im - square * (near_re * z_im + near_im * z_re)
     res_re = res_re + pltpu.roll(res_re, 4, 0)
@@ -248,15 +259,22 @@
 
     def step(source, carry):
         left, right = [], []
-        exponent = data_ref[source, :, at["misc"] : at["misc"] + LANES].astype(i32).astype(f32)
-        vis_unit = jnp.exp2(jnp.broadcast_to(exponent[6:7], (8, LANES)))
+        load = lambda start: data_ref[source, :, start : start + LANES].astype(i32)
+        vis_unit = jnp.exp2(load(at["scale"]).astype(f32))
         for offset in range(0, rows, LANES):
-            load = lambda start: data_ref[source, :, start : start + LANES].astype(i32)
+            place = offset // LANES % 4
+            if place == 0:
+                group = at["misc"] + 3 * offset // 4
+                seen_re = load(group).astype(f32) * vis_unit
+                seen_im = load(group + LANES).astype(f32) * vis_unit
+                stations = load(group + 2 * LANES)
             terms = column_terms(
                 load(at["re"] + offset).astype(f32),
                 load(at["im"] + offset).astype(f32),
-                load(at["misc"] + offset),
-                vis_unit,
+                seen_re,
+                seen_im,
+                stations,
+                place,
                 words,
                 square,
                 sublane,
@@ -471,7 +489,7 @@
     block_shape = shape((pairs, 8, LANES), f32)
     parts_shape = shape((bands, 8, LANES), f32)
     out_shape = shape((2, SKY_DIRECTIONS, owned, channels_dev), f32)
-    width = 3 * rows_dev + LANES
+    width = 11 * rows_dev // 4 + 2 * LANES
     flops = 2 * rows_dev * pairs * 192 * 256
     scratch = [pltpu.VMEM((2 * LANES, 48 * PARTS), f32)]
     sweep = functools.partial(call, flops=flops, scratch=scratch)

time: 123 us -> 122 us (level)
  no operation moved by 1% of the time
where the time goes in v7:
time: 122 us; the launch traced here: 121 us
  blocking collectives  39.5 us (32%)
  Pallas kernels  34.7 us (28%)
  waiting for transfers between devices  23.5 us (19%)
  starting transfers between devices  21.8 us (18%)
    all_to_all x2, blocking collectives, to_pairs(): return lax.all_to_all(block, 'pair', 0, 0, tiled=True)  39.5 us
    pallas_call x14, Pallas kernels, call(): pl.pallas_call(kernel, out_shape=out_shape, in_specs=specs, out_specs=jax...  34.7 us
    all_to_all x2, starting transfers between devices, over_bands(): return lax.all_to_all(block, 'freq', 0, 0, tiled=True)  11.8 us
    all_to_all x2, waiting for transfers between devices, over_bands(): return lax.all_to_all(block, 'freq', 0, 0, tiled=True)  11.7 us
    all_to_all x2, starting transfers between devices, to_pairs(): return lax.all_to_all(block, 'pair', 0, 0, tiled=True)  9.5 us
    all_to_all x2, waiting for transfers between devices, to_pairs(): return lax.all_to_all(block, 'pair', 0, 0, tiled=True)  8.03 us
    ppermute x5, waiting for transfers between devices, exchange(): return lax.ppermute(partial, 'core', swap)  3.83 us
  transfers between devices with their start and end apart: 9, of which 8 were waited for; matrix products, arithmetic and copies ran while one was open for 1% of the time, Pallas kernels for 9%

profile of v7, /device:TPU:2, one launch (start us, length us, event | category | flops | bytes accessed | tf_op | source)
XLA Modules:
  0.0 121.4 jit_solution(14220294929027158739)
XLA Ops:
  0.6 0.1 collective-permute-start
  0.7 0.0 copy-start
  0.7 2.7 %pack.1.packed_ref = s16[16,8,5888]{2,1,0:T(8,128)(2,1)S(1)} custom-call(bf16[2,4,32,2048]{3,2,1,0:T(8,128)(2,1)} %coh_hbm.1, f32[2,32,2048]{2,1,0:T(8,128)} %vis_hbm.1, s32[2,2048]{1,0:T(2,128)} %pairs_hbm.1), custom_call_target="tpu_custom_call" | custom-call | bytes 1589248 | tf_op jit(solution)/shard_map/pack/pallas_call | solution.py:452
  3.5 0.0 collective-permute-done.other_ref
  3.5 0.0 copy-done
  3.5 0.2 seed.1
  3.7 28.7 %all_to_all.30.data_ref = s16[16,8,5888]{2,1,0:T(8,128)(2,1)S(1)} all-to-all(s16[16,8,5888]{2,1,0:T(8,128)(2,1)S(1)} %seed.1), channel_id=1, replica_groups=mesh['freq'=8,'pair'=16,'core'=2] {'pair'}, dimensions={0} | all-to-all | bytes 3014656 | tf_op jit(solution)/shard_map/all_to_all | solution.py:505
  32.4 6.6 %first.1 = (f32[3,8,512]{2,1,0:T(8,128)S(1)}, f32[2,8,512]{2,1,0:T(8,128)S(1)}) custom-call(s16[16,8,5888]{2,1,0:T(8,128)(2,1)S(1)} %all_to_all.30.data_ref), custom_call_target="tpu_custom_call" | custom-call | flops 3221225472 | bytes 1507328 | tf_op jit(solution)/shard_map/first/pallas_call | solution.py:452
  39.1 0.1 collective-permute-start.1
  39.2 1.2 collective-permute-done.1.other_ref
  40.4 6.4 %step.1 = (f32[3,8,512]{2,1,0:T(8,128)S(1)}, f32[2,8,512]{2,1,0:T(8,128)S(1)}) custom-call(s16[16,8,5888]{2,1,0:T(8,128)(2,1)S(1)} %all_to_all.30.data_ref, f32[3,8,512]{2,1,0:T(8,128)S(1)} %get-tuple-element.18.mine_ref, f32[3,8,512]{2,1,0:T(8,128)S(1)} %collective-permute-done.1.other_ref, f32[2,8,512]{2,1,0:T(8,128)S(1)} %get-tuple-element.19.gains_ref.target_ref), custom_call_target="tpu_custom_call" | custom-call | flops 3221225472 | bytes 1638400 | tf_op jit(solution)/shard_map/step/pallas_call | solution.py:452
  46.8 0.2 collective-permute-start.2
  47.1 0.7 constant_dynamic-slice_fusion
  47.8 0.1 copy.9
  47.9 0.1 copy.10
  47.9 0.2 collective-permute-done.2.other_ref
  48.1 0.7 finish.2
  48.9 4.8 %all-to-all-start.1 = ((f32[16,8,128]{2,1,0:T(8,128)}), f32[16,8,128]{2,1,0:T(8,128)S(1)}, u32[]{:S(2)}, u32[]{:S(2)}) async-start(f32[16,8,128]{2,1,0:T(8,128)} %get-tuple-element.22), calls=%async_computation.1 | async-start | bytes 131072 | tf_op jit(solution)/shard_map/all_to_all | solution.py:505
  53.6 3.5 %early.1.before_ref = f32[3,8,512]{2,1,0:T(8,128)S(1)} custom-call(s16[16,8,5888]{2,1,0:T(8,128)(2,1)S(1)} %all_to_all.30.data_ref, f32[2,8,512]{2,1,0:T(8,128)S(1)} %get-tuple-element.23.gains_ref), custom_call_target="tpu_custom_call" | custom-call | flops 1610612736 | bytes 1540096 | tf_op jit(solution)/shard_map/early/pallas_call | solution.py:452
  57.1 2.9 %all-to-all-done.1.refs_0_.gains_ref = f32[16,8,128]{2,1,0:T(8,128)S(1)} async-done(((f32[16,8,128]{2,1,0:T(8,128)}), f32[16,8,128]{2,1,0:T(8,128)S(1)}, u32[]{:S(2)}, u32[]{:S(2)}) %all-to-all-start.1) | async-done | bytes 65568 | tf_op jit(solution)/shard_map/all_to_all | solution.py:505
  60.0 0.1 broadcast_in_dim.14.basis_ref
  60.1 0.7 fit.2
  60.8 8.5 %all-to-all-start.2 = ((f32[8,8,128]{2,1,0:T(8,128)}), f32[8,8,128]{2,1,0:T(8,128)S(1)}, u32[]{:S(2)}, u32[]{:S(2)}) async-start(f32[8,8,128]{2,1,0:T(8,128)} %fit.2), calls=%async_computation.2 | async-start | bytes 65536 | tf_op jit(solution)/shard_map/all_to_all | solution.py:508
  69.3 3.5 %late.1.mine_ref = f32[3,8,512]{2,1,0:T(8,128)S(1)} custom-call(s16[16,8,5888]{2,1,0:T(8,128)(2,1)S(1)} %all_to_all.30.data_ref, f32[2,8,512]{2,1,0:T(8,128)S(1)} %get-tuple-element.23.gains_ref, f32[3,8,512]{2,1,0:T(8,128)S(1)} %early.1.before_ref), custom_call_target="tpu_custom_call" | custom-call | flops 1610612736 | bytes 1589248 | tf_op jit(solution)/shard_map/late/pallas_call | solution.py:452
  72.8 4.6 %all-to-all-done.2.parts_ref = f32[8,8,128]{2,1,0:T(8,128)S(1)} async-done(((f32[8,8,128]{2,1,0:T(8,128)}), f32[8,8,128]{2,1,0:T(8,128)S(1)}, u32[]{:S(2)}, u32[]{:S(2)}) %all-to-all-start.2) | async-done | bytes 32800 | tf_op jit(solution)/shard_map/all_to_all | solution.py:508
  77.3 0.7 spread.1
  78.0 4.7 %all-to-all-start.3 = ((f32[16,8,128]{2,1,0:T(8,128)}), f32[16,8,128]{2,1,0:T(8,128)S(1)}, u32[]{:S(2)}, u32[]{:S(2)}) async-start(f32[16,8,128]{2,1,0:T(8,128)} %get-tuple-element.28), calls=%async_computation.3 | async-start | bytes 131072 | tf_op jit(solution)/shard_map/all_to_all | solution.py:505
  82.8 0.0 collective-permute-start.3
  82.8 1.2 %collective-permute-done.3.other_ref = f32[3,8,512]{2,1,0:T(8,128)S(1)} collective-permute-done((f32[3,8,512]{2,1,0:T(8,128)S(1)}, f32[3,8,512]{2,1,0:T(8,128)S(1)}, u32[]{:S(2)}, u32[]{:S(2)}) %collective-permute-start.3) | collective-permute-done | bytes 49184 | tf_op jit(solution)/shard_map/ppermute | solution.py:502
  84.0 5.1 %all-to-all-done.3.fit_ref = f32[16,8,128]{2,1,0:T(8,128)S(1)} async-done(((f32[16,8,128]{2,1,0:T(8,128)}), f32[16,8,128]{2,1,0:T(8,128)S(1)}, u32[]{:S(2)}, u32[]{:S(2)}) %all-to-all-start.3) | async-done | bytes 65568 | tf_op jit(solution)/shard_map/all_to_all | solution.py:505
  89.2 6.6 %retarget.1 = (f32[3,8,512]{2,1,0:T(8,128)S(1)}, f32[2,8,512]{2,1,0:T(8,128)S(1)}, f32[2,8,512]{2,1,0:T(8,128)S(1)}) custom-call(s16[16,8,5888]{2,1,0:T(8,128)(2,1)S(1)} %all_to_all.30.data_ref, f32[3,8,512]{2,1,0:T(8,128)S(1)} %late.1.mine_ref, f32[3,8,512]{2,1,0:T(8,128)S(1)} %collective-permute-done.3.other_ref, ...), custom_call_target="tpu_custom_call" | custom-call | flops 3221225472 | bytes 1703936 | tf_op jit(solution)/shard_map/retarget/pallas_call | solution.py:452
  95.7 0.1 collective-permute-start.4
  95.8 1.2 %collective-permute-done.4.other_ref = f32[3,8,512]{2,1,0:T(8,128)S(1)} collective-permute-done((f32[3,8,512]{2,1,0:T(8,128)S(1)}, f32[3,8,512]{2,1,0:T(8,128)S(1)}, u32[]{:S(2)}, u32[]{:S(2)}) %collective-permute-start.4) | collective-permute-done | bytes 49184 | tf_op jit(solution)/shard_map/ppermute | solution.py:502
  97.0 0.6 finish.3
  97.7 10.8 %all_to_all.31.blocks_ref.refs_0_ = f32[16,8,128]{2,1,0:T(8,128)S(1)} all-to-all(f32[16,8,128]{2,1,0:T(8,128)S(1)} %get-tuple-element.32), channel_id=1, replica_groups=mesh['freq'=8,'pair'=16,'core'=2] {'pair'}, dimensions={0} | all-to-all | bytes 131072 | tf_op jit(solution)/shard_map/all_to_all | solution.py:505
  108.5 0.7 fit.3
  109.2 3.3 %all-to-all-start.5 = ((f32[8,8,128]{2,1,0:T(8,128)}), f32[8,8,128]{2,1,0:T(8,128)S(1)}, u32[]{:S(2)}, u32[]{:S(2)}) async-start(f32[8,8,128]{2,1,0:T(8,128)} %fit.3), calls=%async_computation.5 | async-start | bytes 65536 | tf_op jit(solution)/shard_map/all_to_all | solution.py:508
  112.5 0.8 place.1
  113.3 7.1 %all-to-all-done.5.parts_ref = f32[8,8,128]{2,1,0:T(8,128)S(1)} async-done(((f32[8,8,128]{2,1,0:T(8,128)}), f32[8,8,128]{2,1,0:T(8,128)S(1)}, u32[]{:S(2)}, u32[]{:S(2)}) %all-to-all-start.5) | async-done | bytes 32800 | tf_op jit(solution)/shard_map/all_to_all | solution.py:508
  120.5 0.9 final.1
  (1 shorter events, 0.0 us)
Async XLA Ops:
  0.6 2.9 %collective-permute-start = (f32[2,4,16,32]{3,2,1,0:T(8,128)}, f32[2,4,16,32]{3,2,1,0:T(8,128)S(1)}, u32[]{:S(2)}, u32[]{:S(2)}) collective-permute-start(f32[2,4,16,32]{3,2,1,0:T(8,128)} %bitcast.6), channel_id=1, source_target_pairs={{0,1},{1,0},{2,3},{3,2},{4,5},{5,4},{6,7},{7,6},{8,9},{9,8},{10,11... | collective-permute-start | bytes 49160 | tf_op jit(solution)/shard_map/ppermute | solution.py:502
  0.7 2.8 %copy-start = (f32[2,4,32,16]{2,3,1,0:T(8,128)S(1)}, f32[2,4,32,16]{2,3,1,0:T(8,128)}, u32[]{:S(2)}) copy-start(f32[2,4,32,16]{2,3,1,0:T(8,128)} %param.7) | copy-start | bytes 49156
  39.1 1.3 %collective-permute-start.1 = (f32[3,8,512]{2,1,0:T(8,128)S(1)}, f32[3,8,512]{2,1,0:T(8,128)S(1)}, u32[]{:S(2)}, u32[]{:S(2)}) collective-permute-start(f32[3,8,512]{2,1,0:T(8,128)S(1)} %get-tuple-element.18.mine_ref), channel_id=1, source_target_pairs={{0,1},{1,0},{2,3},{3,2},{4,5},{5,4},{6,7},{7,6},{8,9},{9,8},{10,11... | collective-permute-start | bytes 147464 | tf_op jit(solution)/shard_map/ppermute | solution.py:502
  46.8 1.3 %collective-permute-start.2 = (f32[3,8,512]{2,1,0:T(8,128)S(1)}, f32[3,8,512]{2,1,0:T(8,128)S(1)}, u32[]{:S(2)}, u32[]{:S(2)}) collective-permute-start(f32[3,8,512]{2,1,0:T(8,128)S(1)} %get-tuple-element.20.mine_ref), channel_id=1, source_target_pairs={{0,1},{1,0},{2,3},{3,2},{4,5},{5,4},{6,7},{7,6},{8,9},{9,8},{10,11... | collective-permute-start | bytes 147464 | tf_op jit(solution)/shard_map/ppermute | solution.py:502
  48.9 11.1 %all-to-all-start.1 = ((f32[16,8,128]{2,1,0:T(8,128)}), f32[16,8,128]{2,1,0:T(8,128)S(1)}, u32[]{:S(2)}, u32[]{:S(2)}) async-start(f32[16,8,128]{2,1,0:T(8,128)} %get-tuple-element.22), calls=%async_computation.1 | async-start | bytes 131072 | tf_op jit(solution)/shard_map/all_to_all | solution.py:505
  60.8 16.5 %all-to-all-start.2 = ((f32[8,8,128]{2,1,0:T(8,128)}), f32[8,8,128]{2,1,0:T(8,128)S(1)}, u32[]{:S(2)}, u32[]{:S(2)}) async-start(f32[8,8,128]{2,1,0:T(8,128)} %fit.2), calls=%async_computation.2 | async-start | bytes 65536 | tf_op jit(solution)/shard_map/all_to_all | solution.py:508
  78.0 11.1 %all-to-all-start.3 = ((f32[16,8,128]{2,1,0:T(8,128)}), f32[16,8,128]{2,1,0:T(8,128)S(1)}, u32[]{:S(2)}, u32[]{:S(2)}) async-start(f32[16,8,128]{2,1,0:T(8,128)} %get-tuple-element.28), calls=%async_computation.3 | async-start | bytes 131072 | tf_op jit(solution)/shard_map/all_to_all | solution.py:505
  82.8 1.2 %collective-permute-start.3 = (f32[3,8,512]{2,1,0:T(8,128)S(1)}, f32[3,8,512]{2,1,0:T(8,128)S(1)}, u32[]{:S(2)}, u32[]{:S(2)}) collective-permute-start(f32[3,8,512]{2,1,0:T(8,128)S(1)} %late.1.mine_ref), channel_id=1, source_target_pairs={{0,1},{1,0},{2,3},{3,2},{4,5},{5,4},{6,7},{7,6},{8,9},{9,8},{10,11... | collective-permute-start | bytes 147464 | tf_op jit(solution)/shard_map/ppermute | solution.py:502
  95.7 1.3 %collective-permute-start.4 = (f32[3,8,512]{2,1,0:T(8,128)S(1)}, f32[3,8,512]{2,1,0:T(8,128)S(1)}, u32[]{:S(2)}, u32[]{:S(2)}) collective-permute-start(f32[3,8,512]{2,1,0:T(8,128)S(1)} %get-tuple-element.29.mine_ref), channel_id=1, source_target_pairs={{0,1},{1,0},{2,3},{3,2},{4,5},{5,4},{6,7},{7,6},{8,9},{9,8},{10,11... | collective-permute-start | bytes 147464 | tf_op jit(solution)/shard_map/ppermute | solution.py:502
  109.2 11.3 %all-to-all-start.5 = ((f32[8,8,128]{2,1,0:T(8,128)}), f32[8,8,128]{2,1,0:T(8,128)S(1)}, u32[]{:S(2)}, u32[]{:S(2)}) async-start(f32[8,8,128]{2,1,0:T(8,128)} %fit.3), calls=%async_computation.5 | async-start | bytes 65536 | tf_op jit(solution)/shard_map/all_to_all | solution.py:508

commit v8 on v7

--- a/solution.py
+++ b/solution.py
@@ -18,7 +18,7 @@
 COH_STEPS = 4096.0
 GAIN_STEPS = 4096.0
 REST_STEPS = 2.0**27
-COPIES = 4
+COPIES = 1
 VMEM_LIMIT = 24 * 1024 * 1024
 f32, bf16, i32, i16 = jnp.float32, jnp.bfloat16, jnp.int32, jnp.int16
 

time: 122 us -> 122 us (level)
  transfers between devices with their start and end apart: 9 -> 9, of which waited for: 8 -> 8; matrix products, arithmetic and copies ran while one was open for 1% -> 1% of each run, Pallas kernels for 9% -> 8%
where the time goes in v8:
time: 122 us; the launch traced here: 121 us
  blocking collectives  39.5 us (32%)
  Pallas kernels  34.4 us (28%)
  waiting for transfers between devices  23.6 us (19%)
  starting transfers between devices  21.8 us (18%)
    all_to_all x2, blocking collectives, to_pairs(): return lax.all_to_all(block, 'pair', 0, 0, tiled=True)  39.5 us
    pallas_call x14, Pallas kernels, call(): pl.pallas_call(kernel, out_shape=out_shape, in_specs=specs, out_specs=jax...  34.4 us
    all_to_all x2, starting transfers between devices, over_bands(): return lax.all_to_all(block, 'freq', 0, 0, tiled=True)  11.8 us
    all_to_all x2, waiting for transfers between devices, over_bands(): return lax.all_to_all(block, 'freq', 0, 0, tiled=True)  11.7 us
    all_to_all x2, starting transfers between devices, to_pairs(): return lax.all_to_all(block, 'pair', 0, 0, tiled=True)  9.5 us
    all_to_all x2, waiting for transfers between devices, to_pairs(): return lax.all_to_all(block, 'pair', 0, 0, tiled=True)  8.04 us
    ppermute x5, waiting for transfers between devices, exchange(): return lax.ppermute(partial, 'core', swap)  3.83 us
  transfers between devices with their start and end apart: 9, of which 8 were waited for; matrix products, arithmetic and copies ran while one was open for 1% of the time, Pallas kernels for 8%

profile of v8, /device:TPU:2, one launch (start us, length us, event | category | flops | bytes accessed | tf_op | source)
XLA Modules:
  0.0 121.1 jit_solution(3364140273753592550)
XLA Ops:
  0.6 0.1 collective-permute-start
  0.7 0.0 copy-start
  0.7 2.4 %pack.1.packed_ref = s16[16,8,5888]{2,1,0:T(8,128)(2,1)S(1)} custom-call(bf16[2,4,32,2048]{3,2,1,0:T(8,128)(2,1)} %coh_hbm.1, f32[2,32,2048]{2,1,0:T(8,128)} %vis_hbm.1, s32[2,2048]{1,0:T(2,128)} %pairs_hbm.1), custom_call_target="tpu_custom_call" | custom-call | bytes 1589248 | tf_op jit(solution)/shard_map/pack/pallas_call | solution.py:452
  3.2 0.0 collective-permute-done.other_ref
  3.2 0.0 copy-done
  3.2 0.2 seed.1
  3.4 28.7 %all_to_all.30.data_ref = s16[16,8,5888]{2,1,0:T(8,128)(2,1)S(1)} all-to-all(s16[16,8,5888]{2,1,0:T(8,128)(2,1)S(1)} %seed.1), channel_id=1, replica_groups=mesh['freq'=8,'pair'=16,'core'=2] {'pair'}, dimensions={0} | all-to-all | bytes 3014656 | tf_op jit(solution)/shard_map/all_to_all | solution.py:505
  32.2 6.6 %first.1 = (f32[3,8,512]{2,1,0:T(8,128)S(1)}, f32[2,8,512]{2,1,0:T(8,128)S(1)}) custom-call(s16[16,8,5888]{2,1,0:T(8,128)(2,1)S(1)} %all_to_all.30.data_ref), custom_call_target="tpu_custom_call" | custom-call | flops 3221225472 | bytes 1507328 | tf_op jit(solution)/shard_map/first/pallas_call | solution.py:452
  38.8 0.1 collective-permute-start.1
  38.9 1.2 %collective-permute-done.1.other_ref = f32[3,8,512]{2,1,0:T(8,128)S(1)} collective-permute-done((f32[3,8,512]{2,1,0:T(8,128)S(1)}, f32[3,8,512]{2,1,0:T(8,128)S(1)}, u32[]{:S(2)}, u32[]{:S(2)}) %collective-permute-start.1) | collective-permute-done | bytes 49184 | tf_op jit(solution)/shard_map/ppermute | solution.py:502
  40.1 6.4 %step.1 = (f32[3,8,512]{2,1,0:T(8,128)S(1)}, f32[2,8,512]{2,1,0:T(8,128)S(1)}) custom-call(s16[16,8,5888]{2,1,0:T(8,128)(2,1)S(1)} %all_to_all.30.data_ref, f32[3,8,512]{2,1,0:T(8,128)S(1)} %get-tuple-element.18.mine_ref, f32[3,8,512]{2,1,0:T(8,128)S(1)} %collective-permute-done.1.other_ref, f32[2,8,512]{2,1,0:T(8,128)S(1)} %get-tuple-element.19.gains_ref.target_ref), custom_call_target="tpu_custom_call" | custom-call | flops 3221225472 | bytes 1638400 | tf_op jit(solution)/shard_map/step/pallas_call | solution.py:452
  46.5 0.2 collective-permute-start.2
  46.8 0.7 constant_dynamic-slice_fusion
  47.5 0.1 copy.9
  47.6 0.1 copy.10
  47.7 0.2 collective-permute-done.2.other_ref
  47.8 0.7 finish.2
  48.6 4.8 %all-to-all-start.1 = ((f32[16,8,128]{2,1,0:T(8,128)}), f32[16,8,128]{2,1,0:T(8,128)S(1)}, u32[]{:S(2)}, u32[]{:S(2)}) async-start(f32[16,8,128]{2,1,0:T(8,128)} %get-tuple-element.22), calls=%async_computation.1 | async-start | bytes 131072 | tf_op jit(solution)/shard_map/all_to_all | solution.py:505
  53.3 3.5 %early.1.before_ref = f32[3,8,512]{2,1,0:T(8,128)S(1)} custom-call(s16[16,8,5888]{2,1,0:T(8,128)(2,1)S(1)} %all_to_all.30.data_ref, f32[2,8,512]{2,1,0:T(8,128)S(1)} %get-tuple-element.23.gains_ref), custom_call_target="tpu_custom_call" | custom-call | flops 1610612736 | bytes 1540096 | tf_op jit(solution)/shard_map/early/pallas_call | solution.py:452
  56.8 2.9 %all-to-all-done.1.refs_0_.gains_ref = f32[16,8,128]{2,1,0:T(8,128)S(1)} async-done(((f32[16,8,128]{2,1,0:T(8,128)}), f32[16,8,128]{2,1,0:T(8,128)S(1)}, u32[]{:S(2)}, u32[]{:S(2)}) %all-to-all-start.1) | async-done | bytes 65568 | tf_op jit(solution)/shard_map/all_to_all | solution.py:505
  59.7 0.1 broadcast_in_dim.14.basis_ref
  59.8 0.7 fit.2
  60.5 8.5 %all-to-all-start.2 = ((f32[8,8,128]{2,1,0:T(8,128)}), f32[8,8,128]{2,1,0:T(8,128)S(1)}, u32[]{:S(2)}, u32[]{:S(2)}) async-start(f32[8,8,128]{2,1,0:T(8,128)} %fit.2), calls=%async_computation.2 | async-start | bytes 65536 | tf_op jit(solution)/shard_map/all_to_all | solution.py:508
  69.0 3.5 %late.1.mine_ref = f32[3,8,512]{2,1,0:T(8,128)S(1)} custom-call(s16[16,8,5888]{2,1,0:T(8,128)(2,1)S(1)} %all_to_all.30.data_ref, f32[2,8,512]{2,1,0:T(8,128)S(1)} %get-tuple-element.23.gains_ref, f32[3,8,512]{2,1,0:T(8,128)S(1)} %early.1.before_ref), custom_call_target="tpu_custom_call" | custom-call | flops 1610612736 | bytes 1589248 | tf_op jit(solution)/shard_map/late/pallas_call | solution.py:452
  72.5 4.6 %all-to-all-done.2.parts_ref = f32[8,8,128]{2,1,0:T(8,128)S(1)} async-done(((f32[8,8,128]{2,1,0:T(8,128)}), f32[8,8,128]{2,1,0:T(8,128)S(1)}, u32[]{:S(2)}, u32[]{:S(2)}) %all-to-all-start.2) | async-done | bytes 32800 | tf_op jit(solution)/shard_map/all_to_all | solution.py:508
  77.0 0.7 spread.1
  77.8 4.7 %all-to-all-start.3 = ((f32[16,8,128]{2,1,0:T(8,128)}), f32[16,8,128]{2,1,0:T(8,128)S(1)}, u32[]{:S(2)}, u32[]{:S(2)}) async-start(f32[16,8,128]{2,1,0:T(8,128)} %get-tuple-element.28), calls=%async_computation.3 | async-start | bytes 131072 | tf_op jit(solution)/shard_map/all_to_all | solution.py:505
  82.5 0.0 collective-permute-start.3
  82.5 1.2 %collective-permute-done.3.other_ref = f32[3,8,512]{2,1,0:T(8,128)S(1)} collective-permute-done((f32[3,8,512]{2,1,0:T(8,128)S(1)}, f32[3,8,512]{2,1,0:T(8,128)S(1)}, u32[]{:S(2)}, u32[]{:S(2)}) %collective-permute-start.3) | collective-permute-done | bytes 49184 | tf_op jit(solution)/shard_map/ppermute | solution.py:502
  83.7 5.1 %all-to-all-done.3.fit_ref = f32[16,8,128]{2,1,0:T(8,128)S(1)} async-done(((f32[16,8,128]{2,1,0:T(8,128)}), f32[16,8,128]{2,1,0:T(8,128)S(1)}, u32[]{:S(2)}, u32[]{:S(2)}) %all-to-all-start.3) | async-done | bytes 65568 | tf_op jit(solution)/shard_map/all_to_all | solution.py:505
  88.9 6.6 %retarget.1 = (f32[3,8,512]{2,1,0:T(8,128)S(1)}, f32[2,8,512]{2,1,0:T(8,128)S(1)}, f32[2,8,512]{2,1,0:T(8,128)S(1)}) custom-call(s16[16,8,5888]{2,1,0:T(8,128)(2,1)S(1)} %all_to_all.30.data_ref, f32[3,8,512]{2,1,0:T(8,128)S(1)} %late.1.mine_ref, f32[3,8,512]{2,1,0:T(8,128)S(1)} %collective-permute-done.3.other_ref, ...), custom_call_target="tpu_custom_call" | custom-call | flops 3221225472 | bytes 1703936 | tf_op jit(solution)/shard_map/retarget/pallas_call | solution.py:452
  95.4 0.1 collective-permute-start.4
  95.5 1.2 %collective-permute-done.4.other_ref = f32[3,8,512]{2,1,0:T(8,128)S(1)} collective-permute-done((f32[3,8,512]{2,1,0:T(8,128)S(1)}, f32[3,8,512]{2,1,0:T(8,128)S(1)}, u32[]{:S(2)}, u32[]{:S(2)}) %collective-permute-start.4) | collective-permute-done | bytes 49184 | tf_op jit(solution)/shard_map/ppermute | solution.py:502
  96.7 0.6 finish.3
  97.4 10.8 %all_to_all.31.blocks_ref.refs_0_ = f32[16,8,128]{2,1,0:T(8,128)S(1)} all-to-all(f32[16,8,128]{2,1,0:T(8,128)S(1)} %get-tuple-element.32), channel_id=1, replica_groups=mesh['freq'=8,'pair'=16,'core'=2] {'pair'}, dimensions={0} | all-to-all | bytes 131072 | tf_op jit(solution)/shard_map/all_to_all | solution.py:505
  108.2 0.7 fit.3
  108.9 3.3 %all-to-all-start.5 = ((f32[8,8,128]{2,1,0:T(8,128)}), f32[8,8,128]{2,1,0:T(8,128)S(1)}, u32[]{:S(2)}, u32[]{:S(2)}) async-start(f32[8,8,128]{2,1,0:T(8,128)} %fit.3), calls=%async_computation.5 | async-start | bytes 65536 | tf_op jit(solution)/shard_map/all_to_all | solution.py:508
  112.3 0.8 place.1
  113.1 7.1 %all-to-all-done.5.parts_ref = f32[8,8,128]{2,1,0:T(8,128)S(1)} async-done(((f32[8,8,128]{2,1,0:T(8,128)}), f32[8,8,128]{2,1,0:T(8,128)S(1)}, u32[]{:S(2)}, u32[]{:S(2)}) %all-to-all-start.5) | async-done | bytes 32800 | tf_op jit(solution)/shard_map/all_to_all | solution.py:508
  120.2 0.9 final.1
  (1 shorter events, 0.0 us)
Async XLA Ops:
  0.6 2.6 %collective-permute-start = (f32[2,4,16,32]{3,2,1,0:T(8,128)}, f32[2,4,16,32]{3,2,1,0:T(8,128)S(1)}, u32[]{:S(2)}, u32[]{:S(2)}) collective-permute-start(f32[2,4,16,32]{3,2,1,0:T(8,128)} %bitcast.6), channel_id=1, source_target_pairs={{0,1},{1,0},{2,3},{3,2},{4,5},{5,4},{6,7},{7,6},{8,9},{9,8},{10,11... | collective-permute-start | bytes 49160 | tf_op jit(solution)/shard_map/ppermute | solution.py:502
  0.7 2.5 %copy-start = (f32[2,4,32,16]{2,3,1,0:T(8,128)S(1)}, f32[2,4,32,16]{2,3,1,0:T(8,128)}, u32[]{:S(2)}) copy-start(f32[2,4,32,16]{2,3,1,0:T(8,128)} %param.7) | copy-start | bytes 49156
  38.8 1.3 %collective-permute-start.1 = (f32[3,8,512]{2,1,0:T(8,128)S(1)}, f32[3,8,512]{2,1,0:T(8,128)S(1)}, u32[]{:S(2)}, u32[]{:S(2)}) collective-permute-start(f32[3,8,512]{2,1,0:T(8,128)S(1)} %get-tuple-element.18.mine_ref), channel_id=1, source_target_pairs={{0,1},{1,0},{2,3},{3,2},{4,5},{5,4},{6,7},{7,6},{8,9},{9,8},{10,11... | collective-permute-start | bytes 147464 | tf_op jit(solution)/shard_map/ppermute | solution.py:502
  46.5 1.3 %collective-permute-start.2 = (f32[3,8,512]{2,1,0:T(8,128)S(1)}, f32[3,8,512]{2,1,0:T(8,128)S(1)}, u32[]{:S(2)}, u32[]{:S(2)}) collective-permute-start(f32[3,8,512]{2,1,0:T(8,128)S(1)} %get-tuple-element.20.mine_ref), channel_id=1, source_target_pairs={{0,1},{1,0},{2,3},{3,2},{4,5},{5,4},{6,7},{7,6},{8,9},{9,8},{10,11... | collective-permute-start | bytes 147464 | tf_op jit(solution)/shard_map/ppermute | solution.py:502
  48.6 11.1 %all-to-all-start.1 = ((f32[16,8,128]{2,1,0:T(8,128)}), f32[16,8,128]{2,1,0:T(8,128)S(1)}, u32[]{:S(2)}, u32[]{:S(2)}) async-start(f32[16,8,128]{2,1,0:T(8,128)} %get-tuple-element.22), calls=%async_computation.1 | async-start | bytes 131072 | tf_op jit(solution)/shard_map/all_to_all | solution.py:505
  60.5 16.5 %all-to-all-start.2 = ((f32[8,8,128]{2,1,0:T(8,128)}), f32[8,8,128]{2,1,0:T(8,128)S(1)}, u32[]{:S(2)}, u32[]{:S(2)}) async-start(f32[8,8,128]{2,1,0:T(8,128)} %fit.2), calls=%async_computation.2 | async-start | bytes 65536 | tf_op jit(solution)/shard_map/all_to_all | solution.py:508
  77.8 11.1 %all-to-all-start.3 = ((f32[16,8,128]{2,1,0:T(8,128)}), f32[16,8,128]{2,1,0:T(8,128)S(1)}, u32[]{:S(2)}, u32[]{:S(2)}) async-start(f32[16,8,128]{2,1,0:T(8,128)} %get-tuple-element.28), calls=%async_computation.3 | async-start | bytes 131072 | tf_op jit(solution)/shard_map/all_to_all | solution.py:505
  82.5 1.2 %collective-permute-start.3 = (f32[3,8,512]{2,1,0:T(8,128)S(1)}, f32[3,8,512]{2,1,0:T(8,128)S(1)}, u32[]{:S(2)}, u32[]{:S(2)}) collective-permute-start(f32[3,8,512]{2,1,0:T(8,128)S(1)} %late.1.mine_ref), channel_id=1, source_target_pairs={{0,1},{1,0},{2,3},{3,2},{4,5},{5,4},{6,7},{7,6},{8,9},{9,8},{10,11... | collective-permute-start | bytes 147464 | tf_op jit(solution)/shard_map/ppermute | solution.py:502
  95.4 1.3 %collective-permute-start.4 = (f32[3,8,512]{2,1,0:T(8,128)S(1)}, f32[3,8,512]{2,1,0:T(8,128)S(1)}, u32[]{:S(2)}, u32[]{:S(2)}) collective-permute-start(f32[3,8,512]{2,1,0:T(8,128)S(1)} %get-tuple-element.29.mine_ref), channel_id=1, source_target_pairs={{0,1},{1,0},{2,3},{3,2},{4,5},{5,4},{6,7},{7,6},{8,9},{9,8},{10,11... | collective-permute-start | bytes 147464 | tf_op jit(solution)/shard_map/ppermute | solution.py:502
  108.9 11.3 %all-to-all-start.5 = ((f32[8,8,128]{2,1,0:T(8,128)}), f32[8,8,128]{2,1,0:T(8,128)S(1)}, u32[]{:S(2)}, u32[]{:S(2)}) async-start(f32[8,8,128]{2,1,0:T(8,128)} %fit.3), calls=%async_computation.5 | async-start | bytes 65536 | tf_op jit(solution)/shard_map/all_to_all | solution.py:508
